TPU v7x, 32 devices: a whole 2x2x4 slice. The times are simulated.
32 devices in a mesh: groups: 2 (over y), tile: 16 (over z, x, core).
Axes of the slice: x: 2, y: 2, z: 4, core: 2. Of those that a mesh axis runs over, the one named last changes fastest.
Arguments:
- features: bfloat16 [192, 16, 16, 256], P(('groups', 'tile')), parts along dimension 0, may hold values from -6 to 6
- weights: bfloat16 [9, 256, 256], replicated, may hold values from -0.125 to 0.125
- grad_out: bfloat16 [192, 16, 16, 256], P(('groups', 'tile')), parts along dimension 0, may hold values from -6 to 6
- tile_pos: int32 [192], P(('groups', 'tile')), parts along dimension 0, may hold values from -1 to 7, as said below
- neighbours: int32 [192, 8], P(('groups', 'tile')), parts along dimension 0, may hold values from -1 to 15, as said below
Outputs:
- activation: bfloat16 [192, 16, 16, 256], P(('groups', 'tile')), parts along dimension 0
- weight_grad: float32 [18, 256, 256], P('groups'), parts along dimension 0
- input_grad: bfloat16 [192, 16, 16, 256], P(('groups', 'tile')), parts along dimension 0
There are 2 independent parts, one for each index of `groups`. A program takes and returns all parts, laid end to end along the dimension named above; an argument that names none is the same for every part. Nothing has to cross between parts.
Inputs may be any that keep to these rules, and one draw needn't show every extreme that they name: `tile_pos`: each device's 6 slots hold the tissue tiles of its band of 2 x 4 tiles first, in raster order, then empty slots; every device holds 2 or more tissue tiles and at least one device holds 6. A code c names slot c % 6 of the device whose index is the own index plus c // 6 - 1; codes of left and right neighbours name the own device, up and up-diagonal neighbours lie on the own or the preceding device, down and down-diagonal ones on the own or the following device. Neighbours are tissue tiles of the slide's grid and the relation is symmetric; empty slots and missing neighbours have -1.
All inputs are finite; a program needn't handle non-finite values.
Results may differ from a plain program's by a relative error of at most 0.0049.
Values may be sent and summed in bfloat16 or wider, within the bound.
No kernel may reach another device: no remote copies, remote signals or barrier semaphores. Data moves between devices by JAX's collectives and lax.ppermute only.
A program may use at most 64 MiB of HBM per device.

v0:
```python
import functools
import math

import jax
import jax.numpy as jnp
from jax import lax
from jax.experimental import pallas as pl
from jax.experimental.pallas import tpu as pltpu
from jax.sharding import PartitionSpec as P


ROOT_HALF = 0.7071067811865476
INV_ROOT_TAU = 0.3989422804014327
F32 = jnp.float32
BF16 = jnp.bfloat16
VMEM = pl.BlockSpec(memory_space=pltpu.VMEM)
SMEM = pl.BlockSpec(memory_space=pltpu.SMEM)
ANY = pl.BlockSpec(memory_space=pl.ANY)
LIMIT = 16 << 20


def shape_of(shape, dtype):
    return jax.ShapeDtypeStruct(shape, dtype)


def held(shape, dtype):
    return pltpu.VMEM(shape, dtype)


def far(value):
    return pltpu.with_memory_space_constraint(value, pltpu.HBM)


def call(kernel, flops, moved, **options):
    return pl.pallas_call(
        kernel,
        compiler_params=pltpu.CompilerParams(vmem_limit_bytes=LIMIT),
        cost_estimate=pl.CostEstimate(flops=flops, bytes_accessed=moved, transcendentals=0),
        **options,
    )


def place():
    index = lax.axis_index("tile").astype(jnp.int32)
    core = lax.rem(index, 2)
    low, high = lax.rem(lax.div(index, 2), 2), lax.rem(lax.div(index, 4), 2)
    return core, jnp.where(core == 0, low, high), jnp.where(core == 0, high, low)


def rows_from(own_rows, far_rows, code, first):
    slots = own_rows.shape[0]
    own = own_rows[jnp.clip(code - slots, 0, slots - 1)].astype(F32)
    far = far_rows[jnp.clip(code - first, 0, slots - 1)].astype(F32)
    inside = (code >= slots) & (code < 2 * slots)
    return jnp.where(inside, own, jnp.where(code >= 0, far, 0.0))


def put_columns(out, at, center, left, right):
    axis = center.ndim - 2
    side, channels = center.shape[-2:]
    cell = lax.broadcasted_iota(jnp.int32, center.shape, axis)
    shifted = pltpu.roll(jnp.where(cell == side - 1, left, center), 1, axis)
    out[at + (Ellipsis, slice(0, channels))] = shifted.astype(BF16)
    out[at + (Ellipsis, slice(channels, 2 * channels))] = center.astype(BF16)
    shifted = pltpu.roll(jnp.where(cell == 0, right, center), side - 1, axis)
    out[at + (Ellipsis, slice(2 * channels, 3 * channels))] = shifted.astype(BF16)


def put_inner(out, maps, codes, tile, at):
    slots = maps.shape[0]

    def neighbour(code):
        return jnp.where(code >= 0, maps[jnp.clip(code - slots, 0, slots - 1)].astype(F32), 0.0)

    put_columns(
        out, (at,), maps[tile].astype(F32), neighbour(codes[tile, 2]), neighbour(codes[tile, 3])
    )


def put_edges(out, first, last, up, down, codes, tile, at):
    slots = first.shape[0]
    top = [rows_from(last, up, codes[tile, j], 0) for j in (0, 4, 5)]
    put_columns(out, (at, 0), *top)
    bottom = [rows_from(first, down, codes[tile, j], 2 * slots) for j in (1, 6, 7)]
    put_columns(out, (at, 1), *bottom)


def rows_for(inner, edge, tile, step):
    side = inner.shape[1]
    if step == 1:
        return inner[tile]
    if step == 0:
        return jnp.concatenate([edge[tile, 0][None], inner[tile, : side - 1]], axis=0)
    return jnp.concatenate([inner[tile, 1:], edge[tile, 1][None]], axis=0)


def load_kernel(codes, maps, weights, grads, inner, weights_out, grads_out, tiles, sems):
    loads = [
        pltpu.make_async_copy(source, target, sems.at[k])
        for k, (source, target) in enumerate(
            [(maps, tiles), (weights, weights_out), (grads, grads_out)]
        )
    ]
    for load in loads:
        load.start()
    loads[0].wait()
    for tile in range(maps.shape[0]):
        put_inner(inner, tiles, codes, tile, tile)
    loads[1].wait()
    loads[2].wait()


def load(codes, maps, weights, grads):
    slots, side, _, channels = maps.shape
    return call(
        load_kernel,
        1 << 20,
        6 << 20,
        in_specs=[SMEM, ANY, ANY, ANY],
        out_specs=[VMEM] * 3,
        out_shape=[
            held((slots, side, side, 3 * channels), BF16),
            held(weights.shape, BF16),
            held(grads.shape, BF16),
        ],
        scratch_shapes=[pltpu.VMEM(maps.shape, BF16), pltpu.SemaphoreType.DMA((3,))],
    )(far(codes), far(maps), far(weights), far(grads))


def forward_kernel(
    codes, pos, inner, first, last, up, down, weights, grads,
    act, grad, edge, grad_first, grad_last, codes_held, pos_held, sems,
):
    slots, side, _, wide = inner.shape
    channels = wide // 3
    loads = [
        pltpu.make_async_copy(codes, codes_held, sems.at[0]),
        pltpu.make_async_copy(pos, pos_held, sems.at[1]),
    ]
    for item in loads:
        item.start()

    def product(tile, step):
        rows = rows_for(inner, edge, tile, step).reshape(side * side, wide)
        return jnp.dot(
            rows,
            weights[3 * step * channels : 3 * (step + 1) * channels],
            preferred_element_type=F32,
        )

    for item in loads:
        item.wait()
    for tile in range(slots):
        put_edges(edge, first, last, up, down, codes_held, tile, tile)
    for tile in range(slots):
        value = product(tile, 1) + product(tile, 0) + product(tile, 2)
        gate = jnp.where(pos_held[tile] >= 0, 1.0, 0.0)
        cumulative = 0.5 * (1.0 + lax.erf(value * ROOT_HALF))
        density = jnp.exp(-0.5 * value * value) * INV_ROOT_TAU
        cells = (side, side, channels)
        act[tile] = (value * cumulative * gate).astype(BF16).reshape(cells)
        slope = cumulative + value * density
        outer = grads[tile].astype(F32).reshape(side * side, channels)
        made = (outer * slope * gate).astype(BF16).reshape(cells)
        grad[tile] = made
        grad_first[tile] = made[0]
        grad_last[tile] = made[side - 1]


def forward(codes, pos, inner, first, last, up, down, weights, grads):
    slots, side, _, wide = inner.shape
    cells = grads.shape
    return call(
        forward_kernel,
        2 * slots * side * side * wide * wide,
        8 << 20,
        in_specs=[ANY, ANY] + [VMEM] * 7,
        out_specs=[VMEM] * 5,
        out_shape=[
            shape_of(cells, BF16),
            held(cells, BF16),
            held((slots, 2, side, wide), BF16),
            held(first.shape, BF16),
            held(first.shape, BF16),
        ],
        scratch_shapes=[
            pltpu.SMEM(codes.shape, jnp.int32),
            pltpu.SMEM(pos.shape, jnp.int32),
            pltpu.SemaphoreType.DMA((2,)),
        ],
    )(far(codes), far(pos), inner, first, last, up, down, weights, grads)


def kernel_grad_kernel(other, inner, edge, grad, out):
    slots, side, _, channels = grad.shape
    lanes = channels // 2
    outer = grad[...].reshape(slots * side * side, channels)
    core = place()[0]
    half = 1 - core if other else core
    for row_step in range(3):
        for col_step in range(3):
            start = pl.multiple_of(col_step * channels + half * lanes, lanes)
            part = pl.ds(start, lanes)
            if row_step == 1:
                rows = inner[:, :, :, part]
            elif row_step == 0:
                rows = jnp.concatenate([edge[:, :1, :, part], inner[:, : side - 1, :, part]], axis=1)
            else:
                rows = jnp.concatenate([inner[:, 1:, :, part], edge[:, 1:, :, part]], axis=1)
            made = lax.dot_general(
                rows.reshape(slots * side * side, lanes),
                outer,
                (((0,), (0,)), ((), ())),
                preferred_element_type=F32,
            )
            out[:, 3 * row_step + col_step] = made.reshape(4, lanes // 4, channels).astype(out.dtype)


def kernel_grad(other, inner, edge, grad, dtype):
    slots, side, _, channels = grad.shape
    return call(
        functools.partial(kernel_grad_kernel, other),
        9 * slots * side * side * channels * channels,
        6 << 20,
        in_specs=[VMEM, VMEM, VMEM],
        out_specs=VMEM,
        out_shape=held((4, 9, channels // 8, channels), dtype),
    )(inner, edge, grad)


def spread_kernel(keep, recv, send):
    first_bit = place()[1]
    for k in range(2):
        piece = 2 * (1 - first_bit) + k
        send[k] = (keep[piece] + recv[piece].astype(F32)).astype(BF16)


def spread(keep, recv):
    return call(
        spread_kernel,
        1 << 20,
        2 << 20,
        in_specs=[VMEM, VMEM],
        out_specs=VMEM,
        out_shape=held((2,) + keep.shape[1:], BF16),
    )(keep, recv)


def narrow_kernel(flip, keep, recv, got, out):
    _, first_bit, second_bit = place()
    second = 1 - second_bit if flip else second_bit
    piece = 2 * first_bit + second
    total = keep[piece] + recv[piece].astype(F32) + got[second].astype(F32)
    out[...] = total.astype(out.dtype)


def narrow(flip, keep, recv, got, dtype):
    return call(
        functools.partial(narrow_kernel, flip),
        1 << 20,
        1 << 20,
        in_specs=[VMEM, VMEM, VMEM],
        out_specs=VMEM,
        out_shape=held(keep.shape[1:], dtype),
    )(keep, recv, got)


def collect_kernel(scale, plan, *refs):
    count = len(plan)
    core, first_bit, second_bit = place()
    own = core * 4 + 2 * first_bit + second_bit
    others = (1 - core) * 4 + 2 * second_bit + first_bit
    pieces, out = refs[:count], refs[-3]
    rows, sem = refs[-2], refs[-1]
    depth = pieces[0].shape[-2]
    copies = []
    for k, piece in enumerate(pieces):
        rows[k] = piece[...].astype(F32) * scale
        slot = (others if plan[k][0] else own) ^ plan[k][1]
        start = pl.multiple_of(slot * depth, depth)
        copy = pltpu.make_async_copy(rows.at[k], out.at[:, pl.ds(start, depth), :], sem.at[k])
        copy.start()
        copies.append(copy)
    for copy in copies:
        copy.wait()


def collect(plan, pieces, scale, whole, base):
    taps, depth, channels = pieces[0].shape
    count = len(pieces)
    operands = list(pieces)
    specs = [VMEM] * count
    aliases = {}
    if base is not None:
        operands.append(base)
        specs.append(ANY)
        aliases = {count: 0}
    return call(
        functools.partial(collect_kernel, scale, plan),
        1 << 20,
        count << 19,
        in_specs=specs,
        out_specs=ANY,
        out_shape=pltpu.HBM(whole, F32),
        input_output_aliases=aliases,
        scratch_shapes=[
            pltpu.VMEM((count, taps, depth, channels), F32),
            pltpu.SemaphoreType.DMA((count,)),
        ],
    )(*operands)


def backward_kernel(tiles, codes, pos, grad, first, last, up, down, weights, out, inner, edge):
    _, side, _, channels = grad.shape
    for k, tile in enumerate(tiles):
        put_inner(inner, grad, codes, tile, k)
        put_edges(edge, first, last, up, down, codes, tile, k)
    for k, tile in enumerate(tiles):
        total = None
        for row_step in range(3):
            rows = rows_for(inner, edge, k, row_step).reshape(side * side, 3 * channels)
            for col_step in range(3):
                tap = 3 * (2 - row_step) + 2 - col_step
                made = lax.dot_general(
                    rows[:, col_step * channels : (col_step + 1) * channels],
                    weights[tap * channels : (tap + 1) * channels],
                    (((1,), (1,)), ((), ())),
                    preferred_element_type=F32,
                )
                total = made if total is None else total + made
        gate = jnp.where(pos[tile] >= 0, 1.0, 0.0)
        out[k] = (total * gate).astype(BF16).reshape(side, side, channels)


def backward(tiles, codes, pos, grad, first, last, up, down, weights):
    _, side, _, channels = grad.shape
    count = len(tiles)
    return call(
        functools.partial(backward_kernel, tiles),
        18 * count * side * side * channels * channels,
        4 << 20,
        in_specs=[SMEM, SMEM] + [VMEM] * 6,
        out_specs=VMEM,
        out_shape=shape_of((count, side, side, channels), BF16),
        scratch_shapes=[
            pltpu.VMEM((count, side, side, 3 * channels), BF16),
            pltpu.VMEM((count, 2, side, 3 * channels), BF16),
        ],
    )(codes, pos, grad, first, last, up, down, weights)


def from_behind(value, steps):
    count = lax.axis_size("tile")
    begin, end = max(0, -steps), min(count, count - steps)
    return lax.ppermute(value, "tile", [(source, source + steps) for source in range(begin, end)])


def swap(value, bit):
    count = lax.axis_size("tile")
    return lax.ppermute(value, "tile", [(source, source ^ bit) for source in range(count)])


def crossed(value, even_bit, odd_bit):
    count = lax.axis_size("tile")
    pairs = [(s, s ^ (odd_bit if s & 1 else even_bit)) for s in range(count)]
    return lax.ppermute(value, "tile", pairs)


def sum_high(total, high):
    shape = total.shape
    index = lax.axis_index("tile")
    for bit in high[:-1]:
        flat = total.reshape(2, -1, shape[-1])
        upper = (index & bit) != 0
        arrived = swap(jnp.where(upper, flat[0], flat[1]).astype(BF16), bit)
        total = jnp.where(upper, flat[1], flat[0]) + arrived.astype(F32)
    mine = total.astype(BF16)
    other = swap(mine, high[-1])
    total = (mine.astype(F32) + other.astype(F32)).astype(BF16)
    for bit in reversed(high[:-1]):
        upper = (index & bit) != 0
        other = swap(total, bit)
        total = jnp.concatenate(
            [jnp.where(upper, other, total), jnp.where(upper, total, other)], axis=0
        )
    return total.reshape(shape)


def step(features, weights, grad_out, tile_pos, neighbours):
    slots, side, _, channels = features.shape
    devices = lax.axis_size("tile")
    flat = weights.reshape(9 * channels, channels)
    first, last = features[:, 0], features[:, -1]
    above = from_behind(last, 1)
    below = from_behind(first, -1)
    inner, flat, grads = load(neighbours, features, flat, grad_out)
    activation, grad, edge, grad_first, grad_last = forward(
        neighbours, tile_pos, inner, first, last, above, below, flat, grads
    )
    send = kernel_grad(True, inner, edge, grad, BF16)
    recv = swap(send, 1)
    keep = kernel_grad(False, inner, edge, grad, F32)
    sent = spread(keep, recv)
    got = crossed(sent, 2, 4)
    sent = narrow(True, keep, recv, got, BF16)
    got_next = crossed(sent, 4, 2)
    own = narrow(False, keep, recv, got, F32)
    piece = sum_high(
        own + got_next.astype(F32), [8 << k for k in range(devices.bit_length() - 4)]
    )
    scale = 1.0 / math.sqrt(slots * devices * side * side)
    whole = weights.shape
    near = crossed(piece, 4, 2)
    away = crossed(piece, 2, 4)
    its = swap(piece, 1)
    away_near = crossed(near, 2, 4)
    its_near = swap(near, 1)
    its_away = swap(away, 1)
    its_away_near = swap(away_near, 1)
    weight_grad = collect(
        ((0, 0), (0, 1), (1, 0), (1, 1), (0, 2)),
        [piece, near, its, its_near, away], scale, whole, None
    )
    weight_grad = collect(((0, 3), (1, 2)), [away_near, its_away], scale, whole, weight_grad)
    weight_grad = collect(((1, 3),), [its_away_near], scale, whole, weight_grad)
    grad_above = from_behind(grad_last, 1)
    grad_below = from_behind(grad_first, -1)
    input_grad = backward(
        tuple(range(slots)), neighbours, tile_pos, grad, grad_first, grad_last,
        grad_above, grad_below, weights.reshape(9 * channels, channels),
    )
    return (activation, weight_grad, input_grad)


def solution(mesh):
    in_specs = (
        P(("groups", "tile"), None, None, None),
        P(),
        P(("groups", "tile"), None, None, None),
        P(("groups", "tile")),
        P(("groups", "tile"), None),
    )
    out_specs = (
        P(("groups", "tile"), None, None, None),
        P("groups", None, None),
        P(("groups", "tile"), None, None, None),
    )
    return jax.shard_map(step, mesh=mesh, in_specs=in_specs, out_specs=out_specs, check_vma=False)
```

profile of v0, /device:TPU:0, one launch (start us, length us, event | category | flops | bytes accessed | tf_op | source)
XLA Modules:
  0.0 60.5 jit_solution(8654414162677253373)
XLA Ops:
  0.6 0.8 %slice_bitcast_fusion = (bf16[6,16,256]{2,1,0:T(8,128)(2,1)S(1)}, bf16[6,16,256]{2,1,0:T(8,128)(2,1)S(1)}) fusion(bf16[6,16,16,256]{3,2,1,0:T(8,128)(2,1)} %maps.1), kind=kLoop, calls=%fused_computation.2 | loop fusion | bytes 196608 | tf_op jit(solution)/shard_map/squeeze | solution.py:393
  1.5 2.4 %collective-permute-start = (bf16[6,16,256]{2,1,0:T(8,128)(2,1)S(1)}, bf16[6,16,256]{2,1,0:T(8,128)(2,1)S(1)}, u32[]{:S(2)}, u32[]{:S(2)}) collective-permute-start(bf16[6,16,256]{2,1,0:T(8,128)(2,1)S(1)} %get-tuple-element.19.last), channel_id=1, source_target_pairs={{0,1},{1,2},{2,3},{3,4},{4,5},{5,6},{6,7},{7,8},{8,9},{9,10},{10,1... | collective-permute-start | bytes 147464 | tf_op jit(solution)/shard_map/ppermute | solution.py:355
  3.9 1.3 %collective-permute-start.1 = (bf16[6,16,256]{2,1,0:T(8,128)(2,1)S(1)}, bf16[6,16,256]{2,1,0:T(8,128)(2,1)S(1)}, u32[]{:S(2)}, u32[]{:S(2)}) collective-permute-start(bf16[6,16,256]{2,1,0:T(8,128)(2,1)S(1)} %get-tuple-element.20.first), channel_id=1, source_target_pairs={{1,0},{2,1},{3,2},{4,3},{5,4},{6,5},{7,6},{8,7},{9,8},{10,9},{11,1... | collective-permute-start | bytes 147464 | tf_op jit(solution)/shard_map/ppermute | solution.py:355
  5.2 2.5 %shard_map.76 = (bf16[6,16,16,768]{3,2,1,0:T(8,128)(2,1)S(1)}, bf16[2304,256]{1,0:T(8,128)(2,1)S(1)}, bf16[6,16,16,256]{3,2,1,0:T(8,128)(2,1)S(1)}) custom-call(s32[6,8]{1,0:T(8,128)} %codes.5, bf16[6,16,16,256]{3,2,1,0:T(8,128)(2,1)} %maps.1, bf16[2304,256]{1,0:T(8,128)(2,1)} %bitcast.9, bf16[6,16,16,256]{3,2,1,0:T(8,128)(2,1)} %grads.1), custom_call_target="tpu_custom_call" | custom-call | flops 1048576 | bytes 6291456 | tf_op jit(solution)/shard_map/pallas_call | solution.py:115
  7.7 1.4 %collective-permute-done.1.down = bf16[6,16,256]{2,1,0:T(8,128)(2,1)S(1)} collective-permute-done((bf16[6,16,256]{2,1,0:T(8,128)(2,1)S(1)}, bf16[6,16,256]{2,1,0:T(8,128)(2,1)S(1)}, u32[]{:S(2)}, u32[]{:S(2)}) %collective-permute-start.1) | collective-permute-done | bytes 49184 | tf_op jit(solution)/shard_map/ppermute | solution.py:355
  9.1 4.4 %shard_map.77 = (bf16[6,16,16,256]{3,2,1,0:T(8,128)(2,1)}, bf16[6,16,16,256]{3,2,1,0:T(8,128)(2,1)S(1)}, bf16[6,2,16,768]{3,2,1,0:T(8,128)(2,1)S(1)}, bf16[6,16,...) custom-call(s32[6,8]{1,0:T(8,128)} %codes.5, s32[6]{0:T(128)} %pos.3, bf16[6,16,16,768]{3,2,1,0:T(8,128)(2,1)S(1)} %get-tuple-element.11.inner, ...), custom_call_target="tpu_custom_call" | custom-call | flops 1811939328 | bytes 8388608 | tf_op jit(solution)/shard_map/pallas_call | solution.py:173
  13.4 1.2 %shard_map.79 = bf16[4,9,32,256]{3,2,1,0:T(8,128)(2,1)S(1)} custom-call(bf16[6,16,16,768]{3,2,1,0:T(8,128)(2,1)S(1)} %get-tuple-element.11.inner, bf16[6,2,16,768]{3,2,1,0:T(8,128)(2,1)S(1)} %get-tuple-element.15.edge, bf16[6,16,16,256]{3,2,1,0:T(8,128)(2,1)S(1)} %get-tuple-element.16.grad), custom_call_target="tpu_custom_call" | custom-call | flops 905969664 | bytes 6291456 | tf_op jit(solution)/shard_map/pallas_call | solution.py:221
  14.7 2.8 %collective-permute-start.2 = (bf16[4,9,32,256]{3,2,1,0:T(8,128)(2,1)S(1)}, bf16[4,9,32,256]{3,2,1,0:T(8,128)(2,1)S(1)}, u32[]{:S(2)}, u32[]{:S(2)}) collective-permute-start(bf16[4,9,32,256]{3,2,1,0:T(8,128)(2,1)S(1)} %shard_map.79), channel_id=1, source_target_pairs={{0,1},{1,0},{2,3},{3,2},{4,5},{5,4},{6,7},{7,6},{8,9},{9,8},{10,11... | collective-permute-start | bytes 1769480 | tf_op jit(solution)/shard_map/ppermute | solution.py:360
  17.5 1.2 %shard_map.78.keep = f32[4,9,32,256]{3,2,1,0:T(8,128)S(1)} custom-call(bf16[6,16,16,768]{3,2,1,0:T(8,128)(2,1)S(1)} %get-tuple-element.11.inner, bf16[6,2,16,768]{3,2,1,0:T(8,128)(2,1)S(1)} %get-tuple-element.15.edge, bf16[6,16,16,256]{3,2,1,0:T(8,128)(2,1)S(1)} %get-tuple-element.16.grad), custom_call_target="tpu_custom_call" | custom-call | flops 905969664 | bytes 6291456 | tf_op jit(solution)/shard_map/pallas_call | solution.py:221
  19.2 2.5 %collective-permute-start.3 = (bf16[2,9,32,256]{3,2,1,0:T(8,128)(2,1)S(1)}, bf16[2,9,32,256]{3,2,1,0:T(8,128)(2,1)S(1)}, u32[]{:S(2)}, u32[]{:S(2)}) collective-permute-start(bf16[2,9,32,256]{3,2,1,0:T(8,128)(2,1)S(1)} %shard_map.80), channel_id=1, source_target_pairs={{0,2},{1,5},{2,0},{3,7},{4,6},{5,1},{6,4},{7,3},{8,10},{9,13},{10,... | collective-permute-start | bytes 884744 | tf_op jit(solution)/shard_map/ppermute | solution.py:366
  21.7 4.7 %collective-permute-done.3.got = bf16[2,9,32,256]{3,2,1,0:T(8,128)(2,1)S(1)} collective-permute-done((bf16[2,9,32,256]{3,2,1,0:T(8,128)(2,1)S(1)}, bf16[2,9,32,256]{3,2,1,0:T(8,128)(2,1)S(1)}, u32[]{:S(2)}, u32[]{:S(2)}) %collective-permute-start.3) | collective-permute-done | bytes 294944 | tf_op jit(solution)/shard_map/ppermute | solution.py:366
  26.5 1.7 %collective-permute-start.4 = (bf16[9,32,256]{2,1,0:T(8,128)(2,1)S(1)}, bf16[9,32,256]{2,1,0:T(8,128)(2,1)S(1)}, u32[]{:S(2)}, u32[]{:S(2)}) collective-permute-start(bf16[9,32,256]{2,1,0:T(8,128)(2,1)S(1)} %shard_map.82), channel_id=1, source_target_pairs={{0,4},{1,3},{2,6},{3,1},{4,0},{5,7},{6,2},{7,5},{8,12},{9,11},{10,... | collective-permute-start | bytes 442376 | tf_op jit(solution)/shard_map/ppermute | solution.py:366
  28.2 3.5 %collective-permute-done.4 = bf16[9,32,256]{2,1,0:T(8,128)(2,1)S(1)} collective-permute-done((bf16[9,32,256]{2,1,0:T(8,128)(2,1)S(1)}, bf16[9,32,256]{2,1,0:T(8,128)(2,1)S(1)}, u32[]{:S(2)}, u32[]{:S(2)}) %collective-permute-start.4) | collective-permute-done | bytes 147488 | tf_op jit(solution)/shard_map/ppermute | solution.py:366
  31.7 2.7 %collective-permute-start.5 = (bf16[9,32,256]{2,1,0:T(8,128)(2,1)S(1)}, bf16[9,32,256]{2,1,0:T(8,128)(2,1)S(1)}, u32[]{:S(2)}, u32[]{:S(2)}) collective-permute-start(bf16[9,32,256]{2,1,0:T(8,128)(2,1)S(1)} %add_convert_fusion.1), channel_id=1, source_target_pairs={{0,8},{1,9},{2,10},{3,11},{4,12},{5,13},{6,14},{7,15},{8,0},{9,1},... | collective-permute-start | bytes 442376 | tf_op jit(solution)/shard_map/ppermute | solution.py:360
  34.4 6.1 %collective-permute-done.5 = bf16[9,32,256]{2,1,0:T(8,128)(2,1)S(1)} collective-permute-done((bf16[9,32,256]{2,1,0:T(8,128)(2,1)S(1)}, bf16[9,32,256]{2,1,0:T(8,128)(2,1)S(1)}, u32[]{:S(2)}, u32[]{:S(2)}) %collective-permute-start.5) | collective-permute-done | bytes 147488 | tf_op jit(solution)/shard_map/ppermute | solution.py:360
  40.7 1.8 %collective-permute-start.9 = (bf16[9,32,256]{2,1,0:T(8,128)(2,1)S(1)}, bf16[9,32,256]{2,1,0:T(8,128)(2,1)S(1)}, u32[]{:S(2)}, u32[]{:S(2)}) collective-permute-start(bf16[9,32,256]{2,1,0:T(8,128)(2,1)S(1)} %add_convert_fusion.refs_0_), channel_id=1, source_target_pairs={{0,2},{1,5},{2,0},{3,7},{4,6},{5,1},{6,4},{7,3},{8,10},{9,13},{10,... | collective-permute-start | bytes 442376 | tf_op jit(solution)/shard_map/ppermute | solution.py:366
  42.5 4.9 %collective-permute-done.6.refs_1_ = bf16[9,32,256]{2,1,0:T(8,128)(2,1)S(1)} collective-permute-done((bf16[9,32,256]{2,1,0:T(8,128)(2,1)S(1)}, bf16[9,32,256]{2,1,0:T(8,128)(2,1)S(1)}, u32[]{:S(2)}, u32[]{:S(2)}) %collective-permute-start.6) | collective-permute-done | bytes 147488 | tf_op jit(solution)/shard_map/ppermute | solution.py:366
  47.5 1.3 %collective-permute-start.14 = (bf16[6,16,256]{2,1,0:T(8,128)(2,1)S(1)}, bf16[6,16,256]{2,1,0:T(8,128)(2,1)S(1)}, u32[]{:S(2)}, u32[]{:S(2)}) collective-permute-start(bf16[6,16,256]{2,1,0:T(8,128)(2,1)S(1)} %get-tuple-element.17.first), channel_id=1, source_target_pairs={{1,0},{2,1},{3,2},{4,3},{5,4},{6,5},{7,6},{8,7},{9,8},{10,9},{11,1... | collective-permute-start | bytes 147464 | tf_op jit(solution)/shard_map/ppermute | solution.py:355
  48.8 3.0 %collective-permute-start.13 = (bf16[6,16,256]{2,1,0:T(8,128)(2,1)S(1)}, bf16[6,16,256]{2,1,0:T(8,128)(2,1)S(1)}, u32[]{:S(2)}, u32[]{:S(2)}) collective-permute-start(bf16[6,16,256]{2,1,0:T(8,128)(2,1)S(1)} %get-tuple-element.18.last), channel_id=1, source_target_pairs={{0,1},{1,2},{2,3},{3,4},{4,5},{5,6},{6,7},{7,8},{8,9},{9,10},{10,1... | collective-permute-start | bytes 147464 | tf_op jit(solution)/shard_map/ppermute | solution.py:355
  51.8 1.5 %collective-permute-start.11 = (bf16[9,32,256]{2,1,0:T(8,128)(2,1)S(1)}, bf16[9,32,256]{2,1,0:T(8,128)(2,1)S(1)}, u32[]{:S(2)}, u32[]{:S(2)}) collective-permute-start(bf16[9,32,256]{2,1,0:T(8,128)(2,1)S(1)} %add_convert_fusion.refs_0_), channel_id=1, source_target_pairs={{0,1},{1,0},{2,3},{3,2},{4,5},{5,4},{6,7},{7,6},{8,9},{9,8},{10,11... | collective-permute-start | bytes 442376 | tf_op jit(solution)/shard_map/ppermute | solution.py:360
  54.0 3.6 %shard_map.86 = bf16[6,16,16,256]{3,2,1,0:T(8,128)(2,1)} custom-call(s32[6,8]{1,0:T(8,128)S(1)} %copy-done.1, s32[6]{0:T(128)S(1)} %copy-done.2, bf16[6,16,16,256]{3,2,1,0:T(8,128)(2,1)S(1)} %get-tuple-element.16.grad, bf16[6,16,256]{2,1,0:T(8,128)(2,1)S(1)} %get-tuple-element.17.first, bf16[6,16,256]{2,1,0:T(8,128)(2,1)S(1)} %get-tuple-element.18.last, ...), custom_call_target="tpu_custom_call" | custom-call | flops 1811939328 | bytes 4194304 | tf_op jit(solution)/shard_map/pallas_call | solution.py:338
  57.6 1.2 %shard_map.83.refs_2_ = f32[9,256,256]{2,1,0:T(8,128)} custom-call(bf16[9,32,256]{2,1,0:T(8,128)(2,1)S(1)} %add_convert_fusion.refs_0_, bf16[9,32,256]{2,1,0:T(8,128)(2,1)S(1)} %collective-permute-done.6.refs_1_, bf16[9,32,256]{2,1,0:T(8,128)(2,1)S(1)} %collective-permute-done.11.refs_2_, bf16[9,32,256]{2,1,0:T(8,128)(2,1)S(1)} %collective-permute-done.12.refs_3_, ...), custom_call_target="tpu_custom_call" | custom-call | flops 1048576 | bytes 2621440 | tf_op jit(solution)/shard_map/pallas_call | solution.py:298
  58.8 0.9 %shard_map.84.refs_1_ = f32[9,256,256]{2,1,0:T(8,128)} custom-call(bf16[9,32,256]{2,1,0:T(8,128)(2,1)S(1)} %collective-permute-done.7.refs_0_, bf16[9,32,256]{2,1,0:T(8,128)(2,1)S(1)} %collective-permute-done.10.refs_1_, f32[9,256,256]{2,1,0:T(8,128)} %shard_map.83.refs_2_), custom_call_target="tpu_custom_call", output_to_operand_aliasing={{}: (2, {})} | custom-call | flops 1048576 | bytes 1048576 | tf_op jit(solution)/shard_map/pallas_call | solution.py:298
  59.7 0.8 %shard_map.85 = f32[9,256,256]{2,1,0:T(8,128)} custom-call(bf16[9,32,256]{2,1,0:T(8,128)(2,1)S(1)} %collective-permute-done.8.refs_0_, f32[9,256,256]{2,1,0:T(8,128)} %shard_map.84.refs_1_), custom_call_target="tpu_custom_call", output_to_operand_aliasing={{}: (1, {})} | custom-call | flops 1048576 | bytes 524288 | tf_op jit(solution)/shard_map/pallas_call | solution.py:298
  (26 shorter events, 1.6 us)
Async XLA Ops:
  1.5 6.2 %collective-permute-start = (bf16[6,16,256]{2,1,0:T(8,128)(2,1)S(1)}, bf16[6,16,256]{2,1,0:T(8,128)(2,1)S(1)}, u32[]{:S(2)}, u32[]{:S(2)}) collective-permute-start(bf16[6,16,256]{2,1,0:T(8,128)(2,1)S(1)} %get-tuple-element.19.last), channel_id=1, source_target_pairs={{0,1},{1,2},{2,3},{3,4},{4,5},{5,6},{6,7},{7,8},{8,9},{9,10},{10,1... | collective-permute-start | bytes 147464 | tf_op jit(solution)/shard_map/ppermute | solution.py:355
  3.9 5.2 %collective-permute-start.1 = (bf16[6,16,256]{2,1,0:T(8,128)(2,1)S(1)}, bf16[6,16,256]{2,1,0:T(8,128)(2,1)S(1)}, u32[]{:S(2)}, u32[]{:S(2)}) collective-permute-start(bf16[6,16,256]{2,1,0:T(8,128)(2,1)S(1)} %get-tuple-element.20.first), channel_id=1, source_target_pairs={{1,0},{2,1},{3,2},{4,3},{5,4},{6,5},{7,6},{8,7},{9,8},{10,9},{11,1... | collective-permute-start | bytes 147464 | tf_op jit(solution)/shard_map/ppermute | solution.py:355
  14.7 4.4 %collective-permute-start.2 = (bf16[4,9,32,256]{3,2,1,0:T(8,128)(2,1)S(1)}, bf16[4,9,32,256]{3,2,1,0:T(8,128)(2,1)S(1)}, u32[]{:S(2)}, u32[]{:S(2)}) collective-permute-start(bf16[4,9,32,256]{3,2,1,0:T(8,128)(2,1)S(1)} %shard_map.79), channel_id=1, source_target_pairs={{0,1},{1,0},{2,3},{3,2},{4,5},{5,4},{6,7},{7,6},{8,9},{9,8},{10,11... | collective-permute-start | bytes 1769480 | tf_op jit(solution)/shard_map/ppermute | solution.py:360
  19.1 34.9 %copy-start = (bf16[9,256,256]{2,1,0:T(8,128)(2,1)S(1)}, bf16[9,256,256]{2,1,0:T(8,128)(2,1)}, u32[]{:S(2)}) copy-start(bf16[9,256,256]{2,1,0:T(8,128)(2,1)} %param.6) | copy-start | bytes 3538948
  19.2 34.9 %copy-start.1 = (s32[6,8]{1,0:T(8,128)S(1)}, s32[6,8]{1,0:T(8,128)}, u32[]{:S(2)}) copy-start(s32[6,8]{1,0:T(8,128)} %codes.5) | copy-start | bytes 580
  19.2 34.8 %copy-start.2 = (s32[6]{0:T(128)S(1)}, s32[6]{0:T(128)}, u32[]{:S(2)}) copy-start(s32[6]{0:T(128)} %pos.3) | copy-start | bytes 76
  19.2 7.2 %collective-permute-start.3 = (bf16[2,9,32,256]{3,2,1,0:T(8,128)(2,1)S(1)}, bf16[2,9,32,256]{3,2,1,0:T(8,128)(2,1)S(1)}, u32[]{:S(2)}, u32[]{:S(2)}) collective-permute-start(bf16[2,9,32,256]{3,2,1,0:T(8,128)(2,1)S(1)} %shard_map.80), channel_id=1, source_target_pairs={{0,2},{1,5},{2,0},{3,7},{4,6},{5,1},{6,4},{7,3},{8,10},{9,13},{10,... | collective-permute-start | bytes 884744 | tf_op jit(solution)/shard_map/ppermute | solution.py:366
  26.5 5.2 %collective-permute-start.4 = (bf16[9,32,256]{2,1,0:T(8,128)(2,1)S(1)}, bf16[9,32,256]{2,1,0:T(8,128)(2,1)S(1)}, u32[]{:S(2)}, u32[]{:S(2)}) collective-permute-start(bf16[9,32,256]{2,1,0:T(8,128)(2,1)S(1)} %shard_map.82), channel_id=1, source_target_pairs={{0,4},{1,3},{2,6},{3,1},{4,0},{5,7},{6,2},{7,5},{8,12},{9,11},{10,... | collective-permute-start | bytes 442376 | tf_op jit(solution)/shard_map/ppermute | solution.py:366
  31.7 8.8 %collective-permute-start.5 = (bf16[9,32,256]{2,1,0:T(8,128)(2,1)S(1)}, bf16[9,32,256]{2,1,0:T(8,128)(2,1)S(1)}, u32[]{:S(2)}, u32[]{:S(2)}) collective-permute-start(bf16[9,32,256]{2,1,0:T(8,128)(2,1)S(1)} %add_convert_fusion.1), channel_id=1, source_target_pairs={{0,8},{1,9},{2,10},{3,11},{4,12},{5,13},{6,14},{7,15},{8,0},{9,1},... | collective-permute-start | bytes 442376 | tf_op jit(solution)/shard_map/ppermute | solution.py:360
  40.6 6.8 %collective-permute-start.6 = (bf16[9,32,256]{2,1,0:T(8,128)(2,1)S(1)}, bf16[9,32,256]{2,1,0:T(8,128)(2,1)S(1)}, u32[]{:S(2)}, u32[]{:S(2)}) collective-permute-start(bf16[9,32,256]{2,1,0:T(8,128)(2,1)S(1)} %add_convert_fusion.refs_0_), channel_id=1, source_target_pairs={{0,4},{1,3},{2,6},{3,1},{4,0},{5,7},{6,2},{7,5},{8,12},{9,11},{10,... | collective-permute-start | bytes 442376 | tf_op jit(solution)/shard_map/ppermute | solution.py:366
  40.7 12.8 %collective-permute-start.9 = (bf16[9,32,256]{2,1,0:T(8,128)(2,1)S(1)}, bf16[9,32,256]{2,1,0:T(8,128)(2,1)S(1)}, u32[]{:S(2)}, u32[]{:S(2)}) collective-permute-start(bf16[9,32,256]{2,1,0:T(8,128)(2,1)S(1)} %add_convert_fusion.refs_0_), channel_id=1, source_target_pairs={{0,2},{1,5},{2,0},{3,7},{4,6},{5,1},{6,4},{7,3},{8,10},{9,13},{10,... | collective-permute-start | bytes 442376 | tf_op jit(solution)/shard_map/ppermute | solution.py:366
  47.4 6.6 %collective-permute-start.7 = (bf16[9,32,256]{2,1,0:T(8,128)(2,1)S(1)}, bf16[9,32,256]{2,1,0:T(8,128)(2,1)S(1)}, u32[]{:S(2)}, u32[]{:S(2)}) collective-permute-start(bf16[9,32,256]{2,1,0:T(8,128)(2,1)S(1)} %collective-permute-done.6.refs_1_), channel_id=1, source_target_pairs={{0,2},{1,5},{2,0},{3,7},{4,6},{5,1},{6,4},{7,3},{8,10},{9,13},{10,... | collective-permute-start | bytes 442376 | tf_op jit(solution)/shard_map/ppermute | solution.py:366
  47.5 5.9 %collective-permute-start.14 = (bf16[6,16,256]{2,1,0:T(8,128)(2,1)S(1)}, bf16[6,16,256]{2,1,0:T(8,128)(2,1)S(1)}, u32[]{:S(2)}, u32[]{:S(2)}) collective-permute-start(bf16[6,16,256]{2,1,0:T(8,128)(2,1)S(1)} %get-tuple-element.17.first), channel_id=1, source_target_pairs={{1,0},{2,1},{3,2},{4,3},{5,4},{6,5},{7,6},{8,7},{9,8},{10,9},{11,1... | collective-permute-start | bytes 147464 | tf_op jit(solution)/shard_map/ppermute | solution.py:355
  48.8 5.2 %collective-permute-start.13 = (bf16[6,16,256]{2,1,0:T(8,128)(2,1)S(1)}, bf16[6,16,256]{2,1,0:T(8,128)(2,1)S(1)}, u32[]{:S(2)}, u32[]{:S(2)}) collective-permute-start(bf16[6,16,256]{2,1,0:T(8,128)(2,1)S(1)} %get-tuple-element.18.last), channel_id=1, source_target_pairs={{0,1},{1,2},{2,3},{3,4},{4,5},{5,6},{6,7},{7,8},{8,9},{9,10},{10,1... | collective-permute-start | bytes 147464 | tf_op jit(solution)/shard_map/ppermute | solution.py:355
  51.8 5.8 %collective-permute-start.11 = (bf16[9,32,256]{2,1,0:T(8,128)(2,1)S(1)}, bf16[9,32,256]{2,1,0:T(8,128)(2,1)S(1)}, u32[]{:S(2)}, u32[]{:S(2)}) collective-permute-start(bf16[9,32,256]{2,1,0:T(8,128)(2,1)S(1)} %add_convert_fusion.refs_0_), channel_id=1, source_target_pairs={{0,1},{1,0},{2,3},{3,2},{4,5},{5,4},{6,7},{7,6},{8,9},{9,8},{10,11... | collective-permute-start | bytes 442376 | tf_op jit(solution)/shard_map/ppermute | solution.py:360
  53.4 4.2 %collective-permute-start.12 = (bf16[9,32,256]{2,1,0:T(8,128)(2,1)S(1)}, bf16[9,32,256]{2,1,0:T(8,128)(2,1)S(1)}, u32[]{:S(2)}, u32[]{:S(2)}) collective-permute-start(bf16[9,32,256]{2,1,0:T(8,128)(2,1)S(1)} %collective-permute-done.6.refs_1_), channel_id=1, source_target_pairs={{0,1},{1,0},{2,3},{3,2},{4,5},{5,4},{6,7},{7,6},{8,9},{9,8},{10,11... | collective-permute-start | bytes 442376 | tf_op jit(solution)/shard_map/ppermute | solution.py:360
  53.5 5.3 %collective-permute-start.10 = (bf16[9,32,256]{2,1,0:T(8,128)(2,1)S(1)}, bf16[9,32,256]{2,1,0:T(8,128)(2,1)S(1)}, u32[]{:S(2)}, u32[]{:S(2)}) collective-permute-start(bf16[9,32,256]{2,1,0:T(8,128)(2,1)S(1)} %collective-permute-done.9.refs_4_), channel_id=1, source_target_pairs={{0,1},{1,0},{2,3},{3,2},{4,5},{5,4},{6,7},{7,6},{8,9},{9,8},{10,11... | collective-permute-start | bytes 442376 | tf_op jit(solution)/shard_map/ppermute | solution.py:360
  53.9 5.8 %collective-permute-start.8 = (bf16[9,32,256]{2,1,0:T(8,128)(2,1)S(1)}, bf16[9,32,256]{2,1,0:T(8,128)(2,1)S(1)}, u32[]{:S(2)}, u32[]{:S(2)}) collective-permute-start(bf16[9,32,256]{2,1,0:T(8,128)(2,1)S(1)} %collective-permute-done.7.refs_0_), channel_id=1, source_target_pairs={{0,1},{1,0},{2,3},{3,2},{4,5},{5,4},{6,7},{7,6},{8,9},{9,8},{10,11... | collective-permute-start | bytes 442376 | tf_op jit(solution)/shard_map/ppermute | solution.py:360
where the time goes:
time: 60.8 us; the launch traced here: 60.5 us
  starting transfers between devices  21.9 us (36%)
  waiting for transfers between devices  21.1 us (35%)
  Pallas kernels  15.7 us (26%)
  local copies, waits for them, and re-layouts  0.86 us (1%)
  between operations  0.8 us (1%)
    ppermute x5, waiting for transfers between devices, crossed(): return lax.ppermute(value, 'tile', pairs)  13.1 us
    ppermute x4, starting transfers between devices, from_behind(): lax.ppermute(value, 'tile', [(source, source + steps) for source in range...  7.99 us
    ppermute x6, starting transfers between devices, swap(): lax.ppermute(value, 'tile', [(source, source ^ bit) for source in range(c...  7.65 us
    ppermute x6, waiting for transfers between devices, swap(): lax.ppermute(value, 'tile', [(source, source ^ bit) for source in range(c...  6.58 us
    ppermute x5, starting transfers between devices, crossed(): return lax.ppermute(value, 'tile', pairs)  6.26 us
    pallas_call x1, Pallas kernels, forward(): call(forward_kernel, 2 * slots * side * side * wide * wide, 8 << 20, in_s...  4.35 us
    pallas_call x1, Pallas kernels, backward(): call(functools.partial(backward_kernel, tiles), 18 * count * side * side...  3.6 us
    pallas_call x3, Pallas kernels, collect(): call(functools.partial(collect_kernel, scale, plan), 1 << 20, count << 19...  2.8 us
  transfers between devices with their start and end apart: 15, of which 6 were waited for; matrix products, arithmetic and copies ran while one was open for 0% of the time, Pallas kernels for 15%

commit v1 on v0

v1 whole, which is shorter than its diff:
```python
import functools
import math

import jax
import jax.numpy as jnp
from jax import lax
from jax.experimental import pallas as pl
from jax.experimental.pallas import tpu as pltpu
from jax.sharding import PartitionSpec as P


ROOT_HALF = 0.7071067811865476
INV_ROOT_TAU = 0.3989422804014327
F32 = jnp.float32
BF16 = jnp.bfloat16
VMEM = pl.BlockSpec(memory_space=pltpu.VMEM)
SMEM = pl.BlockSpec(memory_space=pltpu.SMEM)
ANY = pl.BlockSpec(memory_space=pl.ANY)
LIMIT = 16 << 20


def held(shape, dtype):
    return pltpu.VMEM(shape, dtype)


def far(value):
    return pltpu.with_memory_space_constraint(value, pltpu.HBM)


def call(kernel, flops, moved, **options):
    return pl.pallas_call(
        kernel,
        compiler_params=pltpu.CompilerParams(vmem_limit_bytes=LIMIT),
        cost_estimate=pl.CostEstimate(flops=flops, bytes_accessed=moved, transcendentals=0),
        **options,
    )


def place():
    index = lax.axis_index("tile").astype(jnp.int32)
    return lax.rem(index, 2), lax.rem(lax.div(index, 2), 4)


def put_edges(out, own_row, side, slots, cross, link, codes, tile):
    core = place()[0]

    def named(code, row, begin, of_other_core):
        own = own_row(jnp.clip(code - slots, 0, slots - 1), row)
        away = jnp.clip(code - begin, 0, slots - 1)
        away = jnp.where(of_other_core, cross[away].astype(F32), link[away].astype(F32))
        inside = (code >= slots) & (code < 2 * slots)
        return jnp.where(inside, own, jnp.where(code >= 0, away, 0.0))

    top = [named(codes[tile, j], side - 1, 0, core == 1) for j in (0, 4, 5)]
    put_columns(out, (tile, 0), *top)
    bottom = [named(codes[tile, j], 0, 2 * slots, core == 0) for j in (1, 6, 7)]
    put_columns(out, (tile, 1), *bottom)


def put_sends(to_core, to_link, tile, first, last):
    even = place()[0] == 0
    to_core[tile] = jnp.where(even, last.astype(F32), first.astype(F32)).astype(BF16)
    to_link[tile] = jnp.where(even, first.astype(F32), last.astype(F32)).astype(BF16)


def put_columns(out, at, center, left, right):
    axis = center.ndim - 2
    side, channels = center.shape[-2:]
    cell = lax.broadcasted_iota(jnp.int32, center.shape, axis)
    shifted = pltpu.roll(jnp.where(cell == side - 1, left, center), 1, axis)
    out[at + (Ellipsis, slice(0, channels))] = shifted.astype(BF16)
    out[at + (Ellipsis, slice(channels, 2 * channels))] = center.astype(BF16)
    shifted = pltpu.roll(jnp.where(cell == 0, right, center), side - 1, axis)
    out[at + (Ellipsis, slice(2 * channels, 3 * channels))] = shifted.astype(BF16)


def put_inner(out, maps, codes, tile, at):
    slots = maps.shape[0]

    def neighbour(code):
        return jnp.where(code >= 0, maps[jnp.clip(code - slots, 0, slots - 1)].astype(F32), 0.0)

    put_columns(
        out, (at,), maps[tile].astype(F32), neighbour(codes[tile, 2]), neighbour(codes[tile, 3])
    )


def rows_for(inner, edge, tile, step):
    side = inner.shape[1]
    if step == 1:
        return inner[tile]
    if step == 0:
        return jnp.concatenate([edge[tile, 0][None], inner[tile, : side - 1]], axis=0)
    return jnp.concatenate([inner[tile, 1:], edge[tile, 1][None]], axis=0)


def inner_product(inner, weights, tile):
    side, _, wide = inner.shape[1:]
    channels = wide // 3
    total = jnp.dot(
        inner[tile].reshape(side * side, wide),
        weights[wide : 2 * wide],
        preferred_element_type=F32,
    )
    blank = jnp.zeros((side, channels), F32)
    short = (side - 1) * side
    upper = jnp.dot(
        inner[tile, : side - 1].reshape(short, wide), weights[:wide], preferred_element_type=F32
    )
    lower = jnp.dot(
        inner[tile, 1:].reshape(short, wide), weights[2 * wide :], preferred_element_type=F32
    )
    total += jnp.concatenate([blank, upper], axis=0)
    total += jnp.concatenate([lower, blank], axis=0)
    return total.reshape(side, side, channels)


def load_kernel(
    codes, maps, weights, grads, inner, weights_out, grads_out, to_core, to_link, tiles, sems
):
    loads = [
        pltpu.make_async_copy(source, target, sems.at[k])
        for k, (source, target) in enumerate(
            [(maps, tiles), (weights, weights_out), (grads, grads_out)]
        )
    ]
    for load in loads:
        load.start()
    loads[0].wait()
    slots, side = maps.shape[:2]
    for tile in range(slots):
        put_sends(to_core, to_link, tile, tiles[tile, 0], tiles[tile, side - 1])
        put_inner(inner, tiles, codes, tile, tile)
    loads[1].wait()
    loads[2].wait()


def load(codes, maps, weights, grads):
    slots, side, _, channels = maps.shape
    rims = (slots, side, channels)
    return call(
        load_kernel,
        1 << 20,
        6 << 20,
        in_specs=[SMEM, ANY, ANY, ANY],
        out_specs=[VMEM] * 5,
        out_shape=[
            held((slots, side, side, 3 * channels), BF16),
            held(weights.shape, BF16),
            held(grads.shape, BF16),
            held(rims, BF16),
            held(rims, BF16),
        ],
        scratch_shapes=[pltpu.VMEM(maps.shape, BF16), pltpu.SemaphoreType.DMA((3,))],
    )(far(codes), far(maps), far(weights), far(grads))


def product_kernel(inner, weights, partial):
    for tile in range(inner.shape[0]):
        partial[tile] = inner_product(inner, weights, tile)


def product(inner, weights):
    slots, side, _, wide = inner.shape
    return call(
        product_kernel,
        2 * slots * side * side * wide * wide,
        6 << 20,
        in_specs=[VMEM, VMEM],
        out_specs=VMEM,
        out_shape=held((slots, side, side, wide // 3), F32),
    )(inner, weights)


def forward_kernel(
    codes, pos, partial, inner, cross, link, weights, grads,
    act, grad, edge, to_core, to_link, codes_held, pos_held, sems,
):
    slots, side, _, channels = partial.shape
    wide = 3 * channels
    loads = [
        pltpu.make_async_copy(codes, codes_held, sems.at[0]),
        pltpu.make_async_copy(pos, pos_held, sems.at[1]),
    ]
    for item in loads:
        item.start()

    def finish(value, outer, gate):
        cumulative = 0.5 * (1.0 + lax.erf(value * ROOT_HALF))
        density = jnp.exp(-0.5 * value * value) * INV_ROOT_TAU
        slope = cumulative + value * density
        return (
            (value * cumulative * gate).astype(BF16),
            (outer.astype(F32) * slope * gate).astype(BF16),
        )

    loads[1].wait()
    gates = [jnp.where(pos_held[tile] >= 0, 1.0, 0.0) for tile in range(slots)]
    rows = slice(1, side - 1)
    for tile in range(slots):
        act[tile, rows], grad[tile, rows] = finish(
            partial[tile, rows], grads[tile, rows], gates[tile]
        )
    loads[0].wait()
    center = slice(channels, 2 * channels)
    for tile in range(slots):
        put_edges(
            edge, lambda slot, row: inner[slot, row, :, center].astype(F32),
            side, slots, cross, link, codes_held, tile,
        )
    for end, row, part in ((0, 0, 0), (1, side - 1, 2)):
        added = jnp.dot(
            edge[:, end].reshape(slots * side, wide),
            weights[part * wide : (part + 1) * wide],
            preferred_element_type=F32,
        ).reshape(slots, side, channels)
        for tile in range(slots):
            value, outer = finish(
                partial[tile, row] + added[tile], grads[tile, row], gates[tile]
            )
            act[tile, row] = value
            grad[tile, row] = outer
    for tile in range(slots):
        put_sends(to_core, to_link, tile, grad[tile, 0], grad[tile, side - 1])


def forward(codes, pos, partial, inner, cross, link, weights, grads):
    slots, side, _, channels = partial.shape
    wide = 3 * channels
    return call(
        forward_kernel,
        4 * slots * side * wide * channels,
        8 << 20,
        in_specs=[ANY, ANY] + [VMEM] * 6,
        out_specs=[VMEM] * 5,
        out_shape=[
            held(partial.shape, BF16),
            held(partial.shape, BF16),
            held((slots, 2, side, wide), BF16),
            held(cross.shape, BF16),
            held(cross.shape, BF16),
        ],
        scratch_shapes=[
            pltpu.SMEM(codes.shape, jnp.int32),
            pltpu.SMEM(pos.shape, jnp.int32),
            pltpu.SemaphoreType.DMA((2,)),
        ],
    )(far(codes), far(pos), partial, inner, cross, link, weights, grads)


def kernel_grad_kernel(other, inner, edge, grad, out):
    slots, side, _, channels = grad.shape
    lanes = channels // 2
    outer = grad[...].reshape(slots * side * side, channels)
    core = place()[0]
    half = 1 - core if other else core
    for row_step in range(3):
        for col_step in range(3):
            start = pl.multiple_of(col_step * channels + half * lanes, lanes)
            part = pl.ds(start, lanes)
            if row_step == 1:
                rows = inner[:, :, :, part]
            elif row_step == 0:
                rows = jnp.concatenate([edge[:, :1, :, part], inner[:, : side - 1, :, part]], axis=1)
            else:
                rows = jnp.concatenate([inner[:, 1:, :, part], edge[:, 1:, :, part]], axis=1)
            made = lax.dot_general(
                rows.reshape(slots * side * side, lanes),
                outer,
                (((0,), (0,)), ((), ())),
                preferred_element_type=F32,
            )
            out[:, 3 * row_step + col_step] = made.reshape(4, lanes // 4, channels).astype(out.dtype)


def kernel_grad(other, inner, edge, grad, dtype):
    slots, side, _, channels = grad.shape
    return call(
        functools.partial(kernel_grad_kernel, other),
        9 * slots * side * side * channels * channels,
        6 << 20,
        in_specs=[VMEM, VMEM, VMEM],
        out_specs=VMEM,
        out_shape=held((4, 9, channels // 8, channels), dtype),
    )(inner, edge, grad)


def spread_kernel(keep, recv, own, *sends):
    quad = place()[1]
    own[...] = keep[quad] + recv[quad].astype(F32)
    for k, send in enumerate(sends):
        other = quad ^ (k + 1)
        send[...] = (keep[other] + recv[other].astype(F32)).astype(BF16)


def spread(keep, recv):
    piece = keep.shape[1:]
    return call(
        spread_kernel,
        1 << 20,
        3 << 20,
        in_specs=[VMEM, VMEM],
        out_specs=[VMEM] * 4,
        out_shape=[held(piece, F32)] + [held(piece, BF16)] * 3,
    )(keep, recv)


def collect_kernel(scale, plan, *refs):
    count = len(plan)
    core, quad = place()
    pieces, out = refs[:count], refs[-3]
    rows, sem = refs[-2], refs[-1]
    depth = pieces[0].shape[-2]
    copies = []
    for k, piece in enumerate(pieces):
        rows[k] = piece[...].astype(F32) * scale
        half = 1 - core if plan[k][0] else core
        slot = half * 4 + (quad ^ plan[k][1])
        start = pl.multiple_of(slot * depth, depth)
        copy = pltpu.make_async_copy(rows.at[k], out.at[:, pl.ds(start, depth), :], sem.at[k])
        copy.start()
        copies.append(copy)
    for copy in copies:
        copy.wait()


def collect(plan, pieces, scale, whole, base):
    taps, depth, channels = pieces[0].shape
    count = len(pieces)
    operands = list(pieces)
    specs = [VMEM] * count
    aliases = {}
    if base is not None:
        operands.append(base)
        specs.append(ANY)
        aliases = {count: 0}
    return call(
        functools.partial(collect_kernel, scale, plan),
        1 << 20,
        count << 19,
        in_specs=specs,
        out_specs=ANY,
        out_shape=pltpu.HBM(whole, F32),
        input_output_aliases=aliases,
        scratch_shapes=[
            pltpu.VMEM((count, taps, depth, channels), F32),
            pltpu.SemaphoreType.DMA((count,)),
        ],
    )(*operands)


def backward_kernel(codes, pos, act, grad, cross, link, weights, act_out, out, inner, edge, made, sems):
    slots, side, _, channels = grad.shape
    store = pltpu.make_async_copy(act, act_out, sems.at[slots])
    store.start()
    for tile in range(slots):
        put_inner(inner, grad, codes, tile, tile)
        put_edges(
            edge, lambda slot, row: grad[slot, row].astype(F32),
            side, slots, cross, link, codes, tile,
        )
    stores = [store]
    for tile in range(slots):
        total = None
        for row_step in range(3):
            rows = rows_for(inner, edge, tile, row_step).reshape(side * side, 3 * channels)
            for col_step in range(3):
                tap = 3 * (2 - row_step) + 2 - col_step
                part = lax.dot_general(
                    rows[:, col_step * channels : (col_step + 1) * channels],
                    weights[tap * channels : (tap + 1) * channels],
                    (((1,), (1,)), ((), ())),
                    preferred_element_type=F32,
                )
                total = part if total is None else total + part
        gate = jnp.where(pos[tile] >= 0, 1.0, 0.0)
        made[tile] = (total * gate).astype(BF16).reshape(side, side, channels)
        store = pltpu.make_async_copy(made.at[tile], out.at[tile], sems.at[tile])
        store.start()
        stores.append(store)
    for store in stores:
        store.wait()


def backward(codes, pos, act, grad, cross, link, weights):
    slots, side, _, channels = grad.shape
    return call(
        backward_kernel,
        18 * slots * side * side * channels * channels,
        4 << 20,
        in_specs=[SMEM, SMEM] + [VMEM] * 5,
        out_specs=[ANY, ANY],
        out_shape=[pltpu.HBM(grad.shape, BF16)] * 2,
        scratch_shapes=[
            pltpu.VMEM((slots, side, side, 3 * channels), BF16),
            pltpu.VMEM((slots, 2, side, 3 * channels), BF16),
            pltpu.VMEM(grad.shape, BF16),
            pltpu.SemaphoreType.DMA((slots + 1,)),
        ],
    )(codes, pos, act, grad, cross, link, weights)


def edge_swaps(to_core, to_link):
    count = lax.axis_size("tile")
    ends = [(s, s + 1) for s in range(1, count - 1, 2)]
    link = lax.ppermute(to_link, "tile", ends + [(t, s) for s, t in ends])
    return swap(to_core, 1), link


def swap(value, bit):
    count = lax.axis_size("tile")
    return lax.ppermute(value, "tile", [(source, source ^ bit) for source in range(count)])


def sum_high(total, high):
    shape = total.shape
    index = lax.axis_index("tile")
    for bit in high[:-1]:
        flat = total.reshape(2, -1, shape[-1])
        upper = (index & bit) != 0
        arrived = swap(jnp.where(upper, flat[0], flat[1]).astype(BF16), bit)
        total = jnp.where(upper, flat[1], flat[0]) + arrived.astype(F32)
    mine = total.astype(BF16)
    other = swap(mine, high[-1])
    total = (mine.astype(F32) + other.astype(F32)).astype(BF16)
    for bit in reversed(high[:-1]):
        upper = (index & bit) != 0
        other = swap(total, bit)
        total = jnp.concatenate(
            [jnp.where(upper, other, total), jnp.where(upper, total, other)], axis=0
        )
    return total.reshape(shape)


def step(features, weights, grad_out, tile_pos, neighbours):
    slots, side, _, channels = features.shape
    devices = lax.axis_size("tile")
    flat = weights.reshape(9 * channels, channels)
    inner, flat, grads, to_core, to_link = load(neighbours, features, flat, grad_out)
    cross, link = edge_swaps(to_core, to_link)
    partial = product(inner, flat)
    activation, grad, edge, to_core, to_link = forward(
        neighbours, tile_pos, partial, inner, cross, link, flat, grads
    )
    send = kernel_grad(True, inner, edge, grad, BF16)
    recv = swap(send, 1)
    keep = kernel_grad(False, inner, edge, grad, F32)
    own, *sends = spread(keep, recv)
    got = [swap(sends[k], 2 * (k + 1)) for k in (2, 0, 1)]
    total = own + got[0].astype(F32) + got[1].astype(F32) + got[2].astype(F32)
    piece = sum_high(total, [8 << k for k in range(devices.bit_length() - 4)])
    scale = 1.0 / math.sqrt(slots * devices * side * side)
    whole = weights.shape
    pieces = [piece] + [swap(piece, 2 * k) for k in (1, 2, 3)]
    its = [swap(piece, 1)]
    its += [swap(item, 1) for item in pieces[1:3]]
    its.append(swap(pieces[3], 1))
    weight_grad = collect(((0, 0), (1, 0)), [pieces[0], its[0]], scale, whole, None)
    weight_grad = collect(
        ((0, 1), (0, 2), (0, 3), (1, 1), (1, 2)),
        pieces[1:] + its[1:3], scale, whole, weight_grad,
    )
    weight_grad = collect(((1, 3),), its[3:], scale, whole, weight_grad)
    cross, link = edge_swaps(to_core, to_link)
    activation, input_grad = backward(
        neighbours, tile_pos, activation, grad, cross, link,
        weights.reshape(9 * channels, channels),
    )
    return (activation, weight_grad, input_grad)


def solution(mesh):
    in_specs = (
        P(("groups", "tile"), None, None, None),
        P(),
        P(("groups", "tile"), None, None, None),
        P(("groups", "tile")),
        P(("groups", "tile"), None),
    )
    out_specs = (
        P(("groups", "tile"), None, None, None),
        P("groups", None, None),
        P(("groups", "tile"), None, None, None),
    )
    return jax.shard_map(step, mesh=mesh, in_specs=in_specs, out_specs=out_specs, check_vma=False)
```

time: 60.8 us -> 53.2 us (0.88)
  waiting for transfers between devices: 21.1 us -> 17.9 us
  starting transfers between devices: 21.9 us -> 18.8 us
  local copies, waits for them, and re-layouts: 0.86 us -> 0.02 us
    ppermute x9 -> x2, waiting for transfers between devices: 14.5 us -> 0.01 us  [edge_swaps(): link = lax.ppermute(to_link, 'tile', ends + [(t, s) for s, t in ends])]
    ppermute x9 -> x2, starting transfers between devices: 14.3 us -> 1.3 us  [edge_swaps(): link = lax.ppermute(to_link, 'tile', ends + [(t, s) for s, t in ends])]
    ppermute x6 -> x14, waiting for transfers between devices: 6.58 us -> 17.9 us  [swap(): lax.ppermute(value, 'tile', [(source, source ^ bit) for source in range(c...]
    ppermute x6 -> x14, starting transfers between devices: 7.65 us -> 17.5 us  [swap(): lax.ppermute(value, 'tile', [(source, source ^ bit) for source in range(c...]
    squeeze x1 -> x0, local copies, waits for them, and re-layouts: 0.84 us -> none  [step(): first, last = (features[:, 0], features[:, -1])]
    pallas_call x5 -> x4, Pallas kernels: 8.09 us -> 7.58 us  [the longest x1 3.54 us: backward(): call(backward_kernel, 18 * slots * side * side * channels * channels, 4 <...]
  transfers between devices with their start and end apart: 15 -> 16, of which waited for: 6 -> 8; matrix products, arithmetic and copies ran while one was open for 0% -> 0% of each run, Pallas kernels for 15% -> 16%
where the time goes in v1:
time: 53.2 us; the launch traced here: 53 us
  starting transfers between devices  18.8 us (35%)
  waiting for transfers between devices  17.9 us (34%)
  Pallas kernels  15.2 us (29%)
  between operations  0.82 us (2%)
    ppermute x14, waiting for transfers between devices, swap(): lax.ppermute(value, 'tile', [(source, source ^ bit) for source in range(c...  17.9 us
    ppermute x14, starting transfers between devices, swap(): lax.ppermute(value, 'tile', [(source, source ^ bit) for source in range(c...  17.5 us
    pallas_call x1, Pallas kernels, backward(): call(backward_kernel, 18 * slots * side * side * channels * channels, 4 <...  3.54 us
    pallas_call x3, Pallas kernels, collect(): call(functools.partial(collect_kernel, scale, plan), 1 << 20, count << 19...  2.79 us
    pallas_call x1, Pallas kernels, load(): call(load_kernel, 1 << 20, 6 << 20, in_specs=[SMEM, ANY, ANY, ANY], out_s...  2.48 us
    pallas_call x2, Pallas kernels, kernel_grad(): call(functools.partial(kernel_grad_kernel, other), 9 * slots * side * sid...  2.38 us
    pallas_call x1, Pallas kernels, forward(): call(forward_kernel, 4 * slots * side * wide * channels, 8 << 20, in_spec...  2 us
    pallas_call x1, Pallas kernels, product(): call(product_kernel, 2 * slots * side * side * wide * wide, 6 << 20, in_s...  1.91 us
  transfers between devices with their start and end apart: 16, of which 8 were waited for; matrix products, arithmetic and copies ran while one was open for 0% of the time, Pallas kernels for 16%

profile of v1, /device:TPU:0, one launch (start us, length us, event | category | flops | bytes accessed | tf_op | source)
XLA Modules:
  0.0 53.0 jit_solution(15588168281818343389)
XLA Ops:
  0.6 2.5 %shard_map.76 = (bf16[6,16,16,768]{3,2,1,0:T(8,128)(2,1)S(1)}, bf16[2304,256]{1,0:T(8,128)(2,1)S(1)}, bf16[6,16,16,256]{3,2,1,0:T(8,128)(2,1)S(1)}, bf16[6,16,25...) custom-call(s32[6,8]{1,0:T(8,128)} %codes.5, bf16[6,16,16,256]{3,2,1,0:T(8,128)(2,1)} %maps.1, bf16[2304,256]{1,0:T(8,128)(2,1)} %bitcast.1, ...), custom_call_target="tpu_custom_call" | custom-call | flops 1048576 | bytes 6291456 | tf_op jit(solution)/shard_map/pallas_call | solution.py:141
  3.7 0.7 %collective-permute-start.1 = (bf16[6,16,256]{2,1,0:T(8,128)(2,1)S(1)}, bf16[6,16,256]{2,1,0:T(8,128)(2,1)S(1)}, u32[]{:S(2)}, u32[]{:S(2)}) collective-permute-start(bf16[6,16,256]{2,1,0:T(8,128)(2,1)S(1)} %get-tuple-element.22), channel_id=1, source_target_pairs={{1,2},{3,4},{5,6},{7,8},{9,10},{11,12},{13,14},{2,1},{4,3},{6,5},{... | collective-permute-start | bytes 147464 | tf_op jit(solution)/shard_map/ppermute | solution.py:406
  4.3 1.9 %shard_map.77.partial = f32[6,16,16,256]{3,2,1,0:T(8,128)S(1)} custom-call(bf16[6,16,16,768]{3,2,1,0:T(8,128)(2,1)S(1)} %get-tuple-element.19.inner, bf16[2304,256]{1,0:T(8,128)(2,1)S(1)} %get-tuple-element.20.weights), custom_call_target="tpu_custom_call" | custom-call | flops 1811939328 | bytes 6291456 | tf_op jit(solution)/shard_map/pallas_call | solution.py:165
  6.3 2.0 %shard_map.78 = (bf16[6,16,16,256]{3,2,1,0:T(8,128)(2,1)S(1)}, bf16[6,16,16,256]{3,2,1,0:T(8,128)(2,1)S(1)}, bf16[6,2,16,768]{3,2,1,0:T(8,128)(2,1)S(1)}, bf16[6...) custom-call(s32[6,8]{1,0:T(8,128)} %codes.5, s32[6]{0:T(128)} %pos.3, f32[6,16,16,256]{3,2,1,0:T(8,128)S(1)} %shard_map.77.partial, ...), custom_call_target="tpu_custom_call" | custom-call | flops 75497472 | bytes 8388608 | tf_op jit(solution)/shard_map/pallas_call | solution.py:230
  8.3 1.2 %shard_map.81 = bf16[4,9,32,256]{3,2,1,0:T(8,128)(2,1)S(1)} custom-call(bf16[6,16,16,768]{3,2,1,0:T(8,128)(2,1)S(1)} %get-tuple-element.19.inner, bf16[6,2,16,768]{3,2,1,0:T(8,128)(2,1)S(1)} %get-tuple-element.29.edge, bf16[6,16,16,256]{3,2,1,0:T(8,128)(2,1)S(1)} %get-tuple-element.25.grad), custom_call_target="tpu_custom_call" | custom-call | flops 905969664 | bytes 6291456 | tf_op jit(solution)/shard_map/pallas_call | solution.py:278
  9.5 3.9 %collective-permute-start.4 = (bf16[4,9,32,256]{3,2,1,0:T(8,128)(2,1)S(1)}, bf16[4,9,32,256]{3,2,1,0:T(8,128)(2,1)S(1)}, u32[]{:S(2)}, u32[]{:S(2)}) collective-permute-start(bf16[4,9,32,256]{3,2,1,0:T(8,128)(2,1)S(1)} %shard_map.81), channel_id=1, source_target_pairs={{0,1},{1,0},{2,3},{3,2},{4,5},{5,4},{6,7},{7,6},{8,9},{9,8},{10,11... | collective-permute-start | bytes 1769480 | tf_op jit(solution)/shard_map/ppermute | solution.py:412
  13.4 1.2 %shard_map.80.keep = f32[4,9,32,256]{3,2,1,0:T(8,128)S(1)} custom-call(bf16[6,16,16,768]{3,2,1,0:T(8,128)(2,1)S(1)} %get-tuple-element.19.inner, bf16[6,2,16,768]{3,2,1,0:T(8,128)(2,1)S(1)} %get-tuple-element.29.edge, bf16[6,16,16,256]{3,2,1,0:T(8,128)(2,1)S(1)} %get-tuple-element.25.grad), custom_call_target="tpu_custom_call" | custom-call | flops 905969664 | bytes 6291456 | tf_op jit(solution)/shard_map/pallas_call | solution.py:278
  15.1 3.9 %collective-permute-start.5 = (bf16[9,32,256]{2,1,0:T(8,128)(2,1)S(1)}, bf16[9,32,256]{2,1,0:T(8,128)(2,1)S(1)}, u32[]{:S(2)}, u32[]{:S(2)}) collective-permute-start(bf16[9,32,256]{2,1,0:T(8,128)(2,1)S(1)} %get-tuple-element.31), channel_id=1, source_target_pairs={{0,6},{1,7},{2,4},{3,5},{4,2},{5,3},{6,0},{7,1},{8,14},{9,15},{10,... | collective-permute-start | bytes 442376 | tf_op jit(solution)/shard_map/ppermute | solution.py:412
  19.0 0.6 %collective-permute-start.6 = (bf16[9,32,256]{2,1,0:T(8,128)(2,1)S(1)}, bf16[9,32,256]{2,1,0:T(8,128)(2,1)S(1)}, u32[]{:S(2)}, u32[]{:S(2)}) collective-permute-start(bf16[9,32,256]{2,1,0:T(8,128)(2,1)S(1)} %get-tuple-element.32), channel_id=1, source_target_pairs={{0,2},{1,3},{2,0},{3,1},{4,6},{5,7},{6,4},{7,5},{8,10},{9,11},{10,... | collective-permute-start | bytes 442376 | tf_op jit(solution)/shard_map/ppermute | solution.py:412
  19.7 4.1 %collective-permute-done.5 = bf16[9,32,256]{2,1,0:T(8,128)(2,1)S(1)} collective-permute-done((bf16[9,32,256]{2,1,0:T(8,128)(2,1)S(1)}, bf16[9,32,256]{2,1,0:T(8,128)(2,1)S(1)}, u32[]{:S(2)}, u32[]{:S(2)}) %collective-permute-start.5) | collective-permute-done | bytes 147488 | tf_op jit(solution)/shard_map/ppermute | solution.py:412
  23.7 2.8 %collective-permute-done.6 = bf16[9,32,256]{2,1,0:T(8,128)(2,1)S(1)} collective-permute-done((bf16[9,32,256]{2,1,0:T(8,128)(2,1)S(1)}, bf16[9,32,256]{2,1,0:T(8,128)(2,1)S(1)}, u32[]{:S(2)}, u32[]{:S(2)}) %collective-permute-start.6) | collective-permute-done | bytes 147488 | tf_op jit(solution)/shard_map/ppermute | solution.py:412
  26.9 2.7 %collective-permute-start.8 = (bf16[9,32,256]{2,1,0:T(8,128)(2,1)S(1)}, bf16[9,32,256]{2,1,0:T(8,128)(2,1)S(1)}, u32[]{:S(2)}, u32[]{:S(2)}) collective-permute-start(bf16[9,32,256]{2,1,0:T(8,128)(2,1)S(1)} %add_convert_fusion.1), channel_id=1, source_target_pairs={{0,8},{1,9},{2,10},{3,11},{4,12},{5,13},{6,14},{7,15},{8,0},{9,1},... | collective-permute-start | bytes 442376 | tf_op jit(solution)/shard_map/ppermute | solution.py:412
  29.5 7.1 %collective-permute-done.8 = bf16[9,32,256]{2,1,0:T(8,128)(2,1)S(1)} collective-permute-done((bf16[9,32,256]{2,1,0:T(8,128)(2,1)S(1)}, bf16[9,32,256]{2,1,0:T(8,128)(2,1)S(1)}, u32[]{:S(2)}, u32[]{:S(2)}) %collective-permute-start.8) | collective-permute-done | bytes 147488 | tf_op jit(solution)/shard_map/ppermute | solution.py:412
  36.6 0.7 %collective-permute-start.12 = (bf16[9,32,256]{2,1,0:T(8,128)(2,1)S(1)}, bf16[9,32,256]{2,1,0:T(8,128)(2,1)S(1)}, u32[]{:S(2)}, u32[]{:S(2)}) collective-permute-start(bf16[9,32,256]{2,1,0:T(8,128)(2,1)S(1)} %add_convert_fusion.refs_0_), channel_id=1, source_target_pairs={{0,4},{1,5},{2,6},{3,7},{4,0},{5,1},{6,2},{7,3},{8,12},{9,13},{10,... | collective-permute-start | bytes 442376 | tf_op jit(solution)/shard_map/ppermute | solution.py:412
  37.3 0.9 %collective-permute-start.11 = (bf16[9,32,256]{2,1,0:T(8,128)(2,1)S(1)}, bf16[9,32,256]{2,1,0:T(8,128)(2,1)S(1)}, u32[]{:S(2)}, u32[]{:S(2)}) collective-permute-start(bf16[9,32,256]{2,1,0:T(8,128)(2,1)S(1)} %add_convert_fusion.refs_0_), channel_id=1, source_target_pairs={{0,2},{1,3},{2,0},{3,1},{4,6},{5,7},{6,4},{7,5},{8,10},{9,11},{10,... | collective-permute-start | bytes 442376 | tf_op jit(solution)/shard_map/ppermute | solution.py:412
  38.2 2.0 %collective-permute-start.9 = (bf16[9,32,256]{2,1,0:T(8,128)(2,1)S(1)}, bf16[9,32,256]{2,1,0:T(8,128)(2,1)S(1)}, u32[]{:S(2)}, u32[]{:S(2)}) collective-permute-start(bf16[9,32,256]{2,1,0:T(8,128)(2,1)S(1)} %add_convert_fusion.refs_0_), channel_id=1, source_target_pairs={{0,6},{1,7},{2,4},{3,5},{4,2},{5,3},{6,0},{7,1},{8,14},{9,15},{10,... | collective-permute-start | bytes 442376 | tf_op jit(solution)/shard_map/ppermute | solution.py:412
  40.2 0.7 %collective-permute-start.3 = (bf16[6,16,256]{2,1,0:T(8,128)(2,1)S(1)}, bf16[6,16,256]{2,1,0:T(8,128)(2,1)S(1)}, u32[]{:S(2)}, u32[]{:S(2)}) collective-permute-start(bf16[6,16,256]{2,1,0:T(8,128)(2,1)S(1)} %get-tuple-element.27), channel_id=1, source_target_pairs={{1,2},{3,4},{5,6},{7,8},{9,10},{11,12},{13,14},{2,1},{4,3},{6,5},{... | collective-permute-start | bytes 147464 | tf_op jit(solution)/shard_map/ppermute | solution.py:406
  41.4 2.2 %collective-permute-start.15 = (bf16[9,32,256]{2,1,0:T(8,128)(2,1)S(1)}, bf16[9,32,256]{2,1,0:T(8,128)(2,1)S(1)}, u32[]{:S(2)}, u32[]{:S(2)}) collective-permute-start(bf16[9,32,256]{2,1,0:T(8,128)(2,1)S(1)} %add_convert_fusion.refs_0_), channel_id=1, source_target_pairs={{0,1},{1,0},{2,3},{3,2},{4,5},{5,4},{6,7},{7,6},{8,9},{9,8},{10,11... | collective-permute-start | bytes 442376 | tf_op jit(solution)/shard_map/ppermute | solution.py:412
  43.8 1.4 %collective-permute-done.11.refs_0_ = bf16[9,32,256]{2,1,0:T(8,128)(2,1)S(1)} collective-permute-done((bf16[9,32,256]{2,1,0:T(8,128)(2,1)S(1)}, bf16[9,32,256]{2,1,0:T(8,128)(2,1)S(1)}, u32[]{:S(2)}, u32[]{:S(2)}) %collective-permute-start.11) | collective-permute-done | bytes 147488 | tf_op jit(solution)/shard_map/ppermute | solution.py:412
  45.2 1.4 %collective-permute-done.9.refs_2_ = bf16[9,32,256]{2,1,0:T(8,128)(2,1)S(1)} collective-permute-done((bf16[9,32,256]{2,1,0:T(8,128)(2,1)S(1)}, bf16[9,32,256]{2,1,0:T(8,128)(2,1)S(1)}, u32[]{:S(2)}, u32[]{:S(2)}) %collective-permute-start.9) | collective-permute-done | bytes 147488 | tf_op jit(solution)/shard_map/ppermute | solution.py:412
  46.6 3.5 %shard_map.79 = (bf16[6,16,16,256]{3,2,1,0:T(8,128)(2,1)}, bf16[6,16,16,256]{3,2,1,0:T(8,128)(2,1)}) custom-call(s32[6,8]{1,0:T(8,128)S(1)} %copy-done.1, s32[6]{0:T(128)S(1)} %copy-done.2, bf16[6,16,16,256]{3,2,1,0:T(8,128)(2,1)S(1)} %get-tuple-element.24.act, bf16[6,16,16,256]{3,2,1,0:T(8,128)(2,1)S(1)} %get-tuple-element.25.grad, ...), custom_call_target="tpu_custom_call" | custom-call | flops 1811939328 | bytes 4194304 | tf_op jit(solution)/shard_map/pallas_call | solution.py:387
  50.1 0.9 %shard_map.83.refs_5_ = f32[9,256,256]{2,1,0:T(8,128)} custom-call(bf16[9,32,256]{2,1,0:T(8,128)(2,1)S(1)} %add_convert_fusion.refs_0_, bf16[9,32,256]{2,1,0:T(8,128)(2,1)S(1)} %collective-permute-done.15.refs_1_), custom_call_target="tpu_custom_call" | custom-call | flops 1048576 | bytes 1048576 | tf_op jit(solution)/shard_map/pallas_call | solution.py:337
  51.0 1.2 %shard_map.84.refs_1_ = f32[9,256,256]{2,1,0:T(8,128)} custom-call(bf16[9,32,256]{2,1,0:T(8,128)(2,1)S(1)} %collective-permute-done.11.refs_0_, bf16[9,32,256]{2,1,0:T(8,128)(2,1)S(1)} %collective-permute-done.12.refs_1_, bf16[9,32,256]{2,1,0:T(8,128)(2,1)S(1)} %collective-permute-done.9.refs_2_, ...), custom_call_target="tpu_custom_call", output_to_operand_aliasing={{}: (5, {})} | custom-call | flops 1048576 | bytes 2621440 | tf_op jit(solution)/shard_map/pallas_call | solution.py:337
  52.2 0.8 %shard_map.85 = f32[9,256,256]{2,1,0:T(8,128)} custom-call(bf16[9,32,256]{2,1,0:T(8,128)(2,1)S(1)} %collective-permute-done.10.refs_0_, f32[9,256,256]{2,1,0:T(8,128)} %shard_map.84.refs_1_), custom_call_target="tpu_custom_call", output_to_operand_aliasing={{}: (1, {})} | custom-call | flops 1048576 | bytes 524288 | tf_op jit(solution)/shard_map/pallas_call | solution.py:337
  (26 shorter events, 2.2 us)
Async XLA Ops:
  3.1 3.1 %collective-permute-start = (bf16[6,16,256]{2,1,0:T(8,128)(2,1)S(1)}, bf16[6,16,256]{2,1,0:T(8,128)(2,1)S(1)}, u32[]{:S(2)}, u32[]{:S(2)}) collective-permute-start(bf16[6,16,256]{2,1,0:T(8,128)(2,1)S(1)} %get-tuple-element.21), channel_id=1, source_target_pairs={{0,1},{1,0},{2,3},{3,2},{4,5},{5,4},{6,7},{7,6},{8,9},{9,8},{10,11... | collective-permute-start | bytes 147464 | tf_op jit(solution)/shard_map/ppermute | solution.py:412
  3.7 2.6 %collective-permute-start.1 = (bf16[6,16,256]{2,1,0:T(8,128)(2,1)S(1)}, bf16[6,16,256]{2,1,0:T(8,128)(2,1)S(1)}, u32[]{:S(2)}, u32[]{:S(2)}) collective-permute-start(bf16[6,16,256]{2,1,0:T(8,128)(2,1)S(1)} %get-tuple-element.22), channel_id=1, source_target_pairs={{1,2},{3,4},{5,6},{7,8},{9,10},{11,12},{13,14},{2,1},{4,3},{6,5},{... | collective-permute-start | bytes 147464 | tf_op jit(solution)/shard_map/ppermute | solution.py:406
  9.5 5.5 %collective-permute-start.4 = (bf16[4,9,32,256]{3,2,1,0:T(8,128)(2,1)S(1)}, bf16[4,9,32,256]{3,2,1,0:T(8,128)(2,1)S(1)}, u32[]{:S(2)}, u32[]{:S(2)}) collective-permute-start(bf16[4,9,32,256]{3,2,1,0:T(8,128)(2,1)S(1)} %shard_map.81), channel_id=1, source_target_pairs={{0,1},{1,0},{2,3},{3,2},{4,5},{5,4},{6,7},{7,6},{8,9},{9,8},{10,11... | collective-permute-start | bytes 1769480 | tf_op jit(solution)/shard_map/ppermute | solution.py:412
  14.5 32.0 %copy-start = (bf16[9,256,256]{2,1,0:T(8,128)(2,1)S(1)}, bf16[9,256,256]{2,1,0:T(8,128)(2,1)}, u32[]{:S(2)}) copy-start(bf16[9,256,256]{2,1,0:T(8,128)(2,1)} %param.6) | copy-start | bytes 3538948
  14.5 32.0 %copy-start.1 = (s32[6,8]{1,0:T(8,128)S(1)}, s32[6,8]{1,0:T(8,128)}, u32[]{:S(2)}) copy-start(s32[6,8]{1,0:T(8,128)} %codes.5) | copy-start | bytes 580
  14.6 32.0 %copy-start.2 = (s32[6]{0:T(128)S(1)}, s32[6]{0:T(128)}, u32[]{:S(2)}) copy-start(s32[6]{0:T(128)} %pos.3) | copy-start | bytes 76
  15.1 8.6 %collective-permute-start.5 = (bf16[9,32,256]{2,1,0:T(8,128)(2,1)S(1)}, bf16[9,32,256]{2,1,0:T(8,128)(2,1)S(1)}, u32[]{:S(2)}, u32[]{:S(2)}) collective-permute-start(bf16[9,32,256]{2,1,0:T(8,128)(2,1)S(1)} %get-tuple-element.31), channel_id=1, source_target_pairs={{0,6},{1,7},{2,4},{3,5},{4,2},{5,3},{6,0},{7,1},{8,14},{9,15},{10,... | collective-permute-start | bytes 442376 | tf_op jit(solution)/shard_map/ppermute | solution.py:412
  19.0 7.5 %collective-permute-start.6 = (bf16[9,32,256]{2,1,0:T(8,128)(2,1)S(1)}, bf16[9,32,256]{2,1,0:T(8,128)(2,1)S(1)}, u32[]{:S(2)}, u32[]{:S(2)}) collective-permute-start(bf16[9,32,256]{2,1,0:T(8,128)(2,1)S(1)} %get-tuple-element.32), channel_id=1, source_target_pairs={{0,2},{1,3},{2,0},{3,1},{4,6},{5,7},{6,4},{7,5},{8,10},{9,11},{10,... | collective-permute-start | bytes 442376 | tf_op jit(solution)/shard_map/ppermute | solution.py:412
  19.6 7.2 %collective-permute-start.7 = (bf16[9,32,256]{2,1,0:T(8,128)(2,1)S(1)}, bf16[9,32,256]{2,1,0:T(8,128)(2,1)S(1)}, u32[]{:S(2)}, u32[]{:S(2)}) collective-permute-start(bf16[9,32,256]{2,1,0:T(8,128)(2,1)S(1)} %get-tuple-element.33), channel_id=1, source_target_pairs={{0,4},{1,5},{2,6},{3,7},{4,0},{5,1},{6,2},{7,3},{8,12},{9,13},{10,... | collective-permute-start | bytes 442376 | tf_op jit(solution)/shard_map/ppermute | solution.py:412
  26.9 9.7 %collective-permute-start.8 = (bf16[9,32,256]{2,1,0:T(8,128)(2,1)S(1)}, bf16[9,32,256]{2,1,0:T(8,128)(2,1)S(1)}, u32[]{:S(2)}, u32[]{:S(2)}) collective-permute-start(bf16[9,32,256]{2,1,0:T(8,128)(2,1)S(1)} %add_convert_fusion.1), channel_id=1, source_target_pairs={{0,8},{1,9},{2,10},{3,11},{4,12},{5,13},{6,14},{7,15},{8,0},{9,1},... | collective-permute-start | bytes 442376 | tf_op jit(solution)/shard_map/ppermute | solution.py:412
  36.6 7.0 %collective-permute-start.12 = (bf16[9,32,256]{2,1,0:T(8,128)(2,1)S(1)}, bf16[9,32,256]{2,1,0:T(8,128)(2,1)S(1)}, u32[]{:S(2)}, u32[]{:S(2)}) collective-permute-start(bf16[9,32,256]{2,1,0:T(8,128)(2,1)S(1)} %add_convert_fusion.refs_0_), channel_id=1, source_target_pairs={{0,4},{1,5},{2,6},{3,7},{4,0},{5,1},{6,2},{7,3},{8,12},{9,13},{10,... | collective-permute-start | bytes 442376 | tf_op jit(solution)/shard_map/ppermute | solution.py:412
  37.3 7.8 %collective-permute-start.11 = (bf16[9,32,256]{2,1,0:T(8,128)(2,1)S(1)}, bf16[9,32,256]{2,1,0:T(8,128)(2,1)S(1)}, u32[]{:S(2)}, u32[]{:S(2)}) collective-permute-start(bf16[9,32,256]{2,1,0:T(8,128)(2,1)S(1)} %add_convert_fusion.refs_0_), channel_id=1, source_target_pairs={{0,2},{1,3},{2,0},{3,1},{4,6},{5,7},{6,4},{7,5},{8,10},{9,11},{10,... | collective-permute-start | bytes 442376 | tf_op jit(solution)/shard_map/ppermute | solution.py:412
  38.2 8.4 %collective-permute-start.9 = (bf16[9,32,256]{2,1,0:T(8,128)(2,1)S(1)}, bf16[9,32,256]{2,1,0:T(8,128)(2,1)S(1)}, u32[]{:S(2)}, u32[]{:S(2)}) collective-permute-start(bf16[9,32,256]{2,1,0:T(8,128)(2,1)S(1)} %add_convert_fusion.refs_0_), channel_id=1, source_target_pairs={{0,6},{1,7},{2,4},{3,5},{4,2},{5,3},{6,0},{7,1},{8,14},{9,15},{10,... | collective-permute-start | bytes 442376 | tf_op jit(solution)/shard_map/ppermute | solution.py:412
  40.2 1.2 %collective-permute-start.2 = (bf16[6,16,256]{2,1,0:T(8,128)(2,1)S(1)}, bf16[6,16,256]{2,1,0:T(8,128)(2,1)S(1)}, u32[]{:S(2)}, u32[]{:S(2)}) collective-permute-start(bf16[6,16,256]{2,1,0:T(8,128)(2,1)S(1)} %get-tuple-element.26), channel_id=1, source_target_pairs={{0,1},{1,0},{2,3},{3,2},{4,5},{5,4},{6,7},{7,6},{8,9},{9,8},{10,11... | collective-permute-start | bytes 147464 | tf_op jit(solution)/shard_map/ppermute | solution.py:412
  40.2 6.3 %collective-permute-start.3 = (bf16[6,16,256]{2,1,0:T(8,128)(2,1)S(1)}, bf16[6,16,256]{2,1,0:T(8,128)(2,1)S(1)}, u32[]{:S(2)}, u32[]{:S(2)}) collective-permute-start(bf16[6,16,256]{2,1,0:T(8,128)(2,1)S(1)} %get-tuple-element.27), channel_id=1, source_target_pairs={{1,2},{3,4},{5,6},{7,8},{9,10},{11,12},{13,14},{2,1},{4,3},{6,5},{... | collective-permute-start | bytes 147464 | tf_op jit(solution)/shard_map/ppermute | solution.py:406
  41.4 8.7 %collective-permute-start.15 = (bf16[9,32,256]{2,1,0:T(8,128)(2,1)S(1)}, bf16[9,32,256]{2,1,0:T(8,128)(2,1)S(1)}, u32[]{:S(2)}, u32[]{:S(2)}) collective-permute-start(bf16[9,32,256]{2,1,0:T(8,128)(2,1)S(1)} %add_convert_fusion.refs_0_), channel_id=1, source_target_pairs={{0,1},{1,0},{2,3},{3,2},{4,5},{5,4},{6,7},{7,6},{8,9},{9,8},{10,11... | collective-permute-start | bytes 442376 | tf_op jit(solution)/shard_map/ppermute | solution.py:412
  43.7 7.3 %collective-permute-start.14 = (bf16[9,32,256]{2,1,0:T(8,128)(2,1)S(1)}, bf16[9,32,256]{2,1,0:T(8,128)(2,1)S(1)}, u32[]{:S(2)}, u32[]{:S(2)}) collective-permute-start(bf16[9,32,256]{2,1,0:T(8,128)(2,1)S(1)} %collective-permute-done.12.refs_1_), channel_id=1, source_target_pairs={{0,1},{1,0},{2,3},{3,2},{4,5},{5,4},{6,7},{7,6},{8,9},{9,8},{10,11... | collective-permute-start | bytes 442376 | tf_op jit(solution)/shard_map/ppermute | solution.py:412
  45.2 5.9 %collective-permute-start.13 = (bf16[9,32,256]{2,1,0:T(8,128)(2,1)S(1)}, bf16[9,32,256]{2,1,0:T(8,128)(2,1)S(1)}, u32[]{:S(2)}, u32[]{:S(2)}) collective-permute-start(bf16[9,32,256]{2,1,0:T(8,128)(2,1)S(1)} %collective-permute-done.11.refs_0_), channel_id=1, source_target_pairs={{0,1},{1,0},{2,3},{3,2},{4,5},{5,4},{6,7},{7,6},{8,9},{9,8},{10,11... | collective-permute-start | bytes 442376 | tf_op jit(solution)/shard_map/ppermute | solution.py:412
  46.5 5.7 %collective-permute-start.10 = (bf16[9,32,256]{2,1,0:T(8,128)(2,1)S(1)}, bf16[9,32,256]{2,1,0:T(8,128)(2,1)S(1)}, u32[]{:S(2)}, u32[]{:S(2)}) collective-permute-start(bf16[9,32,256]{2,1,0:T(8,128)(2,1)S(1)} %collective-permute-done.9.refs_2_), channel_id=1, source_target_pairs={{0,1},{1,0},{2,3},{3,2},{4,5},{5,4},{6,7},{7,6},{8,9},{9,8},{10,11... | collective-permute-start | bytes 442376 | tf_op jit(solution)/shard_map/ppermute | solution.py:412

commit v2 on v1

--- a/solution.py
+++ b/solution.py
@@ -155,25 +155,50 @@
     )(far(codes), far(maps), far(weights), far(grads))
 
 
-def product_kernel(inner, weights, partial):
-    for tile in range(inner.shape[0]):
-        partial[tile] = inner_product(inner, weights, tile)
-
-
-def product(inner, weights):
+def finished(value, outer, pos):
+    gate = jnp.where(pos >= 0, 1.0, 0.0)
+    cumulative = 0.5 * (1.0 + lax.erf(value * ROOT_HALF))
+    density = jnp.exp(-0.5 * value * value) * INV_ROOT_TAU
+    slope = cumulative + value * density
+    made = outer.astype(F32) * slope * gate
+    return (value * cumulative * gate).astype(BF16), made.astype(BF16)
+
+
+def product_kernel(early, pos, inner, weights, grads, partial, act, grad, pos_held, sem):
+    slots, side = inner.shape[:2]
+    arrival = pltpu.make_async_copy(pos, pos_held, sem)
+    arrival.start()
+    rows = slice(1, side - 1)
+    partial[0] = inner_product(inner, weights, 0)
+    arrival.wait()
+    for tile in range(slots):
+        if tile + 1 < slots:
+            partial[tile + 1] = inner_product(inner, weights, tile + 1)
+        if tile < early:
+            act[tile, rows], grad[tile, rows] = finished(
+                partial[tile, rows], grads[tile, rows], pos_held[tile]
+            )
+
+
+def product(early, pos, inner, weights, grads):
     slots, side, _, wide = inner.shape
     return call(
-        product_kernel,
+        functools.partial(product_kernel, early),
         2 * slots * side * side * wide * wide,
         6 << 20,
-        in_specs=[VMEM, VMEM],
-        out_specs=VMEM,
-        out_shape=held((slots, side, side, wide // 3), F32),
-    )(inner, weights)
+        in_specs=[ANY] + [VMEM] * 3,
+        out_specs=[VMEM] * 3,
+        out_shape=[
+            held((slots, side, side, wide // 3), F32),
+            held(grads.shape, BF16),
+            held(grads.shape, BF16),
+        ],
+        scratch_shapes=[pltpu.SMEM(pos.shape, jnp.int32), pltpu.SemaphoreType.DMA],
+    )(far(pos), inner, weights, grads)
 
 
 def forward_kernel(
-    codes, pos, partial, inner, cross, link, weights, grads,
+    early, codes, pos, partial, inner, cross, link, weights, grads, act_in, grad_in,
     act, grad, edge, to_core, to_link, codes_held, pos_held, sems,
 ):
     slots, side, _, channels = partial.shape
@@ -184,22 +209,11 @@
     ]
     for item in loads:
         item.start()
-
-    def finish(value, outer, gate):
-        cumulative = 0.5 * (1.0 + lax.erf(value * ROOT_HALF))
-        density = jnp.exp(-0.5 * value * value) * INV_ROOT_TAU
-        slope = cumulative + value * density
-        return (
-            (value * cumulative * gate).astype(BF16),
-            (outer.astype(F32) * slope * gate).astype(BF16),
-        )
-
     loads[1].wait()
-    gates = [jnp.where(pos_held[tile] >= 0, 1.0, 0.0) for tile in range(slots)]
     rows = slice(1, side - 1)
-    for tile in range(slots):
-        act[tile, rows], grad[tile, rows] = finish(
-            partial[tile, rows], grads[tile, rows], gates[tile]
+    for tile in range(early, slots):
+        act[tile, rows], grad[tile, rows] = finished(
+            partial[tile, rows], grads[tile, rows], pos_held[tile]
         )
     loads[0].wait()
     center = slice(channels, 2 * channels)
@@ -208,30 +222,34 @@
             edge, lambda slot, row: inner[slot, row, :, center].astype(F32),
             side, slots, cross, link, codes_held, tile,
         )
+    ends = []
     for end, row, part in ((0, 0, 0), (1, side - 1, 2)):
         added = jnp.dot(
             edge[:, end].reshape(slots * side, wide),
             weights[part * wide : (part + 1) * wide],
             preferred_element_type=F32,
         ).reshape(slots, side, channels)
+        made = []
         for tile in range(slots):
-            value, outer = finish(
-                partial[tile, row] + added[tile], grads[tile, row], gates[tile]
+            value, outer = finished(
+                partial[tile, row] + added[tile], grads[tile, row], pos_held[tile]
             )
             act[tile, row] = value
             grad[tile, row] = outer
+            made.append(outer)
+        ends.append(made)
     for tile in range(slots):
-        put_sends(to_core, to_link, tile, grad[tile, 0], grad[tile, side - 1])
-
-
-def forward(codes, pos, partial, inner, cross, link, weights, grads):
+        put_sends(to_core, to_link, tile, ends[0][tile], ends[1][tile])
+
+
+def forward(early, codes, pos, partial, inner, cross, link, weights, grads, act, grad):
     slots, side, _, channels = partial.shape
     wide = 3 * channels
     return call(
-        forward_kernel,
+        functools.partial(forward_kernel, early),
         4 * slots * side * wide * channels,
         8 << 20,
-        in_specs=[ANY, ANY] + [VMEM] * 6,
+        in_specs=[ANY, ANY] + [VMEM] * 8,
         out_specs=[VMEM] * 5,
         out_shape=[
             held(partial.shape, BF16),
@@ -240,12 +258,13 @@
             held(cross.shape, BF16),
             held(cross.shape, BF16),
         ],
+        input_output_aliases={8: 0, 9: 1},
         scratch_shapes=[
             pltpu.SMEM(codes.shape, jnp.int32),
             pltpu.SMEM(pos.shape, jnp.int32),
             pltpu.SemaphoreType.DMA((2,)),
         ],
-    )(far(codes), far(pos), partial, inner, cross, link, weights, grads)
+    )(far(codes), far(pos), partial, inner, cross, link, weights, grads, act, grad)
 
 
 def kernel_grad_kernel(other, inner, edge, grad, out):
@@ -412,6 +431,13 @@
     return lax.ppermute(value, "tile", [(source, source ^ bit) for source in range(count)])
 
 
+def quad_swaps(values):
+    got = []
+    for k, value in enumerate(values):
+        got.append(swap(value, 2 * (k + 1)))
+    return got
+
+
 def sum_high(total, high):
     shape = total.shape
     index = lax.axis_index("tile")
@@ -436,22 +462,23 @@
     slots, side, _, channels = features.shape
     devices = lax.axis_size("tile")
     flat = weights.reshape(9 * channels, channels)
+    early = slots
     inner, flat, grads, to_core, to_link = load(neighbours, features, flat, grad_out)
     cross, link = edge_swaps(to_core, to_link)
-    partial = product(inner, flat)
+    partial, activation, grad = product(early, tile_pos, inner, flat, grads)
     activation, grad, edge, to_core, to_link = forward(
-        neighbours, tile_pos, partial, inner, cross, link, flat, grads
+        early, neighbours, tile_pos, partial, inner, cross, link, flat, grads, activation, grad
     )
     send = kernel_grad(True, inner, edge, grad, BF16)
     recv = swap(send, 1)
     keep = kernel_grad(False, inner, edge, grad, F32)
     own, *sends = spread(keep, recv)
-    got = [swap(sends[k], 2 * (k + 1)) for k in (2, 0, 1)]
+    got = quad_swaps(sends)
     total = own + got[0].astype(F32) + got[1].astype(F32) + got[2].astype(F32)
     piece = sum_high(total, [8 << k for k in range(devices.bit_length() - 4)])
     scale = 1.0 / math.sqrt(slots * devices * side * side)
     whole = weights.shape
-    pieces = [piece] + [swap(piece, 2 * k) for k in (1, 2, 3)]
+    pieces = [piece] + quad_swaps([piece] * 3)
     its = [swap(piece, 1)]
     its += [swap(item, 1) for item in pieces[1:3]]
     its.append(swap(pieces[3], 1))

time: 53.2 us -> 51.3 us (0.964)
  waiting for transfers between devices: 17.9 us -> 15.9 us
    ppermute x14, waiting for transfers between devices: 17.9 us -> 15.9 us  [swap(): lax.ppermute(value, 'tile', [(source, source ^ bit) for source in range(c...]
  transfers between devices with their start and end apart: 16 -> 16, of which waited for: 8 -> 7; matrix products, arithmetic and copies ran while one was open for 0% -> 0% of each run, Pallas kernels for 16% -> 19%
where the time goes in v2:
time: 51.3 us; the launch traced here: 50.8 us
  starting transfers between devices  18.4 us (36%)
  waiting for transfers between devices  15.9 us (31%)
  Pallas kernels  15.5 us (30%)
  between operations  0.82 us (2%)
    ppermute x14, starting transfers between devices, swap(): lax.ppermute(value, 'tile', [(source, source ^ bit) for source in range(c...  17.1 us
    ppermute x14, waiting for transfers between devices, swap(): lax.ppermute(value, 'tile', [(source, source ^ bit) for source in range(c...  15.9 us
    pallas_call x1, Pallas kernels, backward(): call(backward_kernel, 18 * slots * side * side * channels * channels, 4 <...  3.54 us
    pallas_call x1, Pallas kernels, product(): call(functools.partial(product_kernel, early), 2 * slots * side * side *...  2.95 us
    pallas_call x3, Pallas kernels, collect(): call(functools.partial(collect_kernel, scale, plan), 1 << 20, count << 19...  2.79 us
    pallas_call x1, Pallas kernels, load(): call(load_kernel, 1 << 20, 6 << 20, in_specs=[SMEM, ANY, ANY, ANY], out_s...  2.48 us
    pallas_call x2, Pallas kernels, kernel_grad(): call(functools.partial(kernel_grad_kernel, other), 9 * slots * side * sid...  2.38 us
    ppermute x2, starting transfers between devices, edge_swaps(): link = lax.ppermute(to_link, 'tile', ends + [(t, s) for s, t in ends])  1.3 us
  transfers between devices with their start and end apart: 16, of which 7 were waited for; matrix products, arithmetic and copies ran while one was open for 0% of the time, Pallas kernels for 19%

profile of v2, /device:TPU:0, one launch (start us, length us, event | category | flops | bytes accessed | tf_op | source)
XLA Modules:
  0.0 50.8 jit_solution(4402070757902209863)
XLA Ops:
  0.6 2.5 %shard_map.76 = (bf16[6,16,16,768]{3,2,1,0:T(8,128)(2,1)S(1)}, bf16[2304,256]{1,0:T(8,128)(2,1)S(1)}, bf16[6,16,16,256]{3,2,1,0:T(8,128)(2,1)S(1)}, bf16[6,16,25...) custom-call(s32[6,8]{1,0:T(8,128)} %codes.5, bf16[6,16,16,256]{3,2,1,0:T(8,128)(2,1)} %maps.1, bf16[2304,256]{1,0:T(8,128)(2,1)} %bitcast.1, ...), custom_call_target="tpu_custom_call" | custom-call | flops 1048576 | bytes 6291456 | tf_op jit(solution)/shard_map/pallas_call | solution.py:141
  3.7 0.7 %collective-permute-start.1 = (bf16[6,16,256]{2,1,0:T(8,128)(2,1)S(1)}, bf16[6,16,256]{2,1,0:T(8,128)(2,1)S(1)}, u32[]{:S(2)}, u32[]{:S(2)}) collective-permute-start(bf16[6,16,256]{2,1,0:T(8,128)(2,1)S(1)} %get-tuple-element.27), channel_id=1, source_target_pairs={{1,2},{3,4},{5,6},{7,8},{9,10},{11,12},{13,14},{2,1},{4,3},{6,5},{... | collective-permute-start | bytes 147464 | tf_op jit(solution)/shard_map/ppermute | solution.py:425
  4.3 3.0 %shard_map.77 = (f32[6,16,16,256]{3,2,1,0:T(8,128)S(1)}, bf16[6,16,16,256]{3,2,1,0:T(8,128)(2,1)S(1)}, bf16[6,16,16,256]{3,2,1,0:T(8,128)(2,1)S(1)}) custom-call(s32[6]{0:T(128)} %pos.5, bf16[6,16,16,768]{3,2,1,0:T(8,128)(2,1)S(1)} %get-tuple-element.22.inner, bf16[2304,256]{1,0:T(8,128)(2,1)S(1)} %get-tuple-element.23.weights, ...), custom_call_target="tpu_custom_call" | custom-call | flops 1811939328 | bytes 6291456 | tf_op jit(solution)/shard_map/pallas_call | solution.py:185
  7.3 1.2 %shard_map.78 = (bf16[6,16,16,256]{3,2,1,0:T(8,128)(2,1)S(1)}, bf16[6,16,16,256]{3,2,1,0:T(8,128)(2,1)S(1)}, bf16[6,2,16,768]{3,2,1,0:T(8,128)(2,1)S(1)}, bf16[6...) custom-call(s32[6,8]{1,0:T(8,128)} %codes.5, s32[6]{0:T(128)} %pos.5, ...), custom_call_target="tpu_custom_call", output_to_operand_aliasing={{0}: (8, {}), {1}: (9, {})} | custom-call | flops 75497472 | bytes 8388608 | tf_op jit(solution)/shard_map/pallas_call | solution.py:248
  8.5 1.2 %shard_map.81 = bf16[4,9,32,256]{3,2,1,0:T(8,128)(2,1)S(1)} custom-call(bf16[6,16,16,768]{3,2,1,0:T(8,128)(2,1)S(1)} %get-tuple-element.22.inner, bf16[6,2,16,768]{3,2,1,0:T(8,128)(2,1)S(1)} %get-tuple-element.35.edge, bf16[6,16,16,256]{3,2,1,0:T(8,128)(2,1)S(1)} %get-tuple-element.31.grad), custom_call_target="tpu_custom_call" | custom-call | flops 905969664 | bytes 6291456 | tf_op jit(solution)/shard_map/pallas_call | solution.py:297
  9.8 3.9 %collective-permute-start.4 = (bf16[4,9,32,256]{3,2,1,0:T(8,128)(2,1)S(1)}, bf16[4,9,32,256]{3,2,1,0:T(8,128)(2,1)S(1)}, u32[]{:S(2)}, u32[]{:S(2)}) collective-permute-start(bf16[4,9,32,256]{3,2,1,0:T(8,128)(2,1)S(1)} %shard_map.81), channel_id=1, source_target_pairs={{0,1},{1,0},{2,3},{3,2},{4,5},{5,4},{6,7},{7,6},{8,9},{9,8},{10,11... | collective-permute-start | bytes 1769480 | tf_op jit(solution)/shard_map/ppermute | solution.py:431
  13.6 1.2 %shard_map.80.keep = f32[4,9,32,256]{3,2,1,0:T(8,128)S(1)} custom-call(bf16[6,16,16,768]{3,2,1,0:T(8,128)(2,1)S(1)} %get-tuple-element.22.inner, bf16[6,2,16,768]{3,2,1,0:T(8,128)(2,1)S(1)} %get-tuple-element.35.edge, bf16[6,16,16,256]{3,2,1,0:T(8,128)(2,1)S(1)} %get-tuple-element.31.grad), custom_call_target="tpu_custom_call" | custom-call | flops 905969664 | bytes 6291456 | tf_op jit(solution)/shard_map/pallas_call | solution.py:297
  15.4 1.8 %collective-permute-start.5 = (bf16[9,32,256]{2,1,0:T(8,128)(2,1)S(1)}, bf16[9,32,256]{2,1,0:T(8,128)(2,1)S(1)}, u32[]{:S(2)}, u32[]{:S(2)}) collective-permute-start(bf16[9,32,256]{2,1,0:T(8,128)(2,1)S(1)} %get-tuple-element.37), channel_id=1, source_target_pairs={{0,2},{1,3},{2,0},{3,1},{4,6},{5,7},{6,4},{7,5},{8,10},{9,11},{10,... | collective-permute-start | bytes 442376 | tf_op jit(solution)/shard_map/ppermute | solution.py:431
  17.2 1.6 %collective-permute-start.6 = (bf16[9,32,256]{2,1,0:T(8,128)(2,1)S(1)}, bf16[9,32,256]{2,1,0:T(8,128)(2,1)S(1)}, u32[]{:S(2)}, u32[]{:S(2)}) collective-permute-start(bf16[9,32,256]{2,1,0:T(8,128)(2,1)S(1)} %get-tuple-element.38), channel_id=1, source_target_pairs={{0,4},{1,5},{2,6},{3,7},{4,0},{5,1},{6,2},{7,3},{8,12},{9,13},{10,... | collective-permute-start | bytes 442376 | tf_op jit(solution)/shard_map/ppermute | solution.py:431
  18.9 2.7 %collective-permute-done.5 = bf16[9,32,256]{2,1,0:T(8,128)(2,1)S(1)} collective-permute-done((bf16[9,32,256]{2,1,0:T(8,128)(2,1)S(1)}, bf16[9,32,256]{2,1,0:T(8,128)(2,1)S(1)}, u32[]{:S(2)}, u32[]{:S(2)}) %collective-permute-start.5) | collective-permute-done | bytes 147488 | tf_op jit(solution)/shard_map/ppermute | solution.py:431
  21.6 2.3 %collective-permute-done.6 = bf16[9,32,256]{2,1,0:T(8,128)(2,1)S(1)} collective-permute-done((bf16[9,32,256]{2,1,0:T(8,128)(2,1)S(1)}, bf16[9,32,256]{2,1,0:T(8,128)(2,1)S(1)}, u32[]{:S(2)}, u32[]{:S(2)}) %collective-permute-start.6) | collective-permute-done | bytes 147488 | tf_op jit(solution)/shard_map/ppermute | solution.py:431
  24.0 2.1 %collective-permute-done.7 = bf16[9,32,256]{2,1,0:T(8,128)(2,1)S(1)} collective-permute-done((bf16[9,32,256]{2,1,0:T(8,128)(2,1)S(1)}, bf16[9,32,256]{2,1,0:T(8,128)(2,1)S(1)}, u32[]{:S(2)}, u32[]{:S(2)}) %collective-permute-start.7) | collective-permute-done | bytes 147488 | tf_op jit(solution)/shard_map/ppermute | solution.py:431
  26.1 2.7 %collective-permute-start.8 = (bf16[9,32,256]{2,1,0:T(8,128)(2,1)S(1)}, bf16[9,32,256]{2,1,0:T(8,128)(2,1)S(1)}, u32[]{:S(2)}, u32[]{:S(2)}) collective-permute-start(bf16[9,32,256]{2,1,0:T(8,128)(2,1)S(1)} %add_convert_fusion.1), channel_id=1, source_target_pairs={{0,8},{1,9},{2,10},{3,11},{4,12},{5,13},{6,14},{7,15},{8,0},{9,1},... | collective-permute-start | bytes 442376 | tf_op jit(solution)/shard_map/ppermute | solution.py:431
  28.8 6.6 %collective-permute-done.8 = bf16[9,32,256]{2,1,0:T(8,128)(2,1)S(1)} collective-permute-done((bf16[9,32,256]{2,1,0:T(8,128)(2,1)S(1)}, bf16[9,32,256]{2,1,0:T(8,128)(2,1)S(1)}, u32[]{:S(2)}, u32[]{:S(2)}) %collective-permute-start.8) | collective-permute-done | bytes 147488 | tf_op jit(solution)/shard_map/ppermute | solution.py:431
  35.8 1.3 %collective-permute-start.11 = (bf16[9,32,256]{2,1,0:T(8,128)(2,1)S(1)}, bf16[9,32,256]{2,1,0:T(8,128)(2,1)S(1)}, u32[]{:S(2)}, u32[]{:S(2)}) collective-permute-start(bf16[9,32,256]{2,1,0:T(8,128)(2,1)S(1)} %add_convert_fusion.refs_0_), channel_id=1, source_target_pairs={{0,2},{1,3},{2,0},{3,1},{4,6},{5,7},{6,4},{7,5},{8,10},{9,11},{10,... | collective-permute-start | bytes 442376 | tf_op jit(solution)/shard_map/ppermute | solution.py:431
  37.1 1.9 %collective-permute-start.9 = (bf16[9,32,256]{2,1,0:T(8,128)(2,1)S(1)}, bf16[9,32,256]{2,1,0:T(8,128)(2,1)S(1)}, u32[]{:S(2)}, u32[]{:S(2)}) collective-permute-start(bf16[9,32,256]{2,1,0:T(8,128)(2,1)S(1)} %add_convert_fusion.refs_0_), channel_id=1, source_target_pairs={{0,6},{1,7},{2,4},{3,5},{4,2},{5,3},{6,0},{7,1},{8,14},{9,15},{10,... | collective-permute-start | bytes 442376 | tf_op jit(solution)/shard_map/ppermute | solution.py:431
  38.9 0.7 %collective-permute-start.3 = (bf16[6,16,256]{2,1,0:T(8,128)(2,1)S(1)}, bf16[6,16,256]{2,1,0:T(8,128)(2,1)S(1)}, u32[]{:S(2)}, u32[]{:S(2)}) collective-permute-start(bf16[6,16,256]{2,1,0:T(8,128)(2,1)S(1)} %get-tuple-element.33), channel_id=1, source_target_pairs={{1,2},{3,4},{5,6},{7,8},{9,10},{11,12},{13,14},{2,1},{4,3},{6,5},{... | collective-permute-start | bytes 147464 | tf_op jit(solution)/shard_map/ppermute | solution.py:425
  39.6 0.6 %collective-permute-done.2.cross = bf16[6,16,256]{2,1,0:T(8,128)(2,1)S(1)} collective-permute-done((bf16[6,16,256]{2,1,0:T(8,128)(2,1)S(1)}, bf16[6,16,256]{2,1,0:T(8,128)(2,1)S(1)}, u32[]{:S(2)}, u32[]{:S(2)}) %collective-permute-start.2) | collective-permute-done | bytes 49184 | tf_op jit(solution)/shard_map/ppermute | solution.py:431
  40.2 2.4 %collective-permute-start.15 = (bf16[9,32,256]{2,1,0:T(8,128)(2,1)S(1)}, bf16[9,32,256]{2,1,0:T(8,128)(2,1)S(1)}, u32[]{:S(2)}, u32[]{:S(2)}) collective-permute-start(bf16[9,32,256]{2,1,0:T(8,128)(2,1)S(1)} %add_convert_fusion.refs_0_), channel_id=1, source_target_pairs={{0,1},{1,0},{2,3},{3,2},{4,5},{5,4},{6,7},{7,6},{8,9},{9,8},{10,11... | collective-permute-start | bytes 442376 | tf_op jit(solution)/shard_map/ppermute | solution.py:431
  43.1 1.2 %collective-permute-done.9.refs_2_ = bf16[9,32,256]{2,1,0:T(8,128)(2,1)S(1)} collective-permute-done((bf16[9,32,256]{2,1,0:T(8,128)(2,1)S(1)}, bf16[9,32,256]{2,1,0:T(8,128)(2,1)S(1)}, u32[]{:S(2)}, u32[]{:S(2)}) %collective-permute-start.9) | collective-permute-done | bytes 147488 | tf_op jit(solution)/shard_map/ppermute | solution.py:431
  44.4 3.5 %shard_map.79 = (bf16[6,16,16,256]{3,2,1,0:T(8,128)(2,1)}, bf16[6,16,16,256]{3,2,1,0:T(8,128)(2,1)}) custom-call(s32[6,8]{1,0:T(8,128)S(1)} %copy-done.1, s32[6]{0:T(128)S(1)} %copy-done.2, bf16[6,16,16,256]{3,2,1,0:T(8,128)(2,1)S(1)} %get-tuple-element.30.act, bf16[6,16,16,256]{3,2,1,0:T(8,128)(2,1)S(1)} %get-tuple-element.31.grad, ...), custom_call_target="tpu_custom_call" | custom-call | flops 1811939328 | bytes 4194304 | tf_op jit(solution)/shard_map/pallas_call | solution.py:406
  48.0 0.9 %shard_map.83.refs_5_ = f32[9,256,256]{2,1,0:T(8,128)} custom-call(bf16[9,32,256]{2,1,0:T(8,128)(2,1)S(1)} %add_convert_fusion.refs_0_, bf16[9,32,256]{2,1,0:T(8,128)(2,1)S(1)} %collective-permute-done.15.refs_1_), custom_call_target="tpu_custom_call" | custom-call | flops 1048576 | bytes 1048576 | tf_op jit(solution)/shard_map/pallas_call | solution.py:356
  48.8 1.2 %shard_map.84.refs_1_ = f32[9,256,256]{2,1,0:T(8,128)} custom-call(bf16[9,32,256]{2,1,0:T(8,128)(2,1)S(1)} %collective-permute-done.11.refs_0_, bf16[9,32,256]{2,1,0:T(8,128)(2,1)S(1)} %collective-permute-done.12.refs_1_, bf16[9,32,256]{2,1,0:T(8,128)(2,1)S(1)} %collective-permute-done.9.refs_2_, ...), custom_call_target="tpu_custom_call", output_to_operand_aliasing={{}: (5, {})} | custom-call | flops 1048576 | bytes 2621440 | tf_op jit(solution)/shard_map/pallas_call | solution.py:356
  50.0 0.8 %shard_map.85 = f32[9,256,256]{2,1,0:T(8,128)} custom-call(bf16[9,32,256]{2,1,0:T(8,128)(2,1)S(1)} %collective-permute-done.10.refs_0_, f32[9,256,256]{2,1,0:T(8,128)} %shard_map.84.refs_1_), custom_call_target="tpu_custom_call", output_to_operand_aliasing={{}: (1, {})} | custom-call | flops 1048576 | bytes 524288 | tf_op jit(solution)/shard_map/pallas_call | solution.py:356
  (26 shorter events, 2.3 us)
Async XLA Ops:
  3.1 4.2 %collective-permute-start = (bf16[6,16,256]{2,1,0:T(8,128)(2,1)S(1)}, bf16[6,16,256]{2,1,0:T(8,128)(2,1)S(1)}, u32[]{:S(2)}, u32[]{:S(2)}) collective-permute-start(bf16[6,16,256]{2,1,0:T(8,128)(2,1)S(1)} %get-tuple-element.26), channel_id=1, source_target_pairs={{0,1},{1,0},{2,3},{3,2},{4,5},{5,4},{6,7},{7,6},{8,9},{9,8},{10,11... | collective-permute-start | bytes 147464 | tf_op jit(solution)/shard_map/ppermute | solution.py:431
  3.7 3.6 %collective-permute-start.1 = (bf16[6,16,256]{2,1,0:T(8,128)(2,1)S(1)}, bf16[6,16,256]{2,1,0:T(8,128)(2,1)S(1)}, u32[]{:S(2)}, u32[]{:S(2)}) collective-permute-start(bf16[6,16,256]{2,1,0:T(8,128)(2,1)S(1)} %get-tuple-element.27), channel_id=1, source_target_pairs={{1,2},{3,4},{5,6},{7,8},{9,10},{11,12},{13,14},{2,1},{4,3},{6,5},{... | collective-permute-start | bytes 147464 | tf_op jit(solution)/shard_map/ppermute | solution.py:425
  9.8 5.5 %collective-permute-start.4 = (bf16[4,9,32,256]{3,2,1,0:T(8,128)(2,1)S(1)}, bf16[4,9,32,256]{3,2,1,0:T(8,128)(2,1)S(1)}, u32[]{:S(2)}, u32[]{:S(2)}) collective-permute-start(bf16[4,9,32,256]{3,2,1,0:T(8,128)(2,1)S(1)} %shard_map.81), channel_id=1, source_target_pairs={{0,1},{1,0},{2,3},{3,2},{4,5},{5,4},{6,7},{7,6},{8,9},{9,8},{10,11... | collective-permute-start | bytes 1769480 | tf_op jit(solution)/shard_map/ppermute | solution.py:431
  14.8 29.6 %copy-start = (bf16[9,256,256]{2,1,0:T(8,128)(2,1)S(1)}, bf16[9,256,256]{2,1,0:T(8,128)(2,1)}, u32[]{:S(2)}) copy-start(bf16[9,256,256]{2,1,0:T(8,128)(2,1)} %param.6) | copy-start | bytes 3538948
  14.8 29.6 %copy-start.1 = (s32[6,8]{1,0:T(8,128)S(1)}, s32[6,8]{1,0:T(8,128)}, u32[]{:S(2)}) copy-start(s32[6,8]{1,0:T(8,128)} %codes.5) | copy-start | bytes 580
  14.8 29.6 %copy-start.2 = (s32[6]{0:T(128)S(1)}, s32[6]{0:T(128)}, u32[]{:S(2)}) copy-start(s32[6]{0:T(128)} %pos.5) | copy-start | bytes 76
  15.4 6.2 %collective-permute-start.5 = (bf16[9,32,256]{2,1,0:T(8,128)(2,1)S(1)}, bf16[9,32,256]{2,1,0:T(8,128)(2,1)S(1)}, u32[]{:S(2)}, u32[]{:S(2)}) collective-permute-start(bf16[9,32,256]{2,1,0:T(8,128)(2,1)S(1)} %get-tuple-element.37), channel_id=1, source_target_pairs={{0,2},{1,3},{2,0},{3,1},{4,6},{5,7},{6,4},{7,5},{8,10},{9,11},{10,... | collective-permute-start | bytes 442376 | tf_op jit(solution)/shard_map/ppermute | solution.py:431
  17.2 6.7 %collective-permute-start.6 = (bf16[9,32,256]{2,1,0:T(8,128)(2,1)S(1)}, bf16[9,32,256]{2,1,0:T(8,128)(2,1)S(1)}, u32[]{:S(2)}, u32[]{:S(2)}) collective-permute-start(bf16[9,32,256]{2,1,0:T(8,128)(2,1)S(1)} %get-tuple-element.38), channel_id=1, source_target_pairs={{0,4},{1,5},{2,6},{3,7},{4,0},{5,1},{6,2},{7,3},{8,12},{9,13},{10,... | collective-permute-start | bytes 442376 | tf_op jit(solution)/shard_map/ppermute | solution.py:431
  18.8 7.2 %collective-permute-start.7 = (bf16[9,32,256]{2,1,0:T(8,128)(2,1)S(1)}, bf16[9,32,256]{2,1,0:T(8,128)(2,1)S(1)}, u32[]{:S(2)}, u32[]{:S(2)}) collective-permute-start(bf16[9,32,256]{2,1,0:T(8,128)(2,1)S(1)} %get-tuple-element.39), channel_id=1, source_target_pairs={{0,6},{1,7},{2,4},{3,5},{4,2},{5,3},{6,0},{7,1},{8,14},{9,15},{10,... | collective-permute-start | bytes 442376 | tf_op jit(solution)/shard_map/ppermute | solution.py:431
  26.1 9.2 %collective-permute-start.8 = (bf16[9,32,256]{2,1,0:T(8,128)(2,1)S(1)}, bf16[9,32,256]{2,1,0:T(8,128)(2,1)S(1)}, u32[]{:S(2)}, u32[]{:S(2)}) collective-permute-start(bf16[9,32,256]{2,1,0:T(8,128)(2,1)S(1)} %add_convert_fusion.1), channel_id=1, source_target_pairs={{0,8},{1,9},{2,10},{3,11},{4,12},{5,13},{6,14},{7,15},{8,0},{9,1},... | collective-permute-start | bytes 442376 | tf_op jit(solution)/shard_map/ppermute | solution.py:431
  35.4 7.2 %collective-permute-start.12 = (bf16[9,32,256]{2,1,0:T(8,128)(2,1)S(1)}, bf16[9,32,256]{2,1,0:T(8,128)(2,1)S(1)}, u32[]{:S(2)}, u32[]{:S(2)}) collective-permute-start(bf16[9,32,256]{2,1,0:T(8,128)(2,1)S(1)} %add_convert_fusion.refs_0_), channel_id=1, source_target_pairs={{0,4},{1,5},{2,6},{3,7},{4,0},{5,1},{6,2},{7,3},{8,12},{9,13},{10,... | collective-permute-start | bytes 442376 | tf_op jit(solution)/shard_map/ppermute | solution.py:431
  35.8 6.9 %collective-permute-start.11 = (bf16[9,32,256]{2,1,0:T(8,128)(2,1)S(1)}, bf16[9,32,256]{2,1,0:T(8,128)(2,1)S(1)}, u32[]{:S(2)}, u32[]{:S(2)}) collective-permute-start(bf16[9,32,256]{2,1,0:T(8,128)(2,1)S(1)} %add_convert_fusion.refs_0_), channel_id=1, source_target_pairs={{0,2},{1,3},{2,0},{3,1},{4,6},{5,7},{6,4},{7,5},{8,10},{9,11},{10,... | collective-permute-start | bytes 442376 | tf_op jit(solution)/shard_map/ppermute | solution.py:431
  37.1 7.3 %collective-permute-start.9 = (bf16[9,32,256]{2,1,0:T(8,128)(2,1)S(1)}, bf16[9,32,256]{2,1,0:T(8,128)(2,1)S(1)}, u32[]{:S(2)}, u32[]{:S(2)}) collective-permute-start(bf16[9,32,256]{2,1,0:T(8,128)(2,1)S(1)} %add_convert_fusion.refs_0_), channel_id=1, source_target_pairs={{0,6},{1,7},{2,4},{3,5},{4,2},{5,3},{6,0},{7,1},{8,14},{9,15},{10,... | collective-permute-start | bytes 442376 | tf_op jit(solution)/shard_map/ppermute | solution.py:431
  38.9 1.2 %collective-permute-start.2 = (bf16[6,16,256]{2,1,0:T(8,128)(2,1)S(1)}, bf16[6,16,256]{2,1,0:T(8,128)(2,1)S(1)}, u32[]{:S(2)}, u32[]{:S(2)}) collective-permute-start(bf16[6,16,256]{2,1,0:T(8,128)(2,1)S(1)} %get-tuple-element.32), channel_id=1, source_target_pairs={{0,1},{1,0},{2,3},{3,2},{4,5},{5,4},{6,7},{7,6},{8,9},{9,8},{10,11... | collective-permute-start | bytes 147464 | tf_op jit(solution)/shard_map/ppermute | solution.py:431
  38.9 5.4 %collective-permute-start.3 = (bf16[6,16,256]{2,1,0:T(8,128)(2,1)S(1)}, bf16[6,16,256]{2,1,0:T(8,128)(2,1)S(1)}, u32[]{:S(2)}, u32[]{:S(2)}) collective-permute-start(bf16[6,16,256]{2,1,0:T(8,128)(2,1)S(1)} %get-tuple-element.33), channel_id=1, source_target_pairs={{1,2},{3,4},{5,6},{7,8},{9,10},{11,12},{13,14},{2,1},{4,3},{6,5},{... | collective-permute-start | bytes 147464 | tf_op jit(solution)/shard_map/ppermute | solution.py:425
  40.2 7.8 %collective-permute-start.15 = (bf16[9,32,256]{2,1,0:T(8,128)(2,1)S(1)}, bf16[9,32,256]{2,1,0:T(8,128)(2,1)S(1)}, u32[]{:S(2)}, u32[]{:S(2)}) collective-permute-start(bf16[9,32,256]{2,1,0:T(8,128)(2,1)S(1)} %add_convert_fusion.refs_0_), channel_id=1, source_target_pairs={{0,1},{1,0},{2,3},{3,2},{4,5},{5,4},{6,7},{7,6},{8,9},{9,8},{10,11... | collective-permute-start | bytes 442376 | tf_op jit(solution)/shard_map/ppermute | solution.py:431
  42.6 6.2 %collective-permute-start.14 = (bf16[9,32,256]{2,1,0:T(8,128)(2,1)S(1)}, bf16[9,32,256]{2,1,0:T(8,128)(2,1)S(1)}, u32[]{:S(2)}, u32[]{:S(2)}) collective-permute-start(bf16[9,32,256]{2,1,0:T(8,128)(2,1)S(1)} %collective-permute-done.12.refs_1_), channel_id=1, source_target_pairs={{0,1},{1,0},{2,3},{3,2},{4,5},{5,4},{6,7},{7,6},{8,9},{9,8},{10,11... | collective-permute-start | bytes 442376 | tf_op jit(solution)/shard_map/ppermute | solution.py:431
  42.7 6.1 %collective-permute-start.13 = (bf16[9,32,256]{2,1,0:T(8,128)(2,1)S(1)}, bf16[9,32,256]{2,1,0:T(8,128)(2,1)S(1)}, u32[]{:S(2)}, u32[]{:S(2)}) collective-permute-start(bf16[9,32,256]{2,1,0:T(8,128)(2,1)S(1)} %collective-permute-done.11.refs_0_), channel_id=1, source_target_pairs={{0,1},{1,0},{2,3},{3,2},{4,5},{5,4},{6,7},{7,6},{8,9},{9,8},{10,11... | collective-permute-start | bytes 442376 | tf_op jit(solution)/shard_map/ppermute | solution.py:431
  44.4 5.7 %collective-permute-start.10 = (bf16[9,32,256]{2,1,0:T(8,128)(2,1)S(1)}, bf16[9,32,256]{2,1,0:T(8,128)(2,1)S(1)}, u32[]{:S(2)}, u32[]{:S(2)}) collective-permute-start(bf16[9,32,256]{2,1,0:T(8,128)(2,1)S(1)} %collective-permute-done.9.refs_2_), channel_id=1, source_target_pairs={{0,1},{1,0},{2,3},{3,2},{4,5},{5,4},{6,7},{7,6},{8,9},{9,8},{10,11... | collective-permute-start | bytes 442376 | tf_op jit(solution)/shard_map/ppermute | solution.py:431

commit v3 on v2

--- a/solution.py
+++ b/solution.py
@@ -39,6 +39,10 @@
 def place():
     index = lax.axis_index("tile").astype(jnp.int32)
     return lax.rem(index, 2), lax.rem(lax.div(index, 2), 4)
+
+
+def reach(core, k):
+    return jnp.where(core == 0, k, 3 - k) if k in (1, 2) else k
 
 
 def put_edges(out, own_row, side, slots, cross, link, codes, tile):
@@ -305,10 +309,10 @@
 
 
 def spread_kernel(keep, recv, own, *sends):
-    quad = place()[1]
+    core, quad = place()
     own[...] = keep[quad] + recv[quad].astype(F32)
     for k, send in enumerate(sends):
-        other = quad ^ (k + 1)
+        other = quad ^ reach(core, k + 1)
         send[...] = (keep[other] + recv[other].astype(F32)).astype(BF16)
 
 
@@ -334,7 +338,7 @@
     for k, piece in enumerate(pieces):
         rows[k] = piece[...].astype(F32) * scale
         half = 1 - core if plan[k][0] else core
-        slot = half * 4 + (quad ^ plan[k][1])
+        slot = half * 4 + (quad ^ reach(half, plan[k][1]))
         start = pl.multiple_of(slot * depth, depth)
         copy = pltpu.make_async_copy(rows.at[k], out.at[:, pl.ds(start, depth), :], sem.at[k])
         copy.start()
@@ -420,9 +424,17 @@
 
 
 def edge_swaps(to_core, to_link):
-    count = lax.axis_size("tile")
-    ends = [(s, s + 1) for s in range(1, count - 1, 2)]
-    link = lax.ppermute(to_link, "tile", ends + [(t, s) for s, t in ends])
+    groups, count = lax.axis_size("groups"), lax.axis_size("tile")
+    pairs = []
+    for group in range(groups):
+        other = group ^ 1 if groups % 2 == 0 else group
+        for s in range(count):
+            if s in (0, count - 1):
+                t = s if other != group else count - 1 - s
+                pairs.append((group * count + s, other * count + t))
+            else:
+                pairs.append((group * count + s, group * count + (s + 1 if s & 1 else s - 1)))
+    link = lax.ppermute(to_link, ("groups", "tile"), pairs)
     return swap(to_core, 1), link
 
 
@@ -432,9 +444,12 @@
 
 
 def quad_swaps(values):
+    count = lax.axis_size("tile")
     got = []
     for k, value in enumerate(values):
-        got.append(swap(value, 2 * (k + 1)))
+        even, odd = 2 * (k + 1), 2 * (2 - k if k < 2 else 3)
+        pairs = [(s, s ^ (odd if s & 1 else even)) for s in range(count)]
+        got.append(lax.ppermute(value, "tile", pairs))
     return got
 
 

time: 51.3 us -> 50 us (0.975)
  starting transfers between devices: 18.4 us -> 15 us
  waiting for transfers between devices: 15.9 us -> 18.3 us
    ppermute x14 -> x8, starting transfers between devices: 17.1 us -> 3.83 us  [swap(): lax.ppermute(value, 'tile', [(source, source ^ bit) for source in range(c...]
    ppermute x2 -> x8, waiting for transfers between devices: 0.01 us -> 10.9 us  [the longest x6 10.9 us: quad_swaps(): got.append(lax.ppermute(value, 'tile', pairs))]
    ppermute x2 -> x8, starting transfers between devices: 1.3 us -> 11.2 us  [the longest x6 7.1 us: quad_swaps(): got.append(lax.ppermute(value, 'tile', pairs))]
    ppermute x14 -> x8, waiting for transfers between devices: 15.9 us -> 7.44 us  [swap(): lax.ppermute(value, 'tile', [(source, source ^ bit) for source in range(c...]
where the time goes in v3:
time: 50 us; the launch traced here: 49.8 us
  waiting for transfers between devices  18.3 us (37%)
  Pallas kernels  15.5 us (31%)
  starting transfers between devices  15 us (30%)
  between operations  0.82 us (2%)
    ppermute x6, waiting for transfers between devices, quad_swaps(): got.append(lax.ppermute(value, 'tile', pairs))  10.9 us
    ppermute x8, waiting for transfers between devices, swap(): lax.ppermute(value, 'tile', [(source, source ^ bit) for source in range(c...  7.44 us
    ppermute x6, starting transfers between devices, quad_swaps(): got.append(lax.ppermute(value, 'tile', pairs))  7.1 us
    ppermute x2, starting transfers between devices, edge_swaps(): link = lax.ppermute(to_link, ('groups', 'tile'), pairs)  4.1 us
    ppermute x8, starting transfers between devices, swap(): lax.ppermute(value, 'tile', [(source, source ^ bit) for source in range(c...  3.83 us
    pallas_call x1, Pallas kernels, backward(): call(backward_kernel, 18 * slots * side * side * channels * channels, 4 <...  3.54 us
    pallas_call x1, Pallas kernels, product(): call(functools.partial(product_kernel, early), 2 * slots * side * side *...  2.94 us
    pallas_call x3, Pallas kernels, collect(): call(functools.partial(collect_kernel, scale, plan), 1 << 20, count << 19...  2.79 us
  transfers between devices with their start and end apart: 16, of which 7 were waited for; matrix products, arithmetic and copies ran while one was open for 0% of the time, Pallas kernels for 19%

profile of v3, /device:TPU:0, one launch (start us, length us, event | category | flops | bytes accessed | tf_op | source)
XLA Modules:
  0.0 49.8 jit_solution(13661172726084324904)
XLA Ops:
  0.6 2.5 %shard_map.76 = (bf16[6,16,16,768]{3,2,1,0:T(8,128)(2,1)S(1)}, bf16[2304,256]{1,0:T(8,128)(2,1)S(1)}, bf16[6,16,16,256]{3,2,1,0:T(8,128)(2,1)S(1)}, bf16[6,16,25...) custom-call(s32[6,8]{1,0:T(8,128)} %codes.5, bf16[6,16,16,256]{3,2,1,0:T(8,128)(2,1)} %maps.1, bf16[2304,256]{1,0:T(8,128)(2,1)} %bitcast.1, ...), custom_call_target="tpu_custom_call" | custom-call | flops 1048576 | bytes 6291456 | tf_op jit(solution)/shard_map/pallas_call | solution.py:145
  3.1 0.6 %collective-permute-start = (bf16[6,16,256]{2,1,0:T(8,128)(2,1)S(1)}, bf16[6,16,256]{2,1,0:T(8,128)(2,1)S(1)}, u32[]{:S(2)}, u32[]{:S(2)}) collective-permute-start(bf16[6,16,256]{2,1,0:T(8,128)(2,1)S(1)} %get-tuple-element.26), channel_id=1, source_target_pairs={{0,1},{1,0},{2,3},{3,2},{4,5},{5,4},{6,7},{7,6},{8,9},{9,8},{10,11... | collective-permute-start | bytes 147464 | tf_op jit(solution)/shard_map/ppermute | solution.py:443
  3.7 2.6 %collective-permute-start.1 = (bf16[6,16,256]{2,1,0:T(8,128)(2,1)S(1)}, bf16[6,16,256]{2,1,0:T(8,128)(2,1)S(1)}, u32[]{:S(2)}, u32[]{:S(2)}) collective-permute-start(bf16[6,16,256]{2,1,0:T(8,128)(2,1)S(1)} %get-tuple-element.27), channel_id=1, source_target_pairs={{0,16},{1,2},{2,1},{3,4},{4,3},{5,6},{6,5},{7,8},{8,7},{9,10},{10,... | collective-permute-start | bytes 147464 | tf_op jit(solution)/shard_map/ppermute | solution.py:437
  6.3 2.9 %shard_map.77 = (f32[6,16,16,256]{3,2,1,0:T(8,128)S(1)}, bf16[6,16,16,256]{3,2,1,0:T(8,128)(2,1)S(1)}, bf16[6,16,16,256]{3,2,1,0:T(8,128)(2,1)S(1)}) custom-call(s32[6]{0:T(128)} %pos.5, bf16[6,16,16,768]{3,2,1,0:T(8,128)(2,1)S(1)} %get-tuple-element.22.inner, bf16[2304,256]{1,0:T(8,128)(2,1)S(1)} %get-tuple-element.23.weights, ...), custom_call_target="tpu_custom_call" | custom-call | flops 1811939328 | bytes 6291456 | tf_op jit(solution)/shard_map/pallas_call | solution.py:189
  9.2 1.2 %shard_map.78 = (bf16[6,16,16,256]{3,2,1,0:T(8,128)(2,1)S(1)}, bf16[6,16,16,256]{3,2,1,0:T(8,128)(2,1)S(1)}, bf16[6,2,16,768]{3,2,1,0:T(8,128)(2,1)S(1)}, bf16[6...) custom-call(s32[6,8]{1,0:T(8,128)} %codes.5, s32[6]{0:T(128)} %pos.5, ...), custom_call_target="tpu_custom_call", output_to_operand_aliasing={{0}: (8, {}), {1}: (9, {})} | custom-call | flops 75497472 | bytes 8388608 | tf_op jit(solution)/shard_map/pallas_call | solution.py:252
  10.4 1.2 %shard_map.81 = bf16[4,9,32,256]{3,2,1,0:T(8,128)(2,1)S(1)} custom-call(bf16[6,16,16,768]{3,2,1,0:T(8,128)(2,1)S(1)} %get-tuple-element.22.inner, bf16[6,2,16,768]{3,2,1,0:T(8,128)(2,1)S(1)} %get-tuple-element.35.edge, bf16[6,16,16,256]{3,2,1,0:T(8,128)(2,1)S(1)} %get-tuple-element.31.grad), custom_call_target="tpu_custom_call" | custom-call | flops 905969664 | bytes 6291456 | tf_op jit(solution)/shard_map/pallas_call | solution.py:301
  11.8 1.2 %shard_map.80.keep = f32[4,9,32,256]{3,2,1,0:T(8,128)S(1)} custom-call(bf16[6,16,16,768]{3,2,1,0:T(8,128)(2,1)S(1)} %get-tuple-element.22.inner, bf16[6,2,16,768]{3,2,1,0:T(8,128)(2,1)S(1)} %get-tuple-element.35.edge, bf16[6,16,16,256]{3,2,1,0:T(8,128)(2,1)S(1)} %get-tuple-element.31.grad), custom_call_target="tpu_custom_call" | custom-call | flops 905969664 | bytes 6291456 | tf_op jit(solution)/shard_map/pallas_call | solution.py:301
  13.0 0.8 %collective-permute-done.4.recv = bf16[4,9,32,256]{3,2,1,0:T(8,128)(2,1)S(1)} collective-permute-done((bf16[4,9,32,256]{3,2,1,0:T(8,128)(2,1)S(1)}, bf16[4,9,32,256]{3,2,1,0:T(8,128)(2,1)S(1)}, u32[]{:S(2)}, u32[]{:S(2)}) %collective-permute-start.4) | collective-permute-done | bytes 589856 | tf_op jit(solution)/shard_map/ppermute | solution.py:443
  13.9 1.5 %collective-permute-start.5 = (bf16[9,32,256]{2,1,0:T(8,128)(2,1)S(1)}, bf16[9,32,256]{2,1,0:T(8,128)(2,1)S(1)}, u32[]{:S(2)}, u32[]{:S(2)}) collective-permute-start(bf16[9,32,256]{2,1,0:T(8,128)(2,1)S(1)} %get-tuple-element.37), channel_id=1, source_target_pairs={{0,2},{1,5},{2,0},{3,7},{4,6},{5,1},{6,4},{7,3},{8,10},{9,13},{10,... | collective-permute-start | bytes 442376 | tf_op jit(solution)/shard_map/ppermute | solution.py:452
  15.3 1.6 %collective-permute-start.6 = (bf16[9,32,256]{2,1,0:T(8,128)(2,1)S(1)}, bf16[9,32,256]{2,1,0:T(8,128)(2,1)S(1)}, u32[]{:S(2)}, u32[]{:S(2)}) collective-permute-start(bf16[9,32,256]{2,1,0:T(8,128)(2,1)S(1)} %get-tuple-element.38), channel_id=1, source_target_pairs={{0,4},{1,3},{2,6},{3,1},{4,0},{5,7},{6,2},{7,5},{8,12},{9,11},{10,... | collective-permute-start | bytes 442376 | tf_op jit(solution)/shard_map/ppermute | solution.py:452
  17.4 2.7 %collective-permute-done.5 = bf16[9,32,256]{2,1,0:T(8,128)(2,1)S(1)} collective-permute-done((bf16[9,32,256]{2,1,0:T(8,128)(2,1)S(1)}, bf16[9,32,256]{2,1,0:T(8,128)(2,1)S(1)}, u32[]{:S(2)}, u32[]{:S(2)}) %collective-permute-start.5) | collective-permute-done | bytes 147488 | tf_op jit(solution)/shard_map/ppermute | solution.py:452
  20.2 1.6 %collective-permute-done.6 = bf16[9,32,256]{2,1,0:T(8,128)(2,1)S(1)} collective-permute-done((bf16[9,32,256]{2,1,0:T(8,128)(2,1)S(1)}, bf16[9,32,256]{2,1,0:T(8,128)(2,1)S(1)}, u32[]{:S(2)}, u32[]{:S(2)}) %collective-permute-start.6) | collective-permute-done | bytes 147488 | tf_op jit(solution)/shard_map/ppermute | solution.py:452
  21.8 2.3 %collective-permute-done.7 = bf16[9,32,256]{2,1,0:T(8,128)(2,1)S(1)} collective-permute-done((bf16[9,32,256]{2,1,0:T(8,128)(2,1)S(1)}, bf16[9,32,256]{2,1,0:T(8,128)(2,1)S(1)}, u32[]{:S(2)}, u32[]{:S(2)}) %collective-permute-start.7) | collective-permute-done | bytes 147488 | tf_op jit(solution)/shard_map/ppermute | solution.py:452
  24.2 2.7 %collective-permute-start.8 = (bf16[9,32,256]{2,1,0:T(8,128)(2,1)S(1)}, bf16[9,32,256]{2,1,0:T(8,128)(2,1)S(1)}, u32[]{:S(2)}, u32[]{:S(2)}) collective-permute-start(bf16[9,32,256]{2,1,0:T(8,128)(2,1)S(1)} %add_convert_fusion.1), channel_id=1, source_target_pairs={{0,8},{1,9},{2,10},{3,11},{4,12},{5,13},{6,14},{7,15},{8,0},{9,1},... | collective-permute-start | bytes 442376 | tf_op jit(solution)/shard_map/ppermute | solution.py:443
  26.8 6.7 %collective-permute-done.8 = bf16[9,32,256]{2,1,0:T(8,128)(2,1)S(1)} collective-permute-done((bf16[9,32,256]{2,1,0:T(8,128)(2,1)S(1)}, bf16[9,32,256]{2,1,0:T(8,128)(2,1)S(1)}, u32[]{:S(2)}, u32[]{:S(2)}) %collective-permute-start.8) | collective-permute-done | bytes 147488 | tf_op jit(solution)/shard_map/ppermute | solution.py:443
  33.6 0.9 %collective-permute-start.11 = (bf16[9,32,256]{2,1,0:T(8,128)(2,1)S(1)}, bf16[9,32,256]{2,1,0:T(8,128)(2,1)S(1)}, u32[]{:S(2)}, u32[]{:S(2)}) collective-permute-start(bf16[9,32,256]{2,1,0:T(8,128)(2,1)S(1)} %add_convert_fusion.refs_0_), channel_id=1, source_target_pairs={{0,2},{1,5},{2,0},{3,7},{4,6},{5,1},{6,4},{7,3},{8,10},{9,13},{10,... | collective-permute-start | bytes 442376 | tf_op jit(solution)/shard_map/ppermute | solution.py:452
  34.4 2.6 %collective-permute-start.9 = (bf16[9,32,256]{2,1,0:T(8,128)(2,1)S(1)}, bf16[9,32,256]{2,1,0:T(8,128)(2,1)S(1)}, u32[]{:S(2)}, u32[]{:S(2)}) collective-permute-start(bf16[9,32,256]{2,1,0:T(8,128)(2,1)S(1)} %add_convert_fusion.refs_0_), channel_id=1, source_target_pairs={{0,6},{1,7},{2,4},{3,5},{4,2},{5,3},{6,0},{7,1},{8,14},{9,15},{10,... | collective-permute-start | bytes 442376 | tf_op jit(solution)/shard_map/ppermute | solution.py:452
  37.1 1.5 %collective-permute-start.3 = (bf16[6,16,256]{2,1,0:T(8,128)(2,1)S(1)}, bf16[6,16,256]{2,1,0:T(8,128)(2,1)S(1)}, u32[]{:S(2)}, u32[]{:S(2)}) collective-permute-start(bf16[6,16,256]{2,1,0:T(8,128)(2,1)S(1)} %get-tuple-element.33), channel_id=1, source_target_pairs={{0,16},{1,2},{2,1},{3,4},{4,3},{5,6},{6,5},{7,8},{8,7},{9,10},{10,... | collective-permute-start | bytes 147464 | tf_op jit(solution)/shard_map/ppermute | solution.py:437
  38.6 1.7 %collective-permute-done.12.refs_1_ = bf16[9,32,256]{2,1,0:T(8,128)(2,1)S(1)} collective-permute-done((bf16[9,32,256]{2,1,0:T(8,128)(2,1)S(1)}, bf16[9,32,256]{2,1,0:T(8,128)(2,1)S(1)}, u32[]{:S(2)}, u32[]{:S(2)}) %collective-permute-start.12) | collective-permute-done | bytes 147488 | tf_op jit(solution)/shard_map/ppermute | solution.py:452
  40.8 2.5 %collective-permute-done.9.refs_2_ = bf16[9,32,256]{2,1,0:T(8,128)(2,1)S(1)} collective-permute-done((bf16[9,32,256]{2,1,0:T(8,128)(2,1)S(1)}, bf16[9,32,256]{2,1,0:T(8,128)(2,1)S(1)}, u32[]{:S(2)}, u32[]{:S(2)}) %collective-permute-start.9) | collective-permute-done | bytes 147488 | tf_op jit(solution)/shard_map/ppermute | solution.py:452
  43.4 3.5 %shard_map.79 = (bf16[6,16,16,256]{3,2,1,0:T(8,128)(2,1)}, bf16[6,16,16,256]{3,2,1,0:T(8,128)(2,1)}) custom-call(s32[6,8]{1,0:T(8,128)S(1)} %copy-done.1, s32[6]{0:T(128)S(1)} %copy-done.2, bf16[6,16,16,256]{3,2,1,0:T(8,128)(2,1)S(1)} %get-tuple-element.30.act, bf16[6,16,16,256]{3,2,1,0:T(8,128)(2,1)S(1)} %get-tuple-element.31.grad, ...), custom_call_target="tpu_custom_call" | custom-call | flops 1811939328 | bytes 4194304 | tf_op jit(solution)/shard_map/pallas_call | solution.py:410
  46.9 0.9 %shard_map.83.refs_5_ = f32[9,256,256]{2,1,0:T(8,128)} custom-call(bf16[9,32,256]{2,1,0:T(8,128)(2,1)S(1)} %add_convert_fusion.refs_0_, bf16[9,32,256]{2,1,0:T(8,128)(2,1)S(1)} %collective-permute-done.15.refs_1_), custom_call_target="tpu_custom_call" | custom-call | flops 1048576 | bytes 1048576 | tf_op jit(solution)/shard_map/pallas_call | solution.py:360
  47.8 1.2 %shard_map.84.refs_1_ = f32[9,256,256]{2,1,0:T(8,128)} custom-call(bf16[9,32,256]{2,1,0:T(8,128)(2,1)S(1)} %collective-permute-done.11.refs_0_, bf16[9,32,256]{2,1,0:T(8,128)(2,1)S(1)} %collective-permute-done.12.refs_1_, bf16[9,32,256]{2,1,0:T(8,128)(2,1)S(1)} %collective-permute-done.9.refs_2_, ...), custom_call_target="tpu_custom_call", output_to_operand_aliasing={{}: (5, {})} | custom-call | flops 1048576 | bytes 2621440 | tf_op jit(solution)/shard_map/pallas_call | solution.py:360
  49.0 0.8 %shard_map.85 = f32[9,256,256]{2,1,0:T(8,128)} custom-call(bf16[9,32,256]{2,1,0:T(8,128)(2,1)S(1)} %collective-permute-done.10.refs_0_, f32[9,256,256]{2,1,0:T(8,128)} %shard_map.84.refs_1_), custom_call_target="tpu_custom_call", output_to_operand_aliasing={{}: (1, {})} | custom-call | flops 1048576 | bytes 524288 | tf_op jit(solution)/shard_map/pallas_call | solution.py:360
  (26 shorter events, 1.5 us)
Async XLA Ops:
  3.1 6.1 %collective-permute-start = (bf16[6,16,256]{2,1,0:T(8,128)(2,1)S(1)}, bf16[6,16,256]{2,1,0:T(8,128)(2,1)S(1)}, u32[]{:S(2)}, u32[]{:S(2)}) collective-permute-start(bf16[6,16,256]{2,1,0:T(8,128)(2,1)S(1)} %get-tuple-element.26), channel_id=1, source_target_pairs={{0,1},{1,0},{2,3},{3,2},{4,5},{5,4},{6,7},{7,6},{8,9},{9,8},{10,11... | collective-permute-start | bytes 147464 | tf_op jit(solution)/shard_map/ppermute | solution.py:443
  3.7 5.5 %collective-permute-start.1 = (bf16[6,16,256]{2,1,0:T(8,128)(2,1)S(1)}, bf16[6,16,256]{2,1,0:T(8,128)(2,1)S(1)}, u32[]{:S(2)}, u32[]{:S(2)}) collective-permute-start(bf16[6,16,256]{2,1,0:T(8,128)(2,1)S(1)} %get-tuple-element.27), channel_id=1, source_target_pairs={{0,16},{1,2},{2,1},{3,4},{4,3},{5,6},{6,5},{7,8},{8,7},{9,10},{10,... | collective-permute-start | bytes 147464 | tf_op jit(solution)/shard_map/ppermute | solution.py:437
  11.7 2.1 %collective-permute-start.4 = (bf16[4,9,32,256]{3,2,1,0:T(8,128)(2,1)S(1)}, bf16[4,9,32,256]{3,2,1,0:T(8,128)(2,1)S(1)}, u32[]{:S(2)}, u32[]{:S(2)}) collective-permute-start(bf16[4,9,32,256]{3,2,1,0:T(8,128)(2,1)S(1)} %shard_map.81), channel_id=1, source_target_pairs={{0,1},{1,0},{2,3},{3,2},{4,5},{5,4},{6,7},{7,6},{8,9},{9,8},{10,11... | collective-permute-start | bytes 1769480 | tf_op jit(solution)/shard_map/ppermute | solution.py:443
  12.9 30.4 %copy-start = (bf16[9,256,256]{2,1,0:T(8,128)(2,1)S(1)}, bf16[9,256,256]{2,1,0:T(8,128)(2,1)}, u32[]{:S(2)}) copy-start(bf16[9,256,256]{2,1,0:T(8,128)(2,1)} %param.6) | copy-start | bytes 3538948
  12.9 30.4 %copy-start.1 = (s32[6,8]{1,0:T(8,128)S(1)}, s32[6,8]{1,0:T(8,128)}, u32[]{:S(2)}) copy-start(s32[6,8]{1,0:T(8,128)} %codes.5) | copy-start | bytes 580
  12.9 30.4 %copy-start.2 = (s32[6]{0:T(128)S(1)}, s32[6]{0:T(128)}, u32[]{:S(2)}) copy-start(s32[6]{0:T(128)} %pos.5) | copy-start | bytes 76
  13.9 6.3 %collective-permute-start.5 = (bf16[9,32,256]{2,1,0:T(8,128)(2,1)S(1)}, bf16[9,32,256]{2,1,0:T(8,128)(2,1)S(1)}, u32[]{:S(2)}, u32[]{:S(2)}) collective-permute-start(bf16[9,32,256]{2,1,0:T(8,128)(2,1)S(1)} %get-tuple-element.37), channel_id=1, source_target_pairs={{0,2},{1,5},{2,0},{3,7},{4,6},{5,1},{6,4},{7,3},{8,10},{9,13},{10,... | collective-permute-start | bytes 442376 | tf_op jit(solution)/shard_map/ppermute | solution.py:452
  15.3 6.5 %collective-permute-start.6 = (bf16[9,32,256]{2,1,0:T(8,128)(2,1)S(1)}, bf16[9,32,256]{2,1,0:T(8,128)(2,1)S(1)}, u32[]{:S(2)}, u32[]{:S(2)}) collective-permute-start(bf16[9,32,256]{2,1,0:T(8,128)(2,1)S(1)} %get-tuple-element.38), channel_id=1, source_target_pairs={{0,4},{1,3},{2,6},{3,1},{4,0},{5,7},{6,2},{7,5},{8,12},{9,11},{10,... | collective-permute-start | bytes 442376 | tf_op jit(solution)/shard_map/ppermute | solution.py:452
  16.9 7.1 %collective-permute-start.7 = (bf16[9,32,256]{2,1,0:T(8,128)(2,1)S(1)}, bf16[9,32,256]{2,1,0:T(8,128)(2,1)S(1)}, u32[]{:S(2)}, u32[]{:S(2)}) collective-permute-start(bf16[9,32,256]{2,1,0:T(8,128)(2,1)S(1)} %get-tuple-element.39), channel_id=1, source_target_pairs={{0,6},{1,7},{2,4},{3,5},{4,2},{5,3},{6,0},{7,1},{8,14},{9,15},{10,... | collective-permute-start | bytes 442376 | tf_op jit(solution)/shard_map/ppermute | solution.py:452
  24.2 9.3 %collective-permute-start.8 = (bf16[9,32,256]{2,1,0:T(8,128)(2,1)S(1)}, bf16[9,32,256]{2,1,0:T(8,128)(2,1)S(1)}, u32[]{:S(2)}, u32[]{:S(2)}) collective-permute-start(bf16[9,32,256]{2,1,0:T(8,128)(2,1)S(1)} %add_convert_fusion.1), channel_id=1, source_target_pairs={{0,8},{1,9},{2,10},{3,11},{4,12},{5,13},{6,14},{7,15},{8,0},{9,1},... | collective-permute-start | bytes 442376 | tf_op jit(solution)/shard_map/ppermute | solution.py:443
  33.5 6.8 %collective-permute-start.12 = (bf16[9,32,256]{2,1,0:T(8,128)(2,1)S(1)}, bf16[9,32,256]{2,1,0:T(8,128)(2,1)S(1)}, u32[]{:S(2)}, u32[]{:S(2)}) collective-permute-start(bf16[9,32,256]{2,1,0:T(8,128)(2,1)S(1)} %add_convert_fusion.refs_0_), channel_id=1, source_target_pairs={{0,4},{1,3},{2,6},{3,1},{4,0},{5,7},{6,2},{7,5},{8,12},{9,11},{10,... | collective-permute-start | bytes 442376 | tf_op jit(solution)/shard_map/ppermute | solution.py:452
  33.6 6.7 %collective-permute-start.11 = (bf16[9,32,256]{2,1,0:T(8,128)(2,1)S(1)}, bf16[9,32,256]{2,1,0:T(8,128)(2,1)S(1)}, u32[]{:S(2)}, u32[]{:S(2)}) collective-permute-start(bf16[9,32,256]{2,1,0:T(8,128)(2,1)S(1)} %add_convert_fusion.refs_0_), channel_id=1, source_target_pairs={{0,2},{1,5},{2,0},{3,7},{4,6},{5,1},{6,4},{7,3},{8,10},{9,13},{10,... | collective-permute-start | bytes 442376 | tf_op jit(solution)/shard_map/ppermute | solution.py:452
  34.4 8.9 %collective-permute-start.9 = (bf16[9,32,256]{2,1,0:T(8,128)(2,1)S(1)}, bf16[9,32,256]{2,1,0:T(8,128)(2,1)S(1)}, u32[]{:S(2)}, u32[]{:S(2)}) collective-permute-start(bf16[9,32,256]{2,1,0:T(8,128)(2,1)S(1)} %add_convert_fusion.refs_0_), channel_id=1, source_target_pairs={{0,6},{1,7},{2,4},{3,5},{4,2},{5,3},{6,0},{7,1},{8,14},{9,15},{10,... | collective-permute-start | bytes 442376 | tf_op jit(solution)/shard_map/ppermute | solution.py:452
  37.1 1.5 %collective-permute-start.2 = (bf16[6,16,256]{2,1,0:T(8,128)(2,1)S(1)}, bf16[6,16,256]{2,1,0:T(8,128)(2,1)S(1)}, u32[]{:S(2)}, u32[]{:S(2)}) collective-permute-start(bf16[6,16,256]{2,1,0:T(8,128)(2,1)S(1)} %get-tuple-element.32), channel_id=1, source_target_pairs={{0,1},{1,0},{2,3},{3,2},{4,5},{5,4},{6,7},{7,6},{8,9},{9,8},{10,11... | collective-permute-start | bytes 147464 | tf_op jit(solution)/shard_map/ppermute | solution.py:443
  37.1 6.3 %collective-permute-start.3 = (bf16[6,16,256]{2,1,0:T(8,128)(2,1)S(1)}, bf16[6,16,256]{2,1,0:T(8,128)(2,1)S(1)}, u32[]{:S(2)}, u32[]{:S(2)}) collective-permute-start(bf16[6,16,256]{2,1,0:T(8,128)(2,1)S(1)} %get-tuple-element.33), channel_id=1, source_target_pairs={{0,16},{1,2},{2,1},{3,4},{4,3},{5,6},{6,5},{7,8},{8,7},{9,10},{10,... | collective-permute-start | bytes 147464 | tf_op jit(solution)/shard_map/ppermute | solution.py:437
  38.6 8.3 %collective-permute-start.15 = (bf16[9,32,256]{2,1,0:T(8,128)(2,1)S(1)}, bf16[9,32,256]{2,1,0:T(8,128)(2,1)S(1)}, u32[]{:S(2)}, u32[]{:S(2)}) collective-permute-start(bf16[9,32,256]{2,1,0:T(8,128)(2,1)S(1)} %add_convert_fusion.refs_0_), channel_id=1, source_target_pairs={{0,1},{1,0},{2,3},{3,2},{4,5},{5,4},{6,7},{7,6},{8,9},{9,8},{10,11... | collective-permute-start | bytes 442376 | tf_op jit(solution)/shard_map/ppermute | solution.py:443
  40.3 7.5 %collective-permute-start.14 = (bf16[9,32,256]{2,1,0:T(8,128)(2,1)S(1)}, bf16[9,32,256]{2,1,0:T(8,128)(2,1)S(1)}, u32[]{:S(2)}, u32[]{:S(2)}) collective-permute-start(bf16[9,32,256]{2,1,0:T(8,128)(2,1)S(1)} %collective-permute-done.12.refs_1_), channel_id=1, source_target_pairs={{0,1},{1,0},{2,3},{3,2},{4,5},{5,4},{6,7},{7,6},{8,9},{9,8},{10,11... | collective-permute-start | bytes 442376 | tf_op jit(solution)/shard_map/ppermute | solution.py:443
  40.3 7.5 %collective-permute-start.13 = (bf16[9,32,256]{2,1,0:T(8,128)(2,1)S(1)}, bf16[9,32,256]{2,1,0:T(8,128)(2,1)S(1)}, u32[]{:S(2)}, u32[]{:S(2)}) collective-permute-start(bf16[9,32,256]{2,1,0:T(8,128)(2,1)S(1)} %collective-permute-done.11.refs_0_), channel_id=1, source_target_pairs={{0,1},{1,0},{2,3},{3,2},{4,5},{5,4},{6,7},{7,6},{8,9},{9,8},{10,11... | collective-permute-start | bytes 442376 | tf_op jit(solution)/shard_map/ppermute | solution.py:443
  43.3 5.7 %collective-permute-start.10 = (bf16[9,32,256]{2,1,0:T(8,128)(2,1)S(1)}, bf16[9,32,256]{2,1,0:T(8,128)(2,1)S(1)}, u32[]{:S(2)}, u32[]{:S(2)}) collective-permute-start(bf16[9,32,256]{2,1,0:T(8,128)(2,1)S(1)} %collective-permute-done.9.refs_2_), channel_id=1, source_target_pairs={{0,1},{1,0},{2,3},{3,2},{4,5},{5,4},{6,7},{7,6},{8,9},{9,8},{10,11... | collective-permute-start | bytes 442376 | tf_op jit(solution)/shard_map/ppermute | solution.py:443

commit v4 on v3

--- a/solution.py
+++ b/solution.py
@@ -499,10 +499,10 @@
     its.append(swap(pieces[3], 1))
     weight_grad = collect(((0, 0), (1, 0)), [pieces[0], its[0]], scale, whole, None)
     weight_grad = collect(
-        ((0, 1), (0, 2), (0, 3), (1, 1), (1, 2)),
-        pieces[1:] + its[1:3], scale, whole, weight_grad,
-    )
-    weight_grad = collect(((1, 3),), its[3:], scale, whole, weight_grad)
+        ((0, 1), (0, 2), (0, 3)),
+        pieces[1:], scale, whole, weight_grad,
+    )
+    weight_grad = collect(((1, 1), (1, 2), (1, 3)), its[1:], scale, whole, weight_grad)
     cross, link = edge_swaps(to_core, to_link)
     activation, input_grad = backward(
         neighbours, tile_pos, activation, grad, cross, link,

time: 50 us -> 49.3 us (0.986)
  waiting for transfers between devices: 18.3 us -> 17.6 us
    ppermute x6, waiting for transfers between devices: 10.9 us -> 10.2 us  [quad_swaps(): got.append(lax.ppermute(value, 'tile', pairs))]
where the time goes in v4:
time: 49.3 us; the launch traced here: 49.1 us
  waiting for transfers between devices  17.6 us (36%)
  Pallas kernels  15.5 us (31%)
  starting transfers between devices  15 us (30%)
  between operations  0.8 us (2%)
    ppermute x6, waiting for transfers between devices, quad_swaps(): got.append(lax.ppermute(value, 'tile', pairs))  10.2 us
    ppermute x8, waiting for transfers between devices, swap(): lax.ppermute(value, 'tile', [(source, source ^ bit) for source in range(c...  7.44 us
    ppermute x6, starting transfers between devices, quad_swaps(): got.append(lax.ppermute(value, 'tile', pairs))  7.11 us
    ppermute x2, starting transfers between devices, edge_swaps(): link = lax.ppermute(to_link, ('groups', 'tile'), pairs)  4.1 us
    ppermute x8, starting transfers between devices, swap(): lax.ppermute(value, 'tile', [(source, source ^ bit) for source in range(c...  3.83 us
    pallas_call x1, Pallas kernels, backward(): call(backward_kernel, 18 * slots * side * side * channels * channels, 4 <...  3.54 us
    pallas_call x1, Pallas kernels, product(): call(functools.partial(product_kernel, early), 2 * slots * side * side *...  2.94 us
    pallas_call x3, Pallas kernels, collect(): call(functools.partial(collect_kernel, scale, plan), 1 << 20, count << 19...  2.79 us
  transfers between devices with their start and end apart: 16, of which 7 were waited for; matrix products, arithmetic and copies ran while one was open for 0% of the time, Pallas kernels for 19%

profile of v4, /device:TPU:0, one launch (start us, length us, event | category | flops | bytes accessed | tf_op | source)
XLA Modules:
  0.0 49.1 jit_solution(8774763717720846959)
XLA Ops:
  0.6 2.5 %shard_map.76 = (bf16[6,16,16,768]{3,2,1,0:T(8,128)(2,1)S(1)}, bf16[2304,256]{1,0:T(8,128)(2,1)S(1)}, bf16[6,16,16,256]{3,2,1,0:T(8,128)(2,1)S(1)}, bf16[6,16,25...) custom-call(s32[6,8]{1,0:T(8,128)} %codes.5, bf16[6,16,16,256]{3,2,1,0:T(8,128)(2,1)} %maps.1, bf16[2304,256]{1,0:T(8,128)(2,1)} %bitcast.1, ...), custom_call_target="tpu_custom_call" | custom-call | flops 1048576 | bytes 6291456 | tf_op jit(solution)/shard_map/pallas_call | solution.py:145
  3.1 0.6 %collective-permute-start = (bf16[6,16,256]{2,1,0:T(8,128)(2,1)S(1)}, bf16[6,16,256]{2,1,0:T(8,128)(2,1)S(1)}, u32[]{:S(2)}, u32[]{:S(2)}) collective-permute-start(bf16[6,16,256]{2,1,0:T(8,128)(2,1)S(1)} %get-tuple-element.26), channel_id=1, source_target_pairs={{0,1},{1,0},{2,3},{3,2},{4,5},{5,4},{6,7},{7,6},{8,9},{9,8},{10,11... | collective-permute-start | bytes 147464 | tf_op jit(solution)/shard_map/ppermute | solution.py:443
  3.7 2.6 %collective-permute-start.1 = (bf16[6,16,256]{2,1,0:T(8,128)(2,1)S(1)}, bf16[6,16,256]{2,1,0:T(8,128)(2,1)S(1)}, u32[]{:S(2)}, u32[]{:S(2)}) collective-permute-start(bf16[6,16,256]{2,1,0:T(8,128)(2,1)S(1)} %get-tuple-element.27), channel_id=1, source_target_pairs={{0,16},{1,2},{2,1},{3,4},{4,3},{5,6},{6,5},{7,8},{8,7},{9,10},{10,... | collective-permute-start | bytes 147464 | tf_op jit(solution)/shard_map/ppermute | solution.py:437
  6.3 2.9 %shard_map.77 = (f32[6,16,16,256]{3,2,1,0:T(8,128)S(1)}, bf16[6,16,16,256]{3,2,1,0:T(8,128)(2,1)S(1)}, bf16[6,16,16,256]{3,2,1,0:T(8,128)(2,1)S(1)}) custom-call(s32[6]{0:T(128)} %pos.5, bf16[6,16,16,768]{3,2,1,0:T(8,128)(2,1)S(1)} %get-tuple-element.22.inner, bf16[2304,256]{1,0:T(8,128)(2,1)S(1)} %get-tuple-element.23.weights, ...), custom_call_target="tpu_custom_call" | custom-call | flops 1811939328 | bytes 6291456 | tf_op jit(solution)/shard_map/pallas_call | solution.py:189
  9.2 1.2 %shard_map.78 = (bf16[6,16,16,256]{3,2,1,0:T(8,128)(2,1)S(1)}, bf16[6,16,16,256]{3,2,1,0:T(8,128)(2,1)S(1)}, bf16[6,2,16,768]{3,2,1,0:T(8,128)(2,1)S(1)}, bf16[6...) custom-call(s32[6,8]{1,0:T(8,128)} %codes.5, s32[6]{0:T(128)} %pos.5, ...), custom_call_target="tpu_custom_call", output_to_operand_aliasing={{0}: (8, {}), {1}: (9, {})} | custom-call | flops 75497472 | bytes 8388608 | tf_op jit(solution)/shard_map/pallas_call | solution.py:252
  10.4 1.2 %shard_map.81 = bf16[4,9,32,256]{3,2,1,0:T(8,128)(2,1)S(1)} custom-call(bf16[6,16,16,768]{3,2,1,0:T(8,128)(2,1)S(1)} %get-tuple-element.22.inner, bf16[6,2,16,768]{3,2,1,0:T(8,128)(2,1)S(1)} %get-tuple-element.35.edge, bf16[6,16,16,256]{3,2,1,0:T(8,128)(2,1)S(1)} %get-tuple-element.31.grad), custom_call_target="tpu_custom_call" | custom-call | flops 905969664 | bytes 6291456 | tf_op jit(solution)/shard_map/pallas_call | solution.py:301
  11.8 1.2 %shard_map.80.keep = f32[4,9,32,256]{3,2,1,0:T(8,128)S(1)} custom-call(bf16[6,16,16,768]{3,2,1,0:T(8,128)(2,1)S(1)} %get-tuple-element.22.inner, bf16[6,2,16,768]{3,2,1,0:T(8,128)(2,1)S(1)} %get-tuple-element.35.edge, bf16[6,16,16,256]{3,2,1,0:T(8,128)(2,1)S(1)} %get-tuple-element.31.grad), custom_call_target="tpu_custom_call" | custom-call | flops 905969664 | bytes 6291456 | tf_op jit(solution)/shard_map/pallas_call | solution.py:301
  13.0 0.8 %collective-permute-done.4.recv = bf16[4,9,32,256]{3,2,1,0:T(8,128)(2,1)S(1)} collective-permute-done((bf16[4,9,32,256]{3,2,1,0:T(8,128)(2,1)S(1)}, bf16[4,9,32,256]{3,2,1,0:T(8,128)(2,1)S(1)}, u32[]{:S(2)}, u32[]{:S(2)}) %collective-permute-start.4) | collective-permute-done | bytes 589856 | tf_op jit(solution)/shard_map/ppermute | solution.py:443
  13.9 1.5 %collective-permute-start.5 = (bf16[9,32,256]{2,1,0:T(8,128)(2,1)S(1)}, bf16[9,32,256]{2,1,0:T(8,128)(2,1)S(1)}, u32[]{:S(2)}, u32[]{:S(2)}) collective-permute-start(bf16[9,32,256]{2,1,0:T(8,128)(2,1)S(1)} %get-tuple-element.37), channel_id=1, source_target_pairs={{0,2},{1,5},{2,0},{3,7},{4,6},{5,1},{6,4},{7,3},{8,10},{9,13},{10,... | collective-permute-start | bytes 442376 | tf_op jit(solution)/shard_map/ppermute | solution.py:452
  15.3 1.6 %collective-permute-start.6 = (bf16[9,32,256]{2,1,0:T(8,128)(2,1)S(1)}, bf16[9,32,256]{2,1,0:T(8,128)(2,1)S(1)}, u32[]{:S(2)}, u32[]{:S(2)}) collective-permute-start(bf16[9,32,256]{2,1,0:T(8,128)(2,1)S(1)} %get-tuple-element.38), channel_id=1, source_target_pairs={{0,4},{1,3},{2,6},{3,1},{4,0},{5,7},{6,2},{7,5},{8,12},{9,11},{10,... | collective-permute-start | bytes 442376 | tf_op jit(solution)/shard_map/ppermute | solution.py:452
  17.4 2.7 %collective-permute-done.5 = bf16[9,32,256]{2,1,0:T(8,128)(2,1)S(1)} collective-permute-done((bf16[9,32,256]{2,1,0:T(8,128)(2,1)S(1)}, bf16[9,32,256]{2,1,0:T(8,128)(2,1)S(1)}, u32[]{:S(2)}, u32[]{:S(2)}) %collective-permute-start.5) | collective-permute-done | bytes 147488 | tf_op jit(solution)/shard_map/ppermute | solution.py:452
  20.2 1.6 %collective-permute-done.6 = bf16[9,32,256]{2,1,0:T(8,128)(2,1)S(1)} collective-permute-done((bf16[9,32,256]{2,1,0:T(8,128)(2,1)S(1)}, bf16[9,32,256]{2,1,0:T(8,128)(2,1)S(1)}, u32[]{:S(2)}, u32[]{:S(2)}) %collective-permute-start.6) | collective-permute-done | bytes 147488 | tf_op jit(solution)/shard_map/ppermute | solution.py:452
  21.8 2.3 %collective-permute-done.7 = bf16[9,32,256]{2,1,0:T(8,128)(2,1)S(1)} collective-permute-done((bf16[9,32,256]{2,1,0:T(8,128)(2,1)S(1)}, bf16[9,32,256]{2,1,0:T(8,128)(2,1)S(1)}, u32[]{:S(2)}, u32[]{:S(2)}) %collective-permute-start.7) | collective-permute-done | bytes 147488 | tf_op jit(solution)/shard_map/ppermute | solution.py:452
  24.2 2.7 %collective-permute-start.8 = (bf16[9,32,256]{2,1,0:T(8,128)(2,1)S(1)}, bf16[9,32,256]{2,1,0:T(8,128)(2,1)S(1)}, u32[]{:S(2)}, u32[]{:S(2)}) collective-permute-start(bf16[9,32,256]{2,1,0:T(8,128)(2,1)S(1)} %add_convert_fusion.1), channel_id=1, source_target_pairs={{0,8},{1,9},{2,10},{3,11},{4,12},{5,13},{6,14},{7,15},{8,0},{9,1},... | collective-permute-start | bytes 442376 | tf_op jit(solution)/shard_map/ppermute | solution.py:443
  26.8 6.7 %collective-permute-done.8 = bf16[9,32,256]{2,1,0:T(8,128)(2,1)S(1)} collective-permute-done((bf16[9,32,256]{2,1,0:T(8,128)(2,1)S(1)}, bf16[9,32,256]{2,1,0:T(8,128)(2,1)S(1)}, u32[]{:S(2)}, u32[]{:S(2)}) %collective-permute-start.8) | collective-permute-done | bytes 147488 | tf_op jit(solution)/shard_map/ppermute | solution.py:443
  33.9 1.7 %collective-permute-start.11 = (bf16[9,32,256]{2,1,0:T(8,128)(2,1)S(1)}, bf16[9,32,256]{2,1,0:T(8,128)(2,1)S(1)}, u32[]{:S(2)}, u32[]{:S(2)}) collective-permute-start(bf16[9,32,256]{2,1,0:T(8,128)(2,1)S(1)} %add_convert_fusion.refs_0_), channel_id=1, source_target_pairs={{0,4},{1,3},{2,6},{3,1},{4,0},{5,7},{6,2},{7,5},{8,12},{9,11},{10,... | collective-permute-start | bytes 442376 | tf_op jit(solution)/shard_map/ppermute | solution.py:452
  35.6 1.4 %collective-permute-start.9 = (bf16[9,32,256]{2,1,0:T(8,128)(2,1)S(1)}, bf16[9,32,256]{2,1,0:T(8,128)(2,1)S(1)}, u32[]{:S(2)}, u32[]{:S(2)}) collective-permute-start(bf16[9,32,256]{2,1,0:T(8,128)(2,1)S(1)} %add_convert_fusion.refs_0_), channel_id=1, source_target_pairs={{0,2},{1,5},{2,0},{3,7},{4,6},{5,1},{6,4},{7,3},{8,10},{9,13},{10,... | collective-permute-start | bytes 442376 | tf_op jit(solution)/shard_map/ppermute | solution.py:452
  37.1 1.5 %collective-permute-start.3 = (bf16[6,16,256]{2,1,0:T(8,128)(2,1)S(1)}, bf16[6,16,256]{2,1,0:T(8,128)(2,1)S(1)}, u32[]{:S(2)}, u32[]{:S(2)}) collective-permute-start(bf16[6,16,256]{2,1,0:T(8,128)(2,1)S(1)} %get-tuple-element.33), channel_id=1, source_target_pairs={{0,16},{1,2},{2,1},{3,4},{4,3},{5,6},{6,5},{7,8},{8,7},{9,10},{10,... | collective-permute-start | bytes 147464 | tf_op jit(solution)/shard_map/ppermute | solution.py:437
  38.6 2.6 %collective-permute-done.13.refs_2_ = bf16[9,32,256]{2,1,0:T(8,128)(2,1)S(1)} collective-permute-done((bf16[9,32,256]{2,1,0:T(8,128)(2,1)S(1)}, bf16[9,32,256]{2,1,0:T(8,128)(2,1)S(1)}, u32[]{:S(2)}, u32[]{:S(2)}) %collective-permute-start.13) | collective-permute-done | bytes 147488 | tf_op jit(solution)/shard_map/ppermute | solution.py:452
  41.2 0.9 %collective-permute-done.11.refs_1_ = bf16[9,32,256]{2,1,0:T(8,128)(2,1)S(1)} collective-permute-done((bf16[9,32,256]{2,1,0:T(8,128)(2,1)S(1)}, bf16[9,32,256]{2,1,0:T(8,128)(2,1)S(1)}, u32[]{:S(2)}, u32[]{:S(2)}) %collective-permute-start.11) | collective-permute-done | bytes 147488 | tf_op jit(solution)/shard_map/ppermute | solution.py:452
  42.7 3.5 %shard_map.79 = (bf16[6,16,16,256]{3,2,1,0:T(8,128)(2,1)}, bf16[6,16,16,256]{3,2,1,0:T(8,128)(2,1)}) custom-call(s32[6,8]{1,0:T(8,128)S(1)} %copy-done.1, s32[6]{0:T(128)S(1)} %copy-done.2, bf16[6,16,16,256]{3,2,1,0:T(8,128)(2,1)S(1)} %get-tuple-element.30.act, bf16[6,16,16,256]{3,2,1,0:T(8,128)(2,1)S(1)} %get-tuple-element.31.grad, ...), custom_call_target="tpu_custom_call" | custom-call | flops 1811939328 | bytes 4194304 | tf_op jit(solution)/shard_map/pallas_call | solution.py:410
  46.2 0.9 %shard_map.83.refs_3_ = f32[9,256,256]{2,1,0:T(8,128)} custom-call(bf16[9,32,256]{2,1,0:T(8,128)(2,1)S(1)} %add_convert_fusion.refs_0_, bf16[9,32,256]{2,1,0:T(8,128)(2,1)S(1)} %collective-permute-done.15.refs_1_), custom_call_target="tpu_custom_call" | custom-call | flops 1048576 | bytes 1048576 | tf_op jit(solution)/shard_map/pallas_call | solution.py:360
  47.1 1.0 %shard_map.84.refs_3_ = f32[9,256,256]{2,1,0:T(8,128)} custom-call(bf16[9,32,256]{2,1,0:T(8,128)(2,1)S(1)} %collective-permute-done.9.refs_0_, bf16[9,32,256]{2,1,0:T(8,128)(2,1)S(1)} %collective-permute-done.11.refs_1_, bf16[9,32,256]{2,1,0:T(8,128)(2,1)S(1)} %collective-permute-done.13.refs_2_, ...), custom_call_target="tpu_custom_call", output_to_operand_aliasing={{}: (3, {})} | custom-call | flops 1048576 | bytes 1572864 | tf_op jit(solution)/shard_map/pallas_call | solution.py:360
  48.1 1.0 %shard_map.85 = f32[9,256,256]{2,1,0:T(8,128)} custom-call(bf16[9,32,256]{2,1,0:T(8,128)(2,1)S(1)} %collective-permute-done.10.refs_0_, bf16[9,32,256]{2,1,0:T(8,128)(2,1)S(1)} %collective-permute-done.12.refs_1_, bf16[9,32,256]{2,1,0:T(8,128)(2,1)S(1)} %collective-permute-done.14.refs_2_, ...), custom_call_target="tpu_custom_call", output_to_operand_aliasing={{}: (3, {})} | custom-call | flops 1048576 | bytes 1572864 | tf_op jit(solution)/shard_map/pallas_call | solution.py:360
  (26 shorter events, 1.8 us)
Async XLA Ops:
  3.1 6.1 %collective-permute-start = (bf16[6,16,256]{2,1,0:T(8,128)(2,1)S(1)}, bf16[6,16,256]{2,1,0:T(8,128)(2,1)S(1)}, u32[]{:S(2)}, u32[]{:S(2)}) collective-permute-start(bf16[6,16,256]{2,1,0:T(8,128)(2,1)S(1)} %get-tuple-element.26), channel_id=1, source_target_pairs={{0,1},{1,0},{2,3},{3,2},{4,5},{5,4},{6,7},{7,6},{8,9},{9,8},{10,11... | collective-permute-start | bytes 147464 | tf_op jit(solution)/shard_map/ppermute | solution.py:443
  3.7 5.5 %collective-permute-start.1 = (bf16[6,16,256]{2,1,0:T(8,128)(2,1)S(1)}, bf16[6,16,256]{2,1,0:T(8,128)(2,1)S(1)}, u32[]{:S(2)}, u32[]{:S(2)}) collective-permute-start(bf16[6,16,256]{2,1,0:T(8,128)(2,1)S(1)} %get-tuple-element.27), channel_id=1, source_target_pairs={{0,16},{1,2},{2,1},{3,4},{4,3},{5,6},{6,5},{7,8},{8,7},{9,10},{10,... | collective-permute-start | bytes 147464 | tf_op jit(solution)/shard_map/ppermute | solution.py:437
  11.7 2.1 %collective-permute-start.4 = (bf16[4,9,32,256]{3,2,1,0:T(8,128)(2,1)S(1)}, bf16[4,9,32,256]{3,2,1,0:T(8,128)(2,1)S(1)}, u32[]{:S(2)}, u32[]{:S(2)}) collective-permute-start(bf16[4,9,32,256]{3,2,1,0:T(8,128)(2,1)S(1)} %shard_map.81), channel_id=1, source_target_pairs={{0,1},{1,0},{2,3},{3,2},{4,5},{5,4},{6,7},{7,6},{8,9},{9,8},{10,11... | collective-permute-start | bytes 1769480 | tf_op jit(solution)/shard_map/ppermute | solution.py:443
  12.9 29.7 %copy-start = (bf16[9,256,256]{2,1,0:T(8,128)(2,1)S(1)}, bf16[9,256,256]{2,1,0:T(8,128)(2,1)}, u32[]{:S(2)}) copy-start(bf16[9,256,256]{2,1,0:T(8,128)(2,1)} %param.6) | copy-start | bytes 3538948
  12.9 29.7 %copy-start.1 = (s32[6,8]{1,0:T(8,128)S(1)}, s32[6,8]{1,0:T(8,128)}, u32[]{:S(2)}) copy-start(s32[6,8]{1,0:T(8,128)} %codes.5) | copy-start | bytes 580
  12.9 29.7 %copy-start.2 = (s32[6]{0:T(128)S(1)}, s32[6]{0:T(128)}, u32[]{:S(2)}) copy-start(s32[6]{0:T(128)} %pos.5) | copy-start | bytes 76
  13.9 6.3 %collective-permute-start.5 = (bf16[9,32,256]{2,1,0:T(8,128)(2,1)S(1)}, bf16[9,32,256]{2,1,0:T(8,128)(2,1)S(1)}, u32[]{:S(2)}, u32[]{:S(2)}) collective-permute-start(bf16[9,32,256]{2,1,0:T(8,128)(2,1)S(1)} %get-tuple-element.37), channel_id=1, source_target_pairs={{0,2},{1,5},{2,0},{3,7},{4,6},{5,1},{6,4},{7,3},{8,10},{9,13},{10,... | collective-permute-start | bytes 442376 | tf_op jit(solution)/shard_map/ppermute | solution.py:452
  15.3 6.5 %collective-permute-start.6 = (bf16[9,32,256]{2,1,0:T(8,128)(2,1)S(1)}, bf16[9,32,256]{2,1,0:T(8,128)(2,1)S(1)}, u32[]{:S(2)}, u32[]{:S(2)}) collective-permute-start(bf16[9,32,256]{2,1,0:T(8,128)(2,1)S(1)} %get-tuple-element.38), channel_id=1, source_target_pairs={{0,4},{1,3},{2,6},{3,1},{4,0},{5,7},{6,2},{7,5},{8,12},{9,11},{10,... | collective-permute-start | bytes 442376 | tf_op jit(solution)/shard_map/ppermute | solution.py:452
  16.9 7.1 %collective-permute-start.7 = (bf16[9,32,256]{2,1,0:T(8,128)(2,1)S(1)}, bf16[9,32,256]{2,1,0:T(8,128)(2,1)S(1)}, u32[]{:S(2)}, u32[]{:S(2)}) collective-permute-start(bf16[9,32,256]{2,1,0:T(8,128)(2,1)S(1)} %get-tuple-element.39), channel_id=1, source_target_pairs={{0,6},{1,7},{2,4},{3,5},{4,2},{5,3},{6,0},{7,1},{8,14},{9,15},{10,... | collective-permute-start | bytes 442376 | tf_op jit(solution)/shard_map/ppermute | solution.py:452
  24.2 9.3 %collective-permute-start.8 = (bf16[9,32,256]{2,1,0:T(8,128)(2,1)S(1)}, bf16[9,32,256]{2,1,0:T(8,128)(2,1)S(1)}, u32[]{:S(2)}, u32[]{:S(2)}) collective-permute-start(bf16[9,32,256]{2,1,0:T(8,128)(2,1)S(1)} %add_convert_fusion.1), channel_id=1, source_target_pairs={{0,8},{1,9},{2,10},{3,11},{4,12},{5,13},{6,14},{7,15},{8,0},{9,1},... | collective-permute-start | bytes 442376 | tf_op jit(solution)/shard_map/ppermute | solution.py:443
  33.5 7.7 %collective-permute-start.13 = (bf16[9,32,256]{2,1,0:T(8,128)(2,1)S(1)}, bf16[9,32,256]{2,1,0:T(8,128)(2,1)S(1)}, u32[]{:S(2)}, u32[]{:S(2)}) collective-permute-start(bf16[9,32,256]{2,1,0:T(8,128)(2,1)S(1)} %add_convert_fusion.refs_0_), channel_id=1, source_target_pairs={{0,6},{1,7},{2,4},{3,5},{4,2},{5,3},{6,0},{7,1},{8,14},{9,15},{10,... | collective-permute-start | bytes 442376 | tf_op jit(solution)/shard_map/ppermute | solution.py:452
  33.9 8.3 %collective-permute-start.11 = (bf16[9,32,256]{2,1,0:T(8,128)(2,1)S(1)}, bf16[9,32,256]{2,1,0:T(8,128)(2,1)S(1)}, u32[]{:S(2)}, u32[]{:S(2)}) collective-permute-start(bf16[9,32,256]{2,1,0:T(8,128)(2,1)S(1)} %add_convert_fusion.refs_0_), channel_id=1, source_target_pairs={{0,4},{1,3},{2,6},{3,1},{4,0},{5,7},{6,2},{7,5},{8,12},{9,11},{10,... | collective-permute-start | bytes 442376 | tf_op jit(solution)/shard_map/ppermute | solution.py:452
  35.6 6.5 %collective-permute-start.9 = (bf16[9,32,256]{2,1,0:T(8,128)(2,1)S(1)}, bf16[9,32,256]{2,1,0:T(8,128)(2,1)S(1)}, u32[]{:S(2)}, u32[]{:S(2)}) collective-permute-start(bf16[9,32,256]{2,1,0:T(8,128)(2,1)S(1)} %add_convert_fusion.refs_0_), channel_id=1, source_target_pairs={{0,2},{1,5},{2,0},{3,7},{4,6},{5,1},{6,4},{7,3},{8,10},{9,13},{10,... | collective-permute-start | bytes 442376 | tf_op jit(solution)/shard_map/ppermute | solution.py:452
  37.1 1.5 %collective-permute-start.2 = (bf16[6,16,256]{2,1,0:T(8,128)(2,1)S(1)}, bf16[6,16,256]{2,1,0:T(8,128)(2,1)S(1)}, u32[]{:S(2)}, u32[]{:S(2)}) collective-permute-start(bf16[6,16,256]{2,1,0:T(8,128)(2,1)S(1)} %get-tuple-element.32), channel_id=1, source_target_pairs={{0,1},{1,0},{2,3},{3,2},{4,5},{5,4},{6,7},{7,6},{8,9},{9,8},{10,11... | collective-permute-start | bytes 147464 | tf_op jit(solution)/shard_map/ppermute | solution.py:443
  37.1 5.6 %collective-permute-start.3 = (bf16[6,16,256]{2,1,0:T(8,128)(2,1)S(1)}, bf16[6,16,256]{2,1,0:T(8,128)(2,1)S(1)}, u32[]{:S(2)}, u32[]{:S(2)}) collective-permute-start(bf16[6,16,256]{2,1,0:T(8,128)(2,1)S(1)} %get-tuple-element.33), channel_id=1, source_target_pairs={{0,16},{1,2},{2,1},{3,4},{4,3},{5,6},{6,5},{7,8},{8,7},{9,10},{10,... | collective-permute-start | bytes 147464 | tf_op jit(solution)/shard_map/ppermute | solution.py:437
  38.6 7.6 %collective-permute-start.15 = (bf16[9,32,256]{2,1,0:T(8,128)(2,1)S(1)}, bf16[9,32,256]{2,1,0:T(8,128)(2,1)S(1)}, u32[]{:S(2)}, u32[]{:S(2)}) collective-permute-start(bf16[9,32,256]{2,1,0:T(8,128)(2,1)S(1)} %add_convert_fusion.refs_0_), channel_id=1, source_target_pairs={{0,1},{1,0},{2,3},{3,2},{4,5},{5,4},{6,7},{7,6},{8,9},{9,8},{10,11... | collective-permute-start | bytes 442376 | tf_op jit(solution)/shard_map/ppermute | solution.py:443
  41.2 6.9 %collective-permute-start.14 = (bf16[9,32,256]{2,1,0:T(8,128)(2,1)S(1)}, bf16[9,32,256]{2,1,0:T(8,128)(2,1)S(1)}, u32[]{:S(2)}, u32[]{:S(2)}) collective-permute-start(bf16[9,32,256]{2,1,0:T(8,128)(2,1)S(1)} %collective-permute-done.13.refs_2_), channel_id=1, source_target_pairs={{0,1},{1,0},{2,3},{3,2},{4,5},{5,4},{6,7},{7,6},{8,9},{9,8},{10,11... | collective-permute-start | bytes 442376 | tf_op jit(solution)/shard_map/ppermute | solution.py:443
  42.1 5.9 %collective-permute-start.12 = (bf16[9,32,256]{2,1,0:T(8,128)(2,1)S(1)}, bf16[9,32,256]{2,1,0:T(8,128)(2,1)S(1)}, u32[]{:S(2)}, u32[]{:S(2)}) collective-permute-start(bf16[9,32,256]{2,1,0:T(8,128)(2,1)S(1)} %collective-permute-done.11.refs_1_), channel_id=1, source_target_pairs={{0,1},{1,0},{2,3},{3,2},{4,5},{5,4},{6,7},{7,6},{8,9},{9,8},{10,11... | collective-permute-start | bytes 442376 | tf_op jit(solution)/shard_map/ppermute | solution.py:443
  42.2 6.0 %collective-permute-start.10 = (bf16[9,32,256]{2,1,0:T(8,128)(2,1)S(1)}, bf16[9,32,256]{2,1,0:T(8,128)(2,1)S(1)}, u32[]{:S(2)}, u32[]{:S(2)}) collective-permute-start(bf16[9,32,256]{2,1,0:T(8,128)(2,1)S(1)} %collective-permute-done.9.refs_0_), channel_id=1, source_target_pairs={{0,1},{1,0},{2,3},{3,2},{4,5},{5,4},{6,7},{7,6},{8,9},{9,8},{10,11... | collective-permute-start | bytes 442376 | tf_op jit(solution)/shard_map/ppermute | solution.py:443

commit v5 on v3

--- a/solution.py
+++ b/solution.py
@@ -423,13 +423,15 @@
     )(codes, pos, act, grad, cross, link, weights)
 
 
-def edge_swaps(to_core, to_link):
+def edge_swaps(to_core, to_link, ends):
     groups, count = lax.axis_size("groups"), lax.axis_size("tile")
     pairs = []
     for group in range(groups):
         other = group ^ 1 if groups % 2 == 0 else group
         for s in range(count):
             if s in (0, count - 1):
+                if not ends:
+                    continue
                 t = s if other != group else count - 1 - s
                 pairs.append((group * count + s, other * count + t))
             else:
@@ -479,7 +481,7 @@
     flat = weights.reshape(9 * channels, channels)
     early = slots
     inner, flat, grads, to_core, to_link = load(neighbours, features, flat, grad_out)
-    cross, link = edge_swaps(to_core, to_link)
+    cross, link = edge_swaps(to_core, to_link, True)
     partial, activation, grad = product(early, tile_pos, inner, flat, grads)
     activation, grad, edge, to_core, to_link = forward(
         early, neighbours, tile_pos, partial, inner, cross, link, flat, grads, activation, grad
@@ -503,7 +505,7 @@
         pieces[1:] + its[1:3], scale, whole, weight_grad,
     )
     weight_grad = collect(((1, 3),), its[3:], scale, whole, weight_grad)
-    cross, link = edge_swaps(to_core, to_link)
+    cross, link = edge_swaps(to_core, to_link, False)
     activation, input_grad = backward(
         neighbours, tile_pos, activation, grad, cross, link,
         weights.reshape(9 * channels, channels),

time: 50 us -> 49.9 us (level)
  waiting for transfers between devices: 18.3 us -> 17.7 us
  starting transfers between devices: 15 us -> 15.6 us
    ppermute x8, starting transfers between devices: 3.83 us -> 5.28 us  [swap(): lax.ppermute(value, 'tile', [(source, source ^ bit) for source in range(c...]
    ppermute x6, waiting for transfers between devices: 10.9 us -> 9.67 us  [quad_swaps(): got.append(lax.ppermute(value, 'tile', pairs))]
    ppermute x2, starting transfers between devices: 4.1 us -> 3.23 us  [edge_swaps(): link = lax.ppermute(to_link, ('groups', 'tile'), pairs)]
    ppermute x8, waiting for transfers between devices: 7.44 us -> 8.01 us  [swap(): lax.ppermute(value, 'tile', [(source, source ^ bit) for source in range(c...]
  transfers between devices with their start and end apart: 16 -> 16, of which waited for: 7 -> 8; matrix products, arithmetic and copies ran while one was open for 0% -> 0% of each run, Pallas kernels for 19% -> 19%
where the time goes in v5:
time: 49.9 us; the launch traced here: 49.7 us
  waiting for transfers between devices  17.7 us (35%)
  starting transfers between devices  15.6 us (31%)
  Pallas kernels  15.5 us (31%)
  between operations  0.82 us (2%)
    ppermute x6, waiting for transfers between devices, quad_swaps(): got.append(lax.ppermute(value, 'tile', pairs))  9.67 us
    ppermute x8, waiting for transfers between devices, swap(): lax.ppermute(value, 'tile', [(source, source ^ bit) for source in range(c...  8.01 us
    ppermute x6, starting transfers between devices, quad_swaps(): got.append(lax.ppermute(value, 'tile', pairs))  7.1 us
    ppermute x8, starting transfers between devices, swap(): lax.ppermute(value, 'tile', [(source, source ^ bit) for source in range(c...  5.28 us
    pallas_call x1, Pallas kernels, backward(): call(backward_kernel, 18 * slots * side * side * channels * channels, 4 <...  3.55 us
    ppermute x2, starting transfers between devices, edge_swaps(): link = lax.ppermute(to_link, ('groups', 'tile'), pairs)  3.23 us
    pallas_call x1, Pallas kernels, product(): call(functools.partial(product_kernel, early), 2 * slots * side * side *...  2.94 us
    pallas_call x3, Pallas kernels, collect(): call(functools.partial(collect_kernel, scale, plan), 1 << 20, count << 19...  2.79 us
  transfers between devices with their start and end apart: 16, of which 8 were waited for; matrix products, arithmetic and copies ran while one was open for 0% of the time, Pallas kernels for 19%

profile of v5, /device:TPU:0, one launch (start us, length us, event | category | flops | bytes accessed | tf_op | source)
XLA Modules:
  0.0 49.7 jit_solution(10363154778709685503)
XLA Ops:
  0.6 2.5 %shard_map.76 = (bf16[6,16,16,768]{3,2,1,0:T(8,128)(2,1)S(1)}, bf16[2304,256]{1,0:T(8,128)(2,1)S(1)}, bf16[6,16,16,256]{3,2,1,0:T(8,128)(2,1)S(1)}, bf16[6,16,25...) custom-call(s32[6,8]{1,0:T(8,128)} %codes.5, bf16[6,16,16,256]{3,2,1,0:T(8,128)(2,1)} %maps.1, bf16[2304,256]{1,0:T(8,128)(2,1)} %bitcast.1, ...), custom_call_target="tpu_custom_call" | custom-call | flops 1048576 | bytes 6291456 | tf_op jit(solution)/shard_map/pallas_call | solution.py:145
  3.7 2.6 %collective-permute-start.1 = (bf16[6,16,256]{2,1,0:T(8,128)(2,1)S(1)}, bf16[6,16,256]{2,1,0:T(8,128)(2,1)S(1)}, u32[]{:S(2)}, u32[]{:S(2)}) collective-permute-start(bf16[6,16,256]{2,1,0:T(8,128)(2,1)S(1)} %get-tuple-element.27), channel_id=1, source_target_pairs={{0,16},{1,2},{2,1},{3,4},{4,3},{5,6},{6,5},{7,8},{8,7},{9,10},{10,... | collective-permute-start | bytes 147464 | tf_op jit(solution)/shard_map/ppermute | solution.py:439
  6.3 2.9 %shard_map.77 = (f32[6,16,16,256]{3,2,1,0:T(8,128)S(1)}, bf16[6,16,16,256]{3,2,1,0:T(8,128)(2,1)S(1)}, bf16[6,16,16,256]{3,2,1,0:T(8,128)(2,1)S(1)}) custom-call(s32[6]{0:T(128)} %pos.5, bf16[6,16,16,768]{3,2,1,0:T(8,128)(2,1)S(1)} %get-tuple-element.22.inner, bf16[2304,256]{1,0:T(8,128)(2,1)S(1)} %get-tuple-element.23.weights, ...), custom_call_target="tpu_custom_call" | custom-call | flops 1811939328 | bytes 6291456 | tf_op jit(solution)/shard_map/pallas_call | solution.py:189
  9.2 1.2 %shard_map.78 = (bf16[6,16,16,256]{3,2,1,0:T(8,128)(2,1)S(1)}, bf16[6,16,16,256]{3,2,1,0:T(8,128)(2,1)S(1)}, bf16[6,2,16,768]{3,2,1,0:T(8,128)(2,1)S(1)}, bf16[6...) custom-call(s32[6,8]{1,0:T(8,128)} %codes.5, s32[6]{0:T(128)} %pos.5, ...), custom_call_target="tpu_custom_call", output_to_operand_aliasing={{0}: (8, {}), {1}: (9, {})} | custom-call | flops 75497472 | bytes 8388608 | tf_op jit(solution)/shard_map/pallas_call | solution.py:252
  10.4 1.2 %shard_map.81 = bf16[4,9,32,256]{3,2,1,0:T(8,128)(2,1)S(1)} custom-call(bf16[6,16,16,768]{3,2,1,0:T(8,128)(2,1)S(1)} %get-tuple-element.22.inner, bf16[6,2,16,768]{3,2,1,0:T(8,128)(2,1)S(1)} %get-tuple-element.35.edge, bf16[6,16,16,256]{3,2,1,0:T(8,128)(2,1)S(1)} %get-tuple-element.31.grad), custom_call_target="tpu_custom_call" | custom-call | flops 905969664 | bytes 6291456 | tf_op jit(solution)/shard_map/pallas_call | solution.py:301
  11.8 1.2 %shard_map.80.keep = f32[4,9,32,256]{3,2,1,0:T(8,128)S(1)} custom-call(bf16[6,16,16,768]{3,2,1,0:T(8,128)(2,1)S(1)} %get-tuple-element.22.inner, bf16[6,2,16,768]{3,2,1,0:T(8,128)(2,1)S(1)} %get-tuple-element.35.edge, bf16[6,16,16,256]{3,2,1,0:T(8,128)(2,1)S(1)} %get-tuple-element.31.grad), custom_call_target="tpu_custom_call" | custom-call | flops 905969664 | bytes 6291456 | tf_op jit(solution)/shard_map/pallas_call | solution.py:301
  13.0 0.8 %collective-permute-done.4.recv = bf16[4,9,32,256]{3,2,1,0:T(8,128)(2,1)S(1)} collective-permute-done((bf16[4,9,32,256]{3,2,1,0:T(8,128)(2,1)S(1)}, bf16[4,9,32,256]{3,2,1,0:T(8,128)(2,1)S(1)}, u32[]{:S(2)}, u32[]{:S(2)}) %collective-permute-start.4) | collective-permute-done | bytes 589856 | tf_op jit(solution)/shard_map/ppermute | solution.py:445
  13.9 1.5 %collective-permute-start.5 = (bf16[9,32,256]{2,1,0:T(8,128)(2,1)S(1)}, bf16[9,32,256]{2,1,0:T(8,128)(2,1)S(1)}, u32[]{:S(2)}, u32[]{:S(2)}) collective-permute-start(bf16[9,32,256]{2,1,0:T(8,128)(2,1)S(1)} %get-tuple-element.37), channel_id=1, source_target_pairs={{0,2},{1,5},{2,0},{3,7},{4,6},{5,1},{6,4},{7,3},{8,10},{9,13},{10,... | collective-permute-start | bytes 442376 | tf_op jit(solution)/shard_map/ppermute | solution.py:454
  15.3 1.6 %collective-permute-start.6 = (bf16[9,32,256]{2,1,0:T(8,128)(2,1)S(1)}, bf16[9,32,256]{2,1,0:T(8,128)(2,1)S(1)}, u32[]{:S(2)}, u32[]{:S(2)}) collective-permute-start(bf16[9,32,256]{2,1,0:T(8,128)(2,1)S(1)} %get-tuple-element.38), channel_id=1, source_target_pairs={{0,4},{1,3},{2,6},{3,1},{4,0},{5,7},{6,2},{7,5},{8,12},{9,11},{10,... | collective-permute-start | bytes 442376 | tf_op jit(solution)/shard_map/ppermute | solution.py:454
  17.4 2.7 %collective-permute-done.5 = bf16[9,32,256]{2,1,0:T(8,128)(2,1)S(1)} collective-permute-done((bf16[9,32,256]{2,1,0:T(8,128)(2,1)S(1)}, bf16[9,32,256]{2,1,0:T(8,128)(2,1)S(1)}, u32[]{:S(2)}, u32[]{:S(2)}) %collective-permute-start.5) | collective-permute-done | bytes 147488 | tf_op jit(solution)/shard_map/ppermute | solution.py:454
  20.2 1.6 %collective-permute-done.6 = bf16[9,32,256]{2,1,0:T(8,128)(2,1)S(1)} collective-permute-done((bf16[9,32,256]{2,1,0:T(8,128)(2,1)S(1)}, bf16[9,32,256]{2,1,0:T(8,128)(2,1)S(1)}, u32[]{:S(2)}, u32[]{:S(2)}) %collective-permute-start.6) | collective-permute-done | bytes 147488 | tf_op jit(solution)/shard_map/ppermute | solution.py:454
  21.8 2.3 %collective-permute-done.7 = bf16[9,32,256]{2,1,0:T(8,128)(2,1)S(1)} collective-permute-done((bf16[9,32,256]{2,1,0:T(8,128)(2,1)S(1)}, bf16[9,32,256]{2,1,0:T(8,128)(2,1)S(1)}, u32[]{:S(2)}, u32[]{:S(2)}) %collective-permute-start.7) | collective-permute-done | bytes 147488 | tf_op jit(solution)/shard_map/ppermute | solution.py:454
  24.2 2.7 %collective-permute-start.8 = (bf16[9,32,256]{2,1,0:T(8,128)(2,1)S(1)}, bf16[9,32,256]{2,1,0:T(8,128)(2,1)S(1)}, u32[]{:S(2)}, u32[]{:S(2)}) collective-permute-start(bf16[9,32,256]{2,1,0:T(8,128)(2,1)S(1)} %add_convert_fusion.1), channel_id=1, source_target_pairs={{0,8},{1,9},{2,10},{3,11},{4,12},{5,13},{6,14},{7,15},{8,0},{9,1},... | collective-permute-start | bytes 442376 | tf_op jit(solution)/shard_map/ppermute | solution.py:445
  26.8 6.7 %collective-permute-done.8 = bf16[9,32,256]{2,1,0:T(8,128)(2,1)S(1)} collective-permute-done((bf16[9,32,256]{2,1,0:T(8,128)(2,1)S(1)}, bf16[9,32,256]{2,1,0:T(8,128)(2,1)S(1)}, u32[]{:S(2)}, u32[]{:S(2)}) %collective-permute-start.8) | collective-permute-done | bytes 147488 | tf_op jit(solution)/shard_map/ppermute | solution.py:445
  33.6 0.9 %collective-permute-start.11 = (bf16[9,32,256]{2,1,0:T(8,128)(2,1)S(1)}, bf16[9,32,256]{2,1,0:T(8,128)(2,1)S(1)}, u32[]{:S(2)}, u32[]{:S(2)}) collective-permute-start(bf16[9,32,256]{2,1,0:T(8,128)(2,1)S(1)} %add_convert_fusion.refs_0_), channel_id=1, source_target_pairs={{0,2},{1,5},{2,0},{3,7},{4,6},{5,1},{6,4},{7,3},{8,10},{9,13},{10,... | collective-permute-start | bytes 442376 | tf_op jit(solution)/shard_map/ppermute | solution.py:454
  34.4 2.6 %collective-permute-start.9 = (bf16[9,32,256]{2,1,0:T(8,128)(2,1)S(1)}, bf16[9,32,256]{2,1,0:T(8,128)(2,1)S(1)}, u32[]{:S(2)}, u32[]{:S(2)}) collective-permute-start(bf16[9,32,256]{2,1,0:T(8,128)(2,1)S(1)} %add_convert_fusion.refs_0_), channel_id=1, source_target_pairs={{0,6},{1,7},{2,4},{3,5},{4,2},{5,3},{6,0},{7,1},{8,14},{9,15},{10,... | collective-permute-start | bytes 442376 | tf_op jit(solution)/shard_map/ppermute | solution.py:454
  37.1 0.7 %collective-permute-start.3 = (bf16[6,16,256]{2,1,0:T(8,128)(2,1)S(1)}, bf16[6,16,256]{2,1,0:T(8,128)(2,1)S(1)}, u32[]{:S(2)}, u32[]{:S(2)}) collective-permute-start(bf16[6,16,256]{2,1,0:T(8,128)(2,1)S(1)} %get-tuple-element.33), channel_id=1, source_target_pairs={{1,2},{2,1},{3,4},{4,3},{5,6},{6,5},{7,8},{8,7},{9,10},{10,9},{11,... | collective-permute-start | bytes 147464 | tf_op jit(solution)/shard_map/ppermute | solution.py:439
  37.7 0.6 %collective-permute-done.2.cross = bf16[6,16,256]{2,1,0:T(8,128)(2,1)S(1)} collective-permute-done((bf16[6,16,256]{2,1,0:T(8,128)(2,1)S(1)}, bf16[6,16,256]{2,1,0:T(8,128)(2,1)S(1)}, u32[]{:S(2)}, u32[]{:S(2)}) %collective-permute-start.2) | collective-permute-done | bytes 49184 | tf_op jit(solution)/shard_map/ppermute | solution.py:445
  38.3 1.4 %collective-permute-start.15 = (bf16[9,32,256]{2,1,0:T(8,128)(2,1)S(1)}, bf16[9,32,256]{2,1,0:T(8,128)(2,1)S(1)}, u32[]{:S(2)}, u32[]{:S(2)}) collective-permute-start(bf16[9,32,256]{2,1,0:T(8,128)(2,1)S(1)} %add_convert_fusion.refs_0_), channel_id=1, source_target_pairs={{0,1},{1,0},{2,3},{3,2},{4,5},{5,4},{6,7},{7,6},{8,9},{9,8},{10,11... | collective-permute-start | bytes 442376 | tf_op jit(solution)/shard_map/ppermute | solution.py:445
  40.8 2.5 %collective-permute-done.9.refs_2_ = bf16[9,32,256]{2,1,0:T(8,128)(2,1)S(1)} collective-permute-done((bf16[9,32,256]{2,1,0:T(8,128)(2,1)S(1)}, bf16[9,32,256]{2,1,0:T(8,128)(2,1)S(1)}, u32[]{:S(2)}, u32[]{:S(2)}) %collective-permute-start.9) | collective-permute-done | bytes 147488 | tf_op jit(solution)/shard_map/ppermute | solution.py:454
  43.3 3.5 %shard_map.79 = (bf16[6,16,16,256]{3,2,1,0:T(8,128)(2,1)}, bf16[6,16,16,256]{3,2,1,0:T(8,128)(2,1)}) custom-call(s32[6,8]{1,0:T(8,128)S(1)} %copy-done.1, s32[6]{0:T(128)S(1)} %copy-done.2, bf16[6,16,16,256]{3,2,1,0:T(8,128)(2,1)S(1)} %get-tuple-element.30.act, bf16[6,16,16,256]{3,2,1,0:T(8,128)(2,1)S(1)} %get-tuple-element.31.grad, ...), custom_call_target="tpu_custom_call" | custom-call | flops 1811939328 | bytes 4194304 | tf_op jit(solution)/shard_map/pallas_call | solution.py:410
  46.9 0.9 %shard_map.83.refs_5_ = f32[9,256,256]{2,1,0:T(8,128)} custom-call(bf16[9,32,256]{2,1,0:T(8,128)(2,1)S(1)} %add_convert_fusion.refs_0_, bf16[9,32,256]{2,1,0:T(8,128)(2,1)S(1)} %collective-permute-done.15.refs_1_), custom_call_target="tpu_custom_call" | custom-call | flops 1048576 | bytes 1048576 | tf_op jit(solution)/shard_map/pallas_call | solution.py:360
  47.8 1.2 %shard_map.84.refs_1_ = f32[9,256,256]{2,1,0:T(8,128)} custom-call(bf16[9,32,256]{2,1,0:T(8,128)(2,1)S(1)} %collective-permute-done.11.refs_0_, bf16[9,32,256]{2,1,0:T(8,128)(2,1)S(1)} %collective-permute-done.12.refs_1_, bf16[9,32,256]{2,1,0:T(8,128)(2,1)S(1)} %collective-permute-done.9.refs_2_, ...), custom_call_target="tpu_custom_call", output_to_operand_aliasing={{}: (5, {})} | custom-call | flops 1048576 | bytes 2621440 | tf_op jit(solution)/shard_map/pallas_call | solution.py:360
  49.0 0.8 %shard_map.85 = f32[9,256,256]{2,1,0:T(8,128)} custom-call(bf16[9,32,256]{2,1,0:T(8,128)(2,1)S(1)} %collective-permute-done.10.refs_0_, f32[9,256,256]{2,1,0:T(8,128)} %shard_map.84.refs_1_), custom_call_target="tpu_custom_call", output_to_operand_aliasing={{}: (1, {})} | custom-call | flops 1048576 | bytes 524288 | tf_op jit(solution)/shard_map/pallas_call | solution.py:360
  (26 shorter events, 2.6 us)
Async XLA Ops:
  3.1 6.1 %collective-permute-start = (bf16[6,16,256]{2,1,0:T(8,128)(2,1)S(1)}, bf16[6,16,256]{2,1,0:T(8,128)(2,1)S(1)}, u32[]{:S(2)}, u32[]{:S(2)}) collective-permute-start(bf16[6,16,256]{2,1,0:T(8,128)(2,1)S(1)} %get-tuple-element.26), channel_id=1, source_target_pairs={{0,1},{1,0},{2,3},{3,2},{4,5},{5,4},{6,7},{7,6},{8,9},{9,8},{10,11... | collective-permute-start | bytes 147464 | tf_op jit(solution)/shard_map/ppermute | solution.py:445
  3.7 5.5 %collective-permute-start.1 = (bf16[6,16,256]{2,1,0:T(8,128)(2,1)S(1)}, bf16[6,16,256]{2,1,0:T(8,128)(2,1)S(1)}, u32[]{:S(2)}, u32[]{:S(2)}) collective-permute-start(bf16[6,16,256]{2,1,0:T(8,128)(2,1)S(1)} %get-tuple-element.27), channel_id=1, source_target_pairs={{0,16},{1,2},{2,1},{3,4},{4,3},{5,6},{6,5},{7,8},{8,7},{9,10},{10,... | collective-permute-start | bytes 147464 | tf_op jit(solution)/shard_map/ppermute | solution.py:439
  11.7 2.1 %collective-permute-start.4 = (bf16[4,9,32,256]{3,2,1,0:T(8,128)(2,1)S(1)}, bf16[4,9,32,256]{3,2,1,0:T(8,128)(2,1)S(1)}, u32[]{:S(2)}, u32[]{:S(2)}) collective-permute-start(bf16[4,9,32,256]{3,2,1,0:T(8,128)(2,1)S(1)} %shard_map.81), channel_id=1, source_target_pairs={{0,1},{1,0},{2,3},{3,2},{4,5},{5,4},{6,7},{7,6},{8,9},{9,8},{10,11... | collective-permute-start | bytes 1769480 | tf_op jit(solution)/shard_map/ppermute | solution.py:445
  12.9 30.4 %copy-start = (bf16[9,256,256]{2,1,0:T(8,128)(2,1)S(1)}, bf16[9,256,256]{2,1,0:T(8,128)(2,1)}, u32[]{:S(2)}) copy-start(bf16[9,256,256]{2,1,0:T(8,128)(2,1)} %param.6) | copy-start | bytes 3538948
  12.9 30.4 %copy-start.1 = (s32[6,8]{1,0:T(8,128)S(1)}, s32[6,8]{1,0:T(8,128)}, u32[]{:S(2)}) copy-start(s32[6,8]{1,0:T(8,128)} %codes.5) | copy-start | bytes 580
  12.9 30.4 %copy-start.2 = (s32[6]{0:T(128)S(1)}, s32[6]{0:T(128)}, u32[]{:S(2)}) copy-start(s32[6]{0:T(128)} %pos.5) | copy-start | bytes 76
  13.9 6.3 %collective-permute-start.5 = (bf16[9,32,256]{2,1,0:T(8,128)(2,1)S(1)}, bf16[9,32,256]{2,1,0:T(8,128)(2,1)S(1)}, u32[]{:S(2)}, u32[]{:S(2)}) collective-permute-start(bf16[9,32,256]{2,1,0:T(8,128)(2,1)S(1)} %get-tuple-element.37), channel_id=1, source_target_pairs={{0,2},{1,5},{2,0},{3,7},{4,6},{5,1},{6,4},{7,3},{8,10},{9,13},{10,... | collective-permute-start | bytes 442376 | tf_op jit(solution)/shard_map/ppermute | solution.py:454
  15.3 6.5 %collective-permute-start.6 = (bf16[9,32,256]{2,1,0:T(8,128)(2,1)S(1)}, bf16[9,32,256]{2,1,0:T(8,128)(2,1)S(1)}, u32[]{:S(2)}, u32[]{:S(2)}) collective-permute-start(bf16[9,32,256]{2,1,0:T(8,128)(2,1)S(1)} %get-tuple-element.38), channel_id=1, source_target_pairs={{0,4},{1,3},{2,6},{3,1},{4,0},{5,7},{6,2},{7,5},{8,12},{9,11},{10,... | collective-permute-start | bytes 442376 | tf_op jit(solution)/shard_map/ppermute | solution.py:454
  16.9 7.1 %collective-permute-start.7 = (bf16[9,32,256]{2,1,0:T(8,128)(2,1)S(1)}, bf16[9,32,256]{2,1,0:T(8,128)(2,1)S(1)}, u32[]{:S(2)}, u32[]{:S(2)}) collective-permute-start(bf16[9,32,256]{2,1,0:T(8,128)(2,1)S(1)} %get-tuple-element.39), channel_id=1, source_target_pairs={{0,6},{1,7},{2,4},{3,5},{4,2},{5,3},{6,0},{7,1},{8,14},{9,15},{10,... | collective-permute-start | bytes 442376 | tf_op jit(solution)/shard_map/ppermute | solution.py:454
  24.2 9.3 %collective-permute-start.8 = (bf16[9,32,256]{2,1,0:T(8,128)(2,1)S(1)}, bf16[9,32,256]{2,1,0:T(8,128)(2,1)S(1)}, u32[]{:S(2)}, u32[]{:S(2)}) collective-permute-start(bf16[9,32,256]{2,1,0:T(8,128)(2,1)S(1)} %add_convert_fusion.1), channel_id=1, source_target_pairs={{0,8},{1,9},{2,10},{3,11},{4,12},{5,13},{6,14},{7,15},{8,0},{9,1},... | collective-permute-start | bytes 442376 | tf_op jit(solution)/shard_map/ppermute | solution.py:445
  33.5 6.8 %collective-permute-start.12 = (bf16[9,32,256]{2,1,0:T(8,128)(2,1)S(1)}, bf16[9,32,256]{2,1,0:T(8,128)(2,1)S(1)}, u32[]{:S(2)}, u32[]{:S(2)}) collective-permute-start(bf16[9,32,256]{2,1,0:T(8,128)(2,1)S(1)} %add_convert_fusion.refs_0_), channel_id=1, source_target_pairs={{0,4},{1,3},{2,6},{3,1},{4,0},{5,7},{6,2},{7,5},{8,12},{9,11},{10,... | collective-permute-start | bytes 442376 | tf_op jit(solution)/shard_map/ppermute | solution.py:454
  33.6 6.7 %collective-permute-start.11 = (bf16[9,32,256]{2,1,0:T(8,128)(2,1)S(1)}, bf16[9,32,256]{2,1,0:T(8,128)(2,1)S(1)}, u32[]{:S(2)}, u32[]{:S(2)}) collective-permute-start(bf16[9,32,256]{2,1,0:T(8,128)(2,1)S(1)} %add_convert_fusion.refs_0_), channel_id=1, source_target_pairs={{0,2},{1,5},{2,0},{3,7},{4,6},{5,1},{6,4},{7,3},{8,10},{9,13},{10,... | collective-permute-start | bytes 442376 | tf_op jit(solution)/shard_map/ppermute | solution.py:454
  34.4 8.8 %collective-permute-start.9 = (bf16[9,32,256]{2,1,0:T(8,128)(2,1)S(1)}, bf16[9,32,256]{2,1,0:T(8,128)(2,1)S(1)}, u32[]{:S(2)}, u32[]{:S(2)}) collective-permute-start(bf16[9,32,256]{2,1,0:T(8,128)(2,1)S(1)} %add_convert_fusion.refs_0_), channel_id=1, source_target_pairs={{0,6},{1,7},{2,4},{3,5},{4,2},{5,3},{6,0},{7,1},{8,14},{9,15},{10,... | collective-permute-start | bytes 442376 | tf_op jit(solution)/shard_map/ppermute | solution.py:454
  37.1 1.2 %collective-permute-start.2 = (bf16[6,16,256]{2,1,0:T(8,128)(2,1)S(1)}, bf16[6,16,256]{2,1,0:T(8,128)(2,1)S(1)}, u32[]{:S(2)}, u32[]{:S(2)}) collective-permute-start(bf16[6,16,256]{2,1,0:T(8,128)(2,1)S(1)} %get-tuple-element.32), channel_id=1, source_target_pairs={{0,1},{1,0},{2,3},{3,2},{4,5},{5,4},{6,7},{7,6},{8,9},{9,8},{10,11... | collective-permute-start | bytes 147464 | tf_op jit(solution)/shard_map/ppermute | solution.py:445
  37.1 6.2 %collective-permute-start.3 = (bf16[6,16,256]{2,1,0:T(8,128)(2,1)S(1)}, bf16[6,16,256]{2,1,0:T(8,128)(2,1)S(1)}, u32[]{:S(2)}, u32[]{:S(2)}) collective-permute-start(bf16[6,16,256]{2,1,0:T(8,128)(2,1)S(1)} %get-tuple-element.33), channel_id=1, source_target_pairs={{1,2},{2,1},{3,4},{4,3},{5,6},{6,5},{7,8},{8,7},{9,10},{10,9},{11,... | collective-permute-start | bytes 147464 | tf_op jit(solution)/shard_map/ppermute | solution.py:439
  38.3 8.6 %collective-permute-start.15 = (bf16[9,32,256]{2,1,0:T(8,128)(2,1)S(1)}, bf16[9,32,256]{2,1,0:T(8,128)(2,1)S(1)}, u32[]{:S(2)}, u32[]{:S(2)}) collective-permute-start(bf16[9,32,256]{2,1,0:T(8,128)(2,1)S(1)} %add_convert_fusion.refs_0_), channel_id=1, source_target_pairs={{0,1},{1,0},{2,3},{3,2},{4,5},{5,4},{6,7},{7,6},{8,9},{9,8},{10,11... | collective-permute-start | bytes 442376 | tf_op jit(solution)/shard_map/ppermute | solution.py:445
  40.3 7.5 %collective-permute-start.14 = (bf16[9,32,256]{2,1,0:T(8,128)(2,1)S(1)}, bf16[9,32,256]{2,1,0:T(8,128)(2,1)S(1)}, u32[]{:S(2)}, u32[]{:S(2)}) collective-permute-start(bf16[9,32,256]{2,1,0:T(8,128)(2,1)S(1)} %collective-permute-done.12.refs_1_), channel_id=1, source_target_pairs={{0,1},{1,0},{2,3},{3,2},{4,5},{5,4},{6,7},{7,6},{8,9},{9,8},{10,11... | collective-permute-start | bytes 442376 | tf_op jit(solution)/shard_map/ppermute | solution.py:445
  40.3 7.5 %collective-permute-start.13 = (bf16[9,32,256]{2,1,0:T(8,128)(2,1)S(1)}, bf16[9,32,256]{2,1,0:T(8,128)(2,1)S(1)}, u32[]{:S(2)}, u32[]{:S(2)}) collective-permute-start(bf16[9,32,256]{2,1,0:T(8,128)(2,1)S(1)} %collective-permute-done.11.refs_0_), channel_id=1, source_target_pairs={{0,1},{1,0},{2,3},{3,2},{4,5},{5,4},{6,7},{7,6},{8,9},{9,8},{10,11... | collective-permute-start | bytes 442376 | tf_op jit(solution)/shard_map/ppermute | solution.py:445
  43.3 5.7 %collective-permute-start.10 = (bf16[9,32,256]{2,1,0:T(8,128)(2,1)S(1)}, bf16[9,32,256]{2,1,0:T(8,128)(2,1)S(1)}, u32[]{:S(2)}, u32[]{:S(2)}) collective-permute-start(bf16[9,32,256]{2,1,0:T(8,128)(2,1)S(1)} %collective-permute-done.9.refs_2_), channel_id=1, source_target_pairs={{0,1},{1,0},{2,3},{3,2},{4,5},{5,4},{6,7},{7,6},{8,9},{9,8},{10,11... | collective-permute-start | bytes 442376 | tf_op jit(solution)/shard_map/ppermute | solution.py:445
